TPU v7x, 32 devices: a whole 2x2x4 slice. The times are simulated.
32 devices in a mesh: rows: 8 (over z, y), cam: 4 (over x, core).
Axes of the slice: x: 2, y: 2, z: 4, core: 2. Of those that a mesh axis runs over, the one named last changes fastest.
Arguments:
- prefix_tokens: bfloat16 [4096, 2048], P(('rows', 'cam')), may hold values from -6 to 6
- action_tokens: bfloat16 [512, 1024], P(('rows', 'cam')), may hold values from -6 to 6
- prefix_cotangent: bfloat16 [4096, 2048], P(('rows', 'cam')), may hold values from -6 to 6
- action_cotangent: bfloat16 [512, 1024], P(('rows', 'cam')), may hold values from -6 to 6
- prefix_segments: int32 [8, 512], P('rows'), may hold values from 0 to 1, as said below
- action_codes: int32 [8, 64], P('rows'), may hold values from 1 to 2, as said below
- prefix_query: bfloat16 [2048, 2048], P(('rows', 'cam')), may hold values from -0.125 to 0.125
- prefix_key: bfloat16 [2048, 256], P(('rows', 'cam')), may hold values from -0.125 to 0.125
- prefix_value: bfloat16 [2048, 256], P(('rows', 'cam')), may hold values from -0.125 to 0.125
- prefix_mixer: bfloat16 [2048, 2048], P(('rows', 'cam')), may hold values from -2.5 to 2.5
- action_query: bfloat16 [1024, 2048], P(('rows', 'cam')), may hold values from -0.1875 to 0.1875
- action_key: bfloat16 [1024, 256], P(('rows', 'cam')), may hold values from -0.1875 to 0.1875
- action_value: bfloat16 [1024, 256], P(('rows', 'cam')), may hold values from -0.1875 to 0.1875
- action_mixer: bfloat16 [1024, 2048], P(('rows', 'cam')), may hold values from -2.5 to 2.5
- prefix_prenorm: float32 [2048], replicated, may hold values from 0.5 to 1.5
- prefix_midnorm: float32 [2048], replicated, may hold values from 0.5 to 1.5
- action_prenorm: float32 [1024], replicated, may hold values from 0.5 to 1.5
- action_midnorm: float32 [1024], replicated, may hold values from 0.5 to 1.5
- prefix_gate: bfloat16 [2048, 16384], P('rows', 'cam'), may hold values from -0.125 to 0.125
- prefix_expand: bfloat16 [2048, 16384], P('rows', 'cam'), may hold values from -0.125 to 0.125
- prefix_down: bfloat16 [2048, 16384], P('rows', 'cam'), may hold values from -0.046875 to 0.046875
- action_gate: bfloat16 [1024, 4096], P('rows', 'cam'), may hold values from -0.1875 to 0.1875
- action_expand: bfloat16 [1024, 4096], P('rows', 'cam'), may hold values from -0.1875 to 0.1875
- action_down: bfloat16 [1024, 4096], P('rows', 'cam'), may hold values from -0.09375 to 0.09375
Outputs:
- prefix_result: bfloat16 [4096, 2048], P(('rows', 'cam'))
- action_result: bfloat16 [512, 1024], P(('rows', 'cam'))
- prefix_backward: bfloat16 [4096, 2048], P(('rows', 'cam'))
- action_backward: bfloat16 [512, 1024], P(('rows', 'cam'))
- prefix_query_grad: float32 [2048, 2048], P(('rows', 'cam'))
- prefix_key_grad: float32 [2048, 256], P(('rows', 'cam'))
- prefix_value_grad: float32 [2048, 256], P(('rows', 'cam'))
- prefix_mixer_grad: float32 [2048, 2048], P(('rows', 'cam'))
- action_query_grad: float32 [1024, 2048], P(('rows', 'cam'))
- action_key_grad: float32 [1024, 256], P(('rows', 'cam'))
- action_value_grad: float32 [1024, 256], P(('rows', 'cam'))
- action_mixer_grad: float32 [1024, 2048], P(('rows', 'cam'))
- prefix_prenorm_grad: float32 [2048], P(('rows', 'cam'))
- prefix_midnorm_grad: float32 [2048], P(('rows', 'cam'))
- action_prenorm_grad: float32 [1024], P(('rows', 'cam'))
- action_midnorm_grad: float32 [1024], P(('rows', 'cam'))
- prefix_gate_grad: float32 [2048, 16384], P('rows', 'cam')
- prefix_expand_grad: float32 [2048, 16384], P('rows', 'cam')
- prefix_down_grad: float32 [2048, 16384], P('rows', 'cam')
- action_gate_grad: float32 [1024, 4096], P('rows', 'cam')
- action_expand_grad: float32 [1024, 4096], P('rows', 'cam')
- action_down_grad: float32 [1024, 4096], P('rows', 'cam')
Inputs may be any that keep to these rules, and one draw needn't show every extreme that they name: `prefix_segments`: in each row, position t below 384 belongs to episode (t mod 128) // 64; the last 128 positions hold the texts of the 2 episodes in order, each one token or more. `action_codes`: each episode's 32 tokens lie in a row at positions e * 32 to (e + 1) * 32 - 1; the first 1 to 4 of them have code 1, the others code 2.
All inputs are finite; a program needn't handle non-finite values.
Results may differ from a plain program's by a relative error of at most 0.03.
Values may be sent and summed in bfloat16 or wider, within the bound.
A program may use at most 320 MiB of HBM per device.

v0:
```python
import jax
import jax.numpy as jnp
from jax import lax
from jax.sharding import PartitionSpec as P

ACTT = 32


epsilon = 1e-06
masked_score = -1e30


def merged(x, axis, combine):
    everything = jax.tree.map(
        lambda part, kind: lax.all_gather(part.astype(kind), axis), x, (jnp.bfloat16, jnp.bfloat16)
    )

    def take(k):
        return jax.tree.map(lambda part, own: part[k].astype(own.dtype), everything, x)

    return lax.fori_loop(
        1, lax.axis_size(axis), lambda k, so_far: combine(so_far, take(k)), take(0)
    )


def multiply(operand, matrix):
    return jnp.dot(operand, matrix, preferred_element_type=jnp.float32)


def against(operand, matrix):
    return lax.dot_general(
        operand, matrix, (((1,), (1,)), ((), ())), preferred_element_type=jnp.float32
    )


def outer_sum(operand, matrix):
    return lax.dot_general(
        operand, matrix, (((0,), (0,)), ((), ())), preferred_element_type=jnp.float32
    )


def norm_forward(values):
    scaling = lax.rsqrt(jnp.mean(values * values, axis=-1, keepdims=True) + epsilon)
    return (values * scaling, scaling)


def norm_backward(upstream, normed_unit, scaling, gain_vector):
    weighted = upstream * gain_vector
    average = jnp.mean(weighted * normed_unit, axis=-1, keepdims=True)
    return (scaling * (weighted - normed_unit * average), jnp.sum(upstream * normed_unit, axis=0))


def visible(query_ids, query_codes, key_ids, key_codes):
    matches = query_ids[:, None] == key_ids[None, :]
    return jnp.logical_and(matches, key_codes[None, :] <= query_codes[:, None])


def gated(gate_value, expand_value):
    return jax.nn.gelu(gate_value, approximate=True) * expand_value


def combine_stats(former, latter):
    maximum = jnp.maximum(former[0], latter[0])
    totals = former[1] * jnp.exp(former[0] - maximum) + latter[1] * jnp.exp(latter[0] - maximum)
    return (maximum, totals)


def expand_rows(normed_rows, gate_weight, expand_weight, down_weight):
    gate_value = multiply(normed_rows, gate_weight)
    expand_value = multiply(normed_rows, expand_weight)
    inside, pullback = jax.vjp(gated, gate_value, expand_value)
    inside_low = inside.astype(jnp.bfloat16)
    return (against(inside_low, down_weight), inside_low, pullback)


def expand_back(
    normed_rows, cotangent, inside_low, pullback, gate_weight, expand_weight, down_weight
):
    inside_grad = multiply(cotangent, down_weight)
    down_grad = outer_sum(cotangent, inside_low)
    gate_grad, expand_grad = pullback(inside_grad)
    gate_low = gate_grad.astype(jnp.bfloat16)
    expand_low = expand_grad.astype(jnp.bfloat16)
    normed_grad = against(gate_low, gate_weight) + against(expand_low, expand_weight)
    return (
        normed_grad,
        (outer_sum(normed_rows, gate_low), outer_sum(normed_rows, expand_low), down_grad),
    )


def project_back(
    normed_rows,
    normed_unit,
    scaling,
    gain_vector,
    query_low,
    key_low,
    value_low,
    query_weight,
    key_weight,
    value_weight,
):
    normed_grad = (
        against(query_low, query_weight)
        + against(key_low, key_weight)
        + against(value_low, value_weight)
    )
    residual, gain_grad = norm_backward(normed_grad, normed_unit, scaling, gain_vector)
    weight_grads = (
        outer_sum(normed_rows, query_low),
        outer_sum(normed_rows, key_low),
        outer_sum(normed_rows, value_low),
    )
    return (residual, gain_grad, weight_grads)


def body(
    prefix_tokens,
    action_tokens,
    prefix_cotangent,
    action_cotangent,
    prefix_segments,
    action_codes,
    prefix_query,
    prefix_key,
    prefix_value,
    prefix_mixer,
    action_query,
    action_key,
    action_value,
    action_mixer,
    prefix_prenorm,
    prefix_midnorm,
    action_prenorm,
    action_midnorm,
    prefix_gate,
    prefix_expand,
    prefix_down,
    action_gate,
    action_expand,
    action_down,
):
    groups = lax.axis_size("cam")
    member = lax.axis_index("cam")
    lead_count = prefix_tokens.shape[0]
    tail_count = action_tokens.shape[0]
    local_count = lead_count + tail_count
    head_size = prefix_key.shape[1]
    head_count = prefix_query.shape[1] // head_size
    inverse = float(head_size) ** (-0.5)
    weight_set = (
        lax.all_gather(prefix_query, ("rows", "cam"), axis=0, tiled=True),
        lax.all_gather(prefix_key, ("rows", "cam"), axis=0, tiled=True),
        lax.all_gather(prefix_value, ("rows", "cam"), axis=0, tiled=True),
        lax.all_gather(prefix_mixer, ("rows", "cam"), axis=0, tiled=True),
        lax.all_gather(action_query, ("rows", "cam"), axis=0, tiled=True),
        lax.all_gather(action_key, ("rows", "cam"), axis=0, tiled=True),
        lax.all_gather(action_value, ("rows", "cam"), axis=0, tiled=True),
        lax.all_gather(action_mixer, ("rows", "cam"), axis=0, tiled=True),
    )
    lead_query, lead_key, lead_value, lead_mixer = (
        weight_set[0],
        weight_set[1],
        weight_set[2],
        weight_set[3],
    )
    tail_query, tail_key, tail_value, tail_mixer = (
        weight_set[4],
        weight_set[5],
        weight_set[6],
        weight_set[7],
    )
    ffn_set = (
        lax.all_gather(prefix_gate, "rows", axis=0, tiled=True),
        lax.all_gather(prefix_expand, "rows", axis=0, tiled=True),
        lax.all_gather(prefix_down, "rows", axis=0, tiled=True),
        lax.all_gather(action_gate, "rows", axis=0, tiled=True),
        lax.all_gather(action_expand, "rows", axis=0, tiled=True),
        lax.all_gather(action_down, "rows", axis=0, tiled=True),
    )
    lead_gate, lead_expand, lead_down = (ffn_set[0], ffn_set[1], ffn_set[2])
    tail_gate, tail_expand, tail_down = (ffn_set[3], ffn_set[4], ffn_set[5])
    segment_row = prefix_segments[0]
    code_row = action_codes[0]
    action_ids = jnp.arange(groups * tail_count, dtype=jnp.int32) // ACTT
    group_ids = jnp.concatenate(
        [segment_row.reshape(groups, lead_count), action_ids.reshape(groups, tail_count)], 1
    ).reshape(-1)
    group_codes = jnp.concatenate(
        [jnp.zeros((groups, lead_count), jnp.int32), code_row.reshape(groups, tail_count)], 1
    ).reshape(-1)
    local_ids = lax.dynamic_slice_in_dim(group_ids, member * local_count, local_count)
    local_codes = lax.dynamic_slice_in_dim(group_codes, member * local_count, local_count)
    lead_float = prefix_tokens.astype(jnp.float32)
    tail_float = action_tokens.astype(jnp.float32)
    lead_unit, lead_scale = norm_forward(lead_float)
    tail_unit, tail_scale = norm_forward(tail_float)
    lead_normed = (lead_unit * prefix_prenorm).astype(jnp.bfloat16)
    tail_normed = (tail_unit * action_prenorm).astype(jnp.bfloat16)
    queries = jnp.concatenate(
        [multiply(lead_normed, lead_query), multiply(tail_normed, tail_query)], 0
    ).astype(jnp.bfloat16)
    local_keys = jnp.concatenate(
        [multiply(lead_normed, lead_key), multiply(tail_normed, tail_key)], 0
    ).astype(jnp.bfloat16)
    local_values = jnp.concatenate(
        [multiply(lead_normed, lead_value), multiply(tail_normed, tail_value)], 0
    ).astype(jnp.bfloat16)
    group_heads = lax.all_gather(queries, "cam", axis=0, tiled=True).reshape(
        groups * local_count, head_count, head_size
    )
    allowed = visible(group_ids, group_codes, local_ids, local_codes)
    logits = (
        jnp.einsum("qhd,kd->hqk", group_heads, local_keys, preferred_element_type=jnp.float32)
        * inverse
    )
    scores = jnp.where(allowed[None], logits, masked_score)
    part_maximum = jnp.max(scores, axis=2)
    part_totals = jnp.sum(
        jnp.where(allowed[None], jnp.exp(scores - part_maximum[:, :, None]), 0.0), axis=2
    )
    maximum, totals = merged((part_maximum, part_totals), "cam", combine_stats)
    exponent = jnp.exp(scores - maximum[:, :, None])
    part_output = jnp.einsum(
        "hqk,kd->qhd",
        exponent.astype(jnp.bfloat16),
        local_values,
        preferred_element_type=jnp.float32,
    )
    part_output = part_output.reshape(groups * local_count, head_count * head_size)
    unscaled = (
        lax.psum_scatter(part_output.astype(jnp.bfloat16), "cam", scatter_dimension=0, tiled=True)
        .astype(jnp.float32)
        .reshape(local_count, head_count, head_size)
    )
    own_totals = lax.dynamic_slice_in_dim(totals, member * local_count, local_count, 1)
    attention = unscaled / jnp.transpose(own_totals)[:, :, None]
    mixed_rows = attention.reshape(local_count, head_count * head_size).astype(jnp.bfloat16)
    lead_hidden = lead_float + against(mixed_rows[:lead_count], lead_mixer)
    tail_hidden = tail_float + against(mixed_rows[lead_count:], tail_mixer)
    lead_center, lead_factor = norm_forward(lead_hidden)
    tail_center, tail_factor = norm_forward(tail_hidden)
    lead_second = (lead_center * prefix_midnorm).astype(jnp.bfloat16)
    tail_second = (tail_center * action_midnorm).astype(jnp.bfloat16)
    lead_rows, tail_rows, lead_upper, tail_upper = (
        lax.all_gather(lead_second, "cam", axis=0, tiled=True),
        lax.all_gather(tail_second, "cam", axis=0, tiled=True),
        lax.all_gather(prefix_cotangent, "cam", axis=0, tiled=True),
        lax.all_gather(action_cotangent, "cam", axis=0, tiled=True),
    )
    lead_part, lead_inside, lead_pull = expand_rows(lead_rows, lead_gate, lead_expand, lead_down)
    tail_part, tail_inside, tail_pull = expand_rows(tail_rows, tail_gate, tail_expand, tail_down)
    lead_branch, tail_branch = (
        lax.psum_scatter(
            lead_part.astype(jnp.bfloat16), "cam", scatter_dimension=0, tiled=True
        ).astype(jnp.float32),
        lax.psum_scatter(
            tail_part.astype(jnp.bfloat16), "cam", scatter_dimension=0, tiled=True
        ).astype(jnp.float32),
    )
    lead_result = (lead_hidden + lead_branch).astype(jnp.bfloat16)
    tail_result = (tail_hidden + tail_branch).astype(jnp.bfloat16)
    lead_partial, lead_ffgrads = expand_back(
        lead_rows, lead_upper, lead_inside, lead_pull, lead_gate, lead_expand, lead_down
    )
    tail_partial, tail_ffgrads = expand_back(
        tail_rows, tail_upper, tail_inside, tail_pull, tail_gate, tail_expand, tail_down
    )
    lead_summed, tail_summed = (
        lax.psum_scatter(
            lead_partial.astype(jnp.bfloat16), "cam", scatter_dimension=0, tiled=True
        ).astype(jnp.float32),
        lax.psum_scatter(
            tail_partial.astype(jnp.bfloat16), "cam", scatter_dimension=0, tiled=True
        ).astype(jnp.float32),
    )
    lead_residual, lead_middle = norm_backward(
        lead_summed, lead_center, lead_factor, prefix_midnorm
    )
    tail_residual, tail_middle = norm_backward(
        tail_summed, tail_center, tail_factor, action_midnorm
    )
    lead_upstream = prefix_cotangent.astype(jnp.float32) + lead_residual
    tail_upstream = action_cotangent.astype(jnp.float32) + tail_residual
    lead_sent = lead_upstream.astype(jnp.bfloat16)
    tail_sent = tail_upstream.astype(jnp.bfloat16)
    lead_mixing = outer_sum(lead_sent, mixed_rows[:lead_count])
    tail_mixing = outer_sum(tail_sent, mixed_rows[lead_count:])
    attention_grad = jnp.concatenate(
        [multiply(lead_sent, lead_mixer), multiply(tail_sent, tail_mixer)], 0
    )
    attention_grad = attention_grad.reshape(local_count, head_count, head_size)
    scaled_grad = (attention_grad / jnp.transpose(own_totals)[:, :, None]).astype(jnp.bfloat16)
    deltas = jnp.sum(attention_grad * attention, axis=2) / jnp.transpose(own_totals)
    group_scaled = lax.all_gather(
        scaled_grad.reshape(local_count, head_count * head_size), "cam", axis=0, tiled=True
    )
    group_scaled = group_scaled.reshape(groups * local_count, head_count, head_size)
    group_deltas = lax.all_gather(deltas, "cam", axis=0, tiled=True)
    logits = (
        jnp.einsum("qhd,kd->hqk", group_heads, local_keys, preferred_element_type=jnp.float32)
        * inverse
    )
    scores = jnp.where(allowed[None], logits, masked_score)
    exponent = jnp.exp(scores - maximum[:, :, None])
    value_grad = jnp.einsum(
        "hqk,qhd->kd",
        exponent.astype(jnp.bfloat16),
        group_scaled,
        preferred_element_type=jnp.float32,
    )
    prob_grad = jnp.einsum(
        "qhd,kd->hqk", group_scaled, local_values, preferred_element_type=jnp.float32
    )
    score_grad = (exponent * (prob_grad - jnp.transpose(group_deltas)[:, :, None])).astype(
        jnp.bfloat16
    )
    key_grad = (
        jnp.einsum("hqk,qhd->kd", score_grad, group_heads, preferred_element_type=jnp.float32)
        * inverse
    )
    query_part = (
        jnp.einsum("hqk,kd->qhd", score_grad, local_keys, preferred_element_type=jnp.float32)
        * inverse
    )
    query_part = query_part.reshape(groups * local_count, head_count * head_size)
    query_grad = lax.psum_scatter(
        query_part.astype(jnp.bfloat16), "cam", scatter_dimension=0, tiled=True
    )
    key_low = key_grad.astype(jnp.bfloat16)
    value_low = value_grad.astype(jnp.bfloat16)
    lead_back, lead_first, lead_proj = project_back(
        lead_normed,
        lead_unit,
        lead_scale,
        prefix_prenorm,
        query_grad[:lead_count],
        key_low[:lead_count],
        value_low[:lead_count],
        lead_query,
        lead_key,
        lead_value,
    )
    tail_back, tail_first, tail_proj = project_back(
        tail_normed,
        tail_unit,
        tail_scale,
        action_prenorm,
        query_grad[lead_count:],
        key_low[lead_count:],
        value_low[lead_count:],
        tail_query,
        tail_key,
        tail_value,
    )
    lead_input = (lead_upstream + lead_back).astype(jnp.bfloat16)
    tail_input = (tail_upstream + tail_back).astype(jnp.bfloat16)
    attention_sums = (
        lax.psum_scatter(lead_proj[0], ("rows", "cam"), scatter_dimension=0, tiled=True),
        lax.psum_scatter(lead_proj[1], ("rows", "cam"), scatter_dimension=0, tiled=True),
        lax.psum_scatter(lead_proj[2], ("rows", "cam"), scatter_dimension=0, tiled=True),
        lax.psum_scatter(lead_mixing, ("rows", "cam"), scatter_dimension=0, tiled=True),
        lax.psum_scatter(tail_proj[0], ("rows", "cam"), scatter_dimension=0, tiled=True),
        lax.psum_scatter(tail_proj[1], ("rows", "cam"), scatter_dimension=0, tiled=True),
        lax.psum_scatter(tail_proj[2], ("rows", "cam"), scatter_dimension=0, tiled=True),
        lax.psum_scatter(tail_mixing, ("rows", "cam"), scatter_dimension=0, tiled=True),
        lax.psum_scatter(lead_first, ("rows", "cam"), scatter_dimension=0, tiled=True),
        lax.psum_scatter(lead_middle, ("rows", "cam"), scatter_dimension=0, tiled=True),
        lax.psum_scatter(tail_first, ("rows", "cam"), scatter_dimension=0, tiled=True),
        lax.psum_scatter(tail_middle, ("rows", "cam"), scatter_dimension=0, tiled=True),
    )
    expand_sums = (
        lax.psum_scatter(
            lead_ffgrads[0].astype(jnp.bfloat16), "rows", scatter_dimension=0, tiled=True
        ).astype(jnp.float32),
        lax.psum_scatter(
            lead_ffgrads[1].astype(jnp.bfloat16), "rows", scatter_dimension=0, tiled=True
        ).astype(jnp.float32),
        lax.psum_scatter(
            lead_ffgrads[2].astype(jnp.bfloat16), "rows", scatter_dimension=0, tiled=True
        ).astype(jnp.float32),
        lax.psum_scatter(
            tail_ffgrads[0].astype(jnp.bfloat16), "rows", scatter_dimension=0, tiled=True
        ).astype(jnp.float32),
        lax.psum_scatter(
            tail_ffgrads[1].astype(jnp.bfloat16), "rows", scatter_dimension=0, tiled=True
        ).astype(jnp.float32),
        lax.psum_scatter(
            tail_ffgrads[2].astype(jnp.bfloat16), "rows", scatter_dimension=0, tiled=True
        ).astype(jnp.float32),
    )
    return (
        lead_result,
        tail_result,
        lead_input,
        tail_input,
        attention_sums[0],
        attention_sums[1],
        attention_sums[2],
        attention_sums[3],
        attention_sums[4],
        attention_sums[5],
        attention_sums[6],
        attention_sums[7],
        attention_sums[8],
        attention_sums[9],
        attention_sums[10],
        attention_sums[11],
        expand_sums[0],
        expand_sums[1],
        expand_sums[2],
        expand_sums[3],
        expand_sums[4],
        expand_sums[5],
    )


def solution(mesh):
    in_specs = (
        P(("rows", "cam"), None),
        P(("rows", "cam"), None),
        P(("rows", "cam"), None),
        P(("rows", "cam"), None),
        P("rows", None),
        P("rows", None),
        P(("rows", "cam"), None),
        P(("rows", "cam"), None),
        P(("rows", "cam"), None),
        P(("rows", "cam"), None),
        P(("rows", "cam"), None),
        P(("rows", "cam"), None),
        P(("rows", "cam"), None),
        P(("rows", "cam"), None),
        P(),
        P(),
        P(),
        P(),
        P("rows", "cam"),
        P("rows", "cam"),
        P("rows", "cam"),
        P("rows", "cam"),
        P("rows", "cam"),
        P("rows", "cam"),
    )
    out_specs = (
        P(("rows", "cam"), None),
        P(("rows", "cam"), None),
        P(("rows", "cam"), None),
        P(("rows", "cam"), None),
        P(("rows", "cam"), None),
        P(("rows", "cam"), None),
        P(("rows", "cam"), None),
        P(("rows", "cam"), None),
        P(("rows", "cam"), None),
        P(("rows", "cam"), None),
        P(("rows", "cam"), None),
        P(("rows", "cam"), None),
        P(("rows", "cam")),
        P(("rows", "cam")),
        P(("rows", "cam")),
        P(("rows", "cam")),
        P("rows", "cam"),
        P("rows", "cam"),
        P("rows", "cam"),
        P("rows", "cam"),
        P("rows", "cam"),
        P("rows", "cam"),
    )
    return jax.shard_map(body, mesh=mesh, in_specs=in_specs, out_specs=out_specs, check_vma=False)
```

profile of v0, /device:TPU:0, one launch (start us, length us, event | category | flops | bytes accessed | tf_op | source)
XLA Modules:
  0.0 3839.1 jit_solution(4462726198808305320)
XLA Ops:
  12.2 63.2 %all-gather.26.cloned.1.call-done = bf16[1024,2048]{1,0:T(8,128)(2,1)} async-done(((bf16[32,2048]{1,0:T(8,128)(2,1)}), bf16[1024,2048]{1,0:T(8,128)(2,1)}) %all-gather.26.cloned.1.call-update) | async-done | bytes 4194320 | tf_op jit(solution)/shard_map/all_gather | solution.py:156
  78.3 75.8 %all-gather.24.cloned.1.call-done = bf16[2048,2048]{1,0:T(8,128)(2,1)} async-done(((bf16[64,2048]{1,0:T(8,128)(2,1)}), bf16[2048,2048]{1,0:T(8,128)(2,1)}) %all-gather.24.cloned.1.call-update) | async-done | bytes 8388624 | tf_op jit(solution)/shard_map/all_gather | solution.py:152
  161.5 40.8 %all_gather.74 = bf16[1024,256]{1,0:T(8,128)(2,1)S(1)} all-gather(bf16[32,256]{1,0:T(8,128)(2,1)S(1)} %copy-done.65), channel_id=1, replica_groups=mesh['rows'=8,'cam'=4] {'rows','cam'}, dimensions={0}, use_global_device_ids=true | all-gather | bytes 540672 | tf_op jit(solution)/shard_map/all_gather | solution.py:157
  202.6 38.3 all_gather.72
  243.5 22.1 all-gather.20.cloned.1.call-done
  267.2 23.4 all-gather.28.cloned.1.call-done
  314.0 28.5 reduce-scatter.23.cloned.1.call-done
  343.8 78.7 %all-gather.30.cloned.1.call-done = bf16[2048,2048]{1,0:T(8,128)(2,1)} async-done(((bf16[64,2048]{1,0:T(8,128)(2,1)}), bf16[2048,2048]{1,0:T(8,128)(2,1)}) %all-gather.30.cloned.1.call-update) | async-done | bytes 8388624 | tf_op jit(solution)/shard_map/all_gather | solution.py:155
  439.0 46.8 %all-gather.40.cloned.1.call-done = bf16[1024,2048]{1,0:T(8,128)(2,1)} async-done(((bf16[32,2048]{1,0:T(8,128)(2,1)}), bf16[1024,2048]{1,0:T(8,128)(2,1)}) %all-gather.40.cloned.1.call-update) | async-done | bytes 4194320 | tf_op jit(solution)/shard_map/all_gather | solution.py:159
  494.8 41.0 %all-gather.42.cloned.1.call-done = bf16[1024,1024]{1,0:T(8,128)(2,1)} async-done(((bf16[128,1024]{1,0:T(8,128)(2,1)}), bf16[1024,1024]{1,0:T(8,128)(2,1)}) %all-gather.42.cloned.1.call-update) | async-done | bytes 2097168 | tf_op jit(solution)/shard_map/all_gather | solution.py:177
  537.9 47.6 %all-gather.44.cloned.1.call-done = bf16[1024,1024]{1,0:T(8,128)(2,1)} async-done(((bf16[128,1024]{1,0:T(8,128)(2,1)}), bf16[1024,1024]{1,0:T(8,128)(2,1)}) %all-gather.44.cloned.1.call-update) | async-done | bytes 2097168 | tf_op jit(solution)/shard_map/all_gather | solution.py:178
  587.5 47.7 %all-gather.46.cloned.1.call-done = bf16[1024,1024]{1,0:T(8,128)(2,1)} async-done(((bf16[128,1024]{1,0:T(8,128)(2,1)}), bf16[1024,1024]{1,0:T(8,128)(2,1)}) %all-gather.46.cloned.1.call-update) | async-done | bytes 2097168 | tf_op jit(solution)/shard_map/all_gather | solution.py:179
  658.4 229.4 %all-gather.34.cloned.1.call-done = bf16[2048,4096]{1,0:T(8,128)(2,1)} async-done(((bf16[256,4096]{1,0:T(8,128)(2,1)}), bf16[2048,4096]{1,0:T(8,128)(2,1)}) %all-gather.34.cloned.1.call-update) | async-done | bytes 16777232 | tf_op jit(solution)/shard_map/all_gather | solution.py:174
  902.7 212.5 %all-gather.36.cloned.1.call-done = bf16[2048,4096]{1,0:T(8,128)(2,1)} async-done(((bf16[256,4096]{1,0:T(8,128)(2,1)}), bf16[2048,4096]{1,0:T(8,128)(2,1)}) %all-gather.36.cloned.1.call-update) | async-done | bytes 16777232 | tf_op jit(solution)/shard_map/all_gather | solution.py:175
  1137.4 229.3 %all-gather.38.cloned.1.call-done = bf16[2048,4096]{1,0:T(8,128)(2,1)} async-done(((bf16[256,4096]{1,0:T(8,128)(2,1)}), bf16[2048,4096]{1,0:T(8,128)(2,1)}) %all-gather.38.cloned.1.call-update) | async-done | bytes 16777232 | tf_op jit(solution)/shard_map/all_gather | solution.py:176
  1366.7 25.1 multiply_convert_fusion
  1449.5 32.1 reduce-scatter.25.cloned.1.call-done
  1497.3 16.8 all-gather.50.cloned.1.call-done
  1629.3 66.9 %reduce-scatter.57.cloned.1.call-done = bf16[128,1024]{1,0:T(8,128)(2,1)} async-done(((bf16[1024,1024]{1,0:T(8,128)(2,1)}), bf16[128,1024]{1,0:T(8,128)(2,1)}) %reduce-scatter.57.cloned.1.call-update) | async-done | bytes 262160 | tf_op jit(solution)/shard_map/reduce_scatter | solution.py:382
  1698.0 69.1 %reduce-scatter.59.cloned.1.call-done = bf16[128,1024]{1,0:T(8,128)(2,1)} async-done(((bf16[1024,1024]{1,0:T(8,128)(2,1)}), bf16[128,1024]{1,0:T(8,128)(2,1)}) %reduce-scatter.59.cloned.1.call-update) | async-done | bytes 262160 | tf_op jit(solution)/shard_map/reduce_scatter | solution.py:385
  1780.0 42.9 %all-reduce.5 = (f32[2048]{0:T(1024)S(1)}, f32[2048]{0:T(1024)S(1)}, f32[1024]{0:T(1024)S(1)}, f32[1024]{0:T(1024)S(1)}) all-reduce(f32[2048]{0:T(1024)S(1)} %get-tuple-element.225, f32[2048]{0:T(1024)S(1)} %get-tuple-element.223, f32[1024]{0:T(1024)S(1)} %get-tuple-element.229, ...), channel_id=18, replica_groups=mesh['rows'=8,'cam'=4] {'rows','cam'}, use_global_device_ids=true, to_apply=%region_28.29.clone | all-reduce | flops 6144 | bytes 49152
  1827.1 224.0 %reduce-scatter.51.cloned.1.call-done = bf16[256,4096]{1,0:T(8,128)(2,1)} async-done(((bf16[2048,4096]{1,0:T(8,128)(2,1)}), bf16[256,4096]{1,0:T(8,128)(2,1)}) %reduce-scatter.51.cloned.1.call-update) | async-done | bytes 2097168 | tf_op jit(solution)/shard_map/reduce_scatter | solution.py:373
  2055.3 278.9 %reduce-scatter.53.cloned.1.call-done = bf16[256,4096]{1,0:T(8,128)(2,1)} async-done(((bf16[2048,4096]{1,0:T(8,128)(2,1)}), bf16[256,4096]{1,0:T(8,128)(2,1)}) %reduce-scatter.53.cloned.1.call-update) | async-done | bytes 2097168 | tf_op jit(solution)/shard_map/reduce_scatter | solution.py:376
  2338.2 279.0 %reduce-scatter.55.cloned.1.call-done = bf16[256,4096]{0,1:T(8,128)(2,1)} async-done(((bf16[2048,4096]{0,1:T(8,128)(2,1)}), bf16[256,4096]{0,1:T(8,128)(2,1)}) %reduce-scatter.55.cloned.1.call-update) | async-done | bytes 2097168 | tf_op jit(solution)/shard_map/reduce_scatter | solution.py:379
  2621.6 134.3 %reduce-scatter.45.cloned.1.call-done = f32[32,256]{1,0:T(8,128)} async-done(((f32[1024,256]{1,0:T(8,128)}), f32[32,256]{1,0:T(8,128)}) %reduce-scatter.45.cloned.1.call-update) | async-done | bytes 32784 | tf_op jit(solution)/shard_map/reduce_scatter | solution.py:364
  2755.8 135.2 %reduce-scatter.47.cloned.1.call-done = f32[32,256]{1,0:T(8,128)} async-done(((f32[1024,256]{1,0:T(8,128)}), f32[32,256]{1,0:T(8,128)}) %reduce-scatter.47.cloned.1.call-update) | async-done | bytes 32784 | tf_op jit(solution)/shard_map/reduce_scatter | solution.py:365
  2891.0 137.3 %reduce-scatter.37.cloned.1.call-done = f32[64,256]{1,0:T(8,128)} async-done(((f32[2048,256]{1,0:T(8,128)}), f32[64,256]{1,0:T(8,128)}) %reduce-scatter.37.cloned.1.call-update) | async-done | bytes 65552 | tf_op jit(solution)/shard_map/reduce_scatter | solution.py:360
  3028.3 137.2 %reduce-scatter.39.cloned.1.call-done = f32[64,256]{1,0:T(8,128)} async-done(((f32[2048,256]{1,0:T(8,128)}), f32[64,256]{1,0:T(8,128)}) %reduce-scatter.39.cloned.1.call-update) | async-done | bytes 65552 | tf_op jit(solution)/shard_map/reduce_scatter | solution.py:361
  3165.5 148.7 %reduce-scatter.49.cloned.1.call-done = f32[32,2048]{1,0:T(8,128)} async-done(((f32[1024,2048]{1,0:T(8,128)}), f32[32,2048]{1,0:T(8,128)}) %reduce-scatter.49.cloned.1.call-update) | async-done | bytes 262160 | tf_op jit(solution)/shard_map/reduce_scatter | solution.py:366
  3314.3 148.8 %reduce-scatter.43.cloned.1.call-done = f32[32,2048]{1,0:T(8,128)} async-done(((f32[1024,2048]{1,0:T(8,128)}), f32[32,2048]{1,0:T(8,128)}) %reduce-scatter.43.cloned.1.call-update) | async-done | bytes 262160 | tf_op jit(solution)/shard_map/reduce_scatter | solution.py:363
  3463.1 181.7 %reduce-scatter.41.cloned.1.call-done = f32[64,2048]{1,0:T(8,128)} async-done(((f32[2048,2048]{1,0:T(8,128)}), f32[64,2048]{1,0:T(8,128)}) %reduce-scatter.41.cloned.1.call-update) | async-done | bytes 524304 | tf_op jit(solution)/shard_map/reduce_scatter | solution.py:362
  3644.7 187.4 %reduce-scatter.35.cloned.1.call-done = f32[64,2048]{1,0:T(8,128)} async-done(((f32[2048,2048]{1,0:T(8,128)}), f32[64,2048]{1,0:T(8,128)}) %reduce-scatter.35.cloned.1.call-update) | async-done | bytes 524304 | tf_op jit(solution)/shard_map/reduce_scatter | solution.py:359
  (348 shorter events, 352.9 us)
Async XLA Ops:
  7.9 146.1 %all-gather.24.cloned.1.call-start = ((), (), s32[]{:S(2)}) async-start(), calls=%async_computation.22 | async-start | bytes 8650752 | tf_op jit(solution)/shard_map/all_gather | solution.py:152
  8.7 233.2 %all-gather.22.cloned.1.call-start = ((), (), s32[]{:S(2)}) async-start(), calls=%async_computation.21 | async-start | bytes 1081344 | tf_op jit(solution)/shard_map/all_gather | solution.py:153
  9.4 256.1 %all-gather.20.cloned.1.call-start = ((), (), s32[]{:S(2)}) async-start(), calls=%async_computation.20 | async-start | bytes 1081344 | tf_op jit(solution)/shard_map/all_gather | solution.py:154
  10.0 280.6 %all-gather.28.cloned.1.call-start = ((), (), s32[]{:S(2)}) async-start(), calls=%async_computation.24 | async-start | bytes 2949120 | tf_op jit(solution)/shard_map/all_gather | solution.py:209
  159.7 182.8 %reduce-scatter.23.cloned.1.call-start = ((), (), s32[]{:S(2)}) async-start(), calls=%async_computation.25 | async-start | bytes 2949120 | tf_op jit(solution)/shard_map/reduce_scatter | solution.py:232
  309.5 112.9 %all-gather.30.cloned.1.call-start = ((), (), s32[]{:S(2)}) async-start(), calls=%async_computation.26 | async-start | bytes 8650752 | tf_op jit(solution)/shard_map/all_gather | solution.py:155
  310.3 175.5 %all-gather.40.cloned.1.call-start = ((), (), s32[]{:S(2)}) async-start(), calls=%async_computation.32 | async-start | bytes 4325376 | tf_op jit(solution)/shard_map/all_gather | solution.py:159
  311.0 224.8 %all-gather.42.cloned.1.call-start = ((), (), s32[]{:S(2)}) async-start(), calls=%async_computation.33 | async-start | bytes 2359296 | tf_op jit(solution)/shard_map/all_gather | solution.py:177
  311.7 273.7 %all-gather.44.cloned.1.call-start = ((), (), s32[]{:S(2)}) async-start(), calls=%async_computation.34 | async-start | bytes 2359296 | tf_op jit(solution)/shard_map/all_gather | solution.py:178
  312.3 322.9 %all-gather.46.cloned.1.call-start = ((), (), s32[]{:S(2)}) async-start(), calls=%async_computation.35 | async-start | bytes 2359296 | tf_op jit(solution)/shard_map/all_gather | solution.py:179
  313.1 345.3 %all-gather.32.cloned.1.call-start = ((), (), s32[]{:S(2)}) async-start(), calls=%async_computation.27 | async-start | bytes 2621440 | tf_op jit(solution)/shard_map/all_gather | solution.py:246
  430.8 457.0 %all-gather.34.cloned.1.call-start = ((), (), s32[]{:S(2)}) async-start(), calls=%async_computation.28 | async-start | bytes 18874368 | tf_op jit(solution)/shard_map/all_gather | solution.py:174
  431.6 683.7 %all-gather.36.cloned.1.call-start = ((), (), s32[]{:S(2)}) async-start(), calls=%async_computation.29 | async-start | bytes 18874368 | tf_op jit(solution)/shard_map/all_gather | solution.py:175
  432.1 705.3 %all-gather.48.cloned.1.call-start = ((), (), s32[]{:S(2)}) async-start(), calls=%async_computation.37 | async-start | bytes 2621440 | tf_op jit(solution)/shard_map/all_gather | solution.py:248
  432.7 934.0 %all-gather.38.cloned.1.call-start = ((), (), s32[]{:S(2)}) async-start(), calls=%async_computation.30 | async-start | bytes 18874368 | tf_op jit(solution)/shard_map/all_gather | solution.py:176
  433.3 1000.8 %reduce-scatter.31.cloned.1.call-start = ((), (), s32[]{:S(2)}) async-start(), calls=%async_computation.39 | async-start | bytes 163840 | tf_op jit(solution)/shard_map/reduce_scatter | solution.py:273
  641.4 793.8 %reduce-scatter.27.cloned.1.call-start = ((), (), s32[]{:S(2)}) async-start(), calls=%async_computation.36 | async-start | bytes 163840 | tf_op jit(solution)/shard_map/reduce_scatter | solution.py:257
  644.6 803.4 %reduce-scatter.29.cloned.1.call-start = ((), (), s32[]{:S(2)}) async-start(), calls=%async_computation.38 | async-start | bytes 2621440 | tf_op jit(solution)/shard_map/reduce_scatter | solution.py:270
  1489.9 105.5 %reduce-scatter.33.cloned.1.call-start = ((), (), s32[]{:S(2)}) async-start(), calls=%async_computation.41 | async-start | bytes 2949120 | tf_op jit(solution)/shard_map/reduce_scatter | solution.py:327
  1524.3 172.0 %reduce-scatter.57.cloned.1.call-start = ((), (), s32[]{:S(2)}) async-start(), calls=%async_computation.53 | async-start | bytes 2359296 | tf_op jit(solution)/shard_map/reduce_scatter | solution.py:382
  1526.6 240.5 %reduce-scatter.59.cloned.1.call-start = ((), (), s32[]{:S(2)}) async-start(), calls=%async_computation.54 | async-start | bytes 2359296 | tf_op jit(solution)/shard_map/reduce_scatter | solution.py:385
  1528.7 522.4 %reduce-scatter.51.cloned.1.call-start = ((), (), s32[]{:S(2)}) async-start(), calls=%async_computation.50 | async-start | bytes 18874368 | tf_op jit(solution)/shard_map/reduce_scatter | solution.py:373
  1544.0 790.1 %reduce-scatter.53.cloned.1.call-start = ((), (), s32[]{:S(2)}) async-start(), calls=%async_computation.51 | async-start | bytes 18874368 | tf_op jit(solution)/shard_map/reduce_scatter | solution.py:376
  1560.2 1057.0 %reduce-scatter.55.cloned.1.call-start = ((), (), s32[]{:S(2)}) async-start(), calls=%async_computation.52 | async-start | bytes 18874368 | tf_op jit(solution)/shard_map/reduce_scatter | solution.py:379
  1576.5 1179.3 %reduce-scatter.45.cloned.1.call-start = ((), (), s32[]{:S(2)}) async-start(), calls=%async_computation.47 | async-start | bytes 1081344 | tf_op jit(solution)/shard_map/reduce_scatter | solution.py:364
  1581.6 1309.4 %reduce-scatter.47.cloned.1.call-start = ((), (), s32[]{:S(2)}) async-start(), calls=%async_computation.48 | async-start | bytes 1081344 | tf_op jit(solution)/shard_map/reduce_scatter | solution.py:365
  1586.6 1441.6 %reduce-scatter.37.cloned.1.call-start = ((), (), s32[]{:S(2)}) async-start(), calls=%async_computation.43 | async-start | bytes 2162688 | tf_op jit(solution)/shard_map/reduce_scatter | solution.py:360
  1588.6 1576.9 %reduce-scatter.39.cloned.1.call-start = ((), (), s32[]{:S(2)}) async-start(), calls=%async_computation.44 | async-start | bytes 2162688 | tf_op jit(solution)/shard_map/reduce_scatter | solution.py:361
  1590.6 1723.7 %reduce-scatter.49.cloned.1.call-start = ((), (), s32[]{:S(2)}) async-start(), calls=%async_computation.49 | async-start | bytes 8650752 | tf_op jit(solution)/shard_map/reduce_scatter | solution.py:366
  1595.3 1867.8 %reduce-scatter.43.cloned.1.call-start = ((), (), s32[]{:S(2)}) async-start(), calls=%async_computation.46 | async-start | bytes 8650752 | tf_op jit(solution)/shard_map/reduce_scatter | solution.py:363
  1600.9 2043.8 %reduce-scatter.41.cloned.1.call-start = ((), (), s32[]{:S(2)}) async-start(), calls=%async_computation.45 | async-start | bytes 17301504 | tf_op jit(solution)/shard_map/reduce_scatter | solution.py:362
  1609.1 2223.0 %reduce-scatter.35.cloned.1.call-start = ((), (), s32[]{:S(2)}) async-start(), calls=%async_computation.42 | async-start | bytes 17301504 | tf_op jit(solution)/shard_map/reduce_scatter | solution.py:359
  (79 other events, 4209.5 us)
Sparse Core Ops, SparseCore 0:
  10.9 64.4 all-gather.25
  78.2 75.8 all-gather.23
  156.9 52.9 all-gather.21
  212.6 52.9 all-gather.19
  267.6 23.0 all-gather.27
  309.6 32.8 reduce-scatter.22
  345.3 77.0 all-gather.29
  425.3 60.4 all-gather.39
  487.9 47.8 all-gather.41
  537.8 47.6 all-gather.43
  587.6 47.6 all-gather.45
  660.5 227.2 all-gather.33
  889.7 225.4 all-gather.35
  1139.4 227.2 all-gather.37
  1418.7 29.3 reduce-scatter.28
  1450.4 31.1 reduce-scatter.24
  1490.0 24.0 all-gather.49
  1520.9 32.8 reduce-scatter.32
  1557.3 68.2 reduce-scatter.60
  1629.0 67.1 reduce-scatter.56
  1699.8 67.2 reduce-scatter.58
  1770.7 280.4 reduce-scatter.50
  2054.8 279.3 reduce-scatter.52
  2337.9 279.3 reduce-scatter.54
  2620.1 135.6 reduce-scatter.44
  2758.5 132.4 reduce-scatter.46
  2893.8 134.4 reduce-scatter.36
  3031.1 134.3 reduce-scatter.38
  3168.2 145.9 reduce-scatter.48
  3317.1 145.9 reduce-scatter.42
  3466.0 178.7 reduce-scatter.40
  3647.5 184.6 reduce-scatter.34
  (4 shorter events, 79.1 us)
where the time goes:
time: 3850 us; the launch traced here: 3840 us
  waiting for transfers between devices  3370 us (88%)
  matrix products  247 us (6%)
  blocking collectives  149 us (4%)
    reduce_scatter x1, waiting for transfers between devices, body(): lax.psum_scatter(lead_ffgrads[2].astype(jnp.bfloat16), 'rows', scatter_di...  279 us
    reduce_scatter x1, waiting for transfers between devices, body(): lax.psum_scatter(lead_ffgrads[1].astype(jnp.bfloat16), 'rows', scatter_di...  279 us
    all_gather x1, waiting for transfers between devices, body(): lax.all_gather(prefix_gate, 'rows', axis=0, tiled=True)  229 us
    all_gather x1, waiting for transfers between devices, body(): lax.all_gather(prefix_down, 'rows', axis=0, tiled=True)  229 us
    reduce_scatter x1, waiting for transfers between devices, body(): lax.psum_scatter(lead_ffgrads[0].astype(jnp.bfloat16), 'rows', scatter_di...  224 us
    all_gather x1, waiting for transfers between devices, body(): lax.all_gather(prefix_expand, 'rows', axis=0, tiled=True)  212 us
    reduce_scatter x1, waiting for transfers between devices, body(): lax.psum_scatter(lead_proj[0], ('rows', 'cam'), scatter_dimension=0, tile...  187 us
    reduce_scatter x1, waiting for transfers between devices, body(): lax.psum_scatter(lead_mixing, ('rows', 'cam'), scatter_dimension=0, tiled...  182 us
  transfers between devices with their start and end apart: 36, of which 32 were waited for; matrix products, arithmetic and copies ran while one was open for 7% of the time, Pallas kernels for 0%

commit v1 on v0

v1 whole, which is shorter than its diff:
```python
import functools

import jax
import jax.numpy as jnp
from jax import lax
from jax.experimental import pallas as pl
from jax.experimental.pallas import tpu as pltpu
from jax.sharding import PartitionSpec as P

ACTT = 32


epsilon = 1e-06
masked_score = -1e30


class Place:
    def __init__(self, depth, breadth):
        self.depth, self.breadth = depth, breadth
        row, member = lax.axis_index("rows"), lax.axis_index("cam")
        self.z, self.y = row // 2, row % 2
        self.x, self.k = member // 2, member % 2

    def device(self, z=None, y=None, x=None, k=None):
        z = self.z if z is None else z
        y = self.y if y is None else y
        x = self.x if x is None else x
        k = self.k if k is None else k
        return (z * 2 + y, x * 2 + k)

    def later_x(self, step):
        return lax.rem(self.x + step, self.breadth)

    def later_z(self, step):
        return lax.rem(self.z + step, self.depth)


def guarded(condition, action):
    if condition is None:
        action()
    else:
        pl.when(condition)(action)


class Transfer:
    def __init__(self, net, source, target, device, sends=None, gets=None):
        self.net, self.number = net, net.remote
        net.remote += 1
        self.source, self.target, self.device = source, target, device
        self.sends, self.gets = sends, gets
        net.pending.append(self)

    def describe(self):
        return pltpu.make_async_remote_copy(
            src_ref=self.source(),
            dst_ref=self.target(),
            send_sem=self.net.sent.at[self.number],
            recv_sem=self.net.received.at[self.number],
            device_id=self.device,
            device_id_type=pl.DeviceIdType.MESH,
        )

    def start(self):
        guarded(self.sends, lambda: self.describe().start())

    def got(self):
        guarded(self.gets, lambda: self.describe().wait_recv())

    def finish(self):
        guarded(self.sends, lambda: self.describe().wait_send())


class Local:
    def __init__(self, net, source, target):
        self.net, self.number = net, net.local
        net.local += 1
        self.source, self.target = source, target

    def describe(self):
        return pltpu.make_async_copy(
            self.source(), self.target(), self.net.moved.at[self.number]
        )

    def start(self):
        self.describe().start()
        return self

    def wait(self):
        self.describe().wait()


class Net:
    def __init__(self, sent, received, moved):
        self.sent, self.received, self.moved = sent, received, moved
        self.remote, self.local = 0, 0
        self.pending = []

    def settle(self):
        for transfer in self.pending:
            transfer.finish()


def greet(at, kinds):
    peers = []
    count = 0
    if "z" in kinds and "deal" not in kinds:
        count = count + (at.z > 0).astype(jnp.int32) + (at.z < at.depth - 1).astype(jnp.int32)
        peers.append((at.z > 0, at.device(z=at.z - 1)))
        peers.append((at.z < at.depth - 1, at.device(z=at.z + 1)))
    if "deal" in kinds:
        peers += [(None, at.device(z=at.later_z(step))) for step in range(1, at.depth)]
    if "y" in kinds:
        peers.append((None, at.device(y=1 - at.y)))
    if "cam" in kinds:
        for step in range(at.breadth):
            for core in (at.k, 1 - at.k):
                if step > 0 or core is not at.k:
                    peers.append((None, at.device(x=at.later_x(step), k=core)))
    barrier = pltpu.get_barrier_semaphore()
    for condition, device in peers:
        guarded(
            condition,
            lambda device=device: pl.semaphore_signal(
                barrier, inc=1, device_id=device, device_id_type=pl.DeviceIdType.MESH
            ),
        )
    count = count + sum(1 for condition, _ in peers if condition is None)
    pl.semaphore_wait(barrier, count)


def run_all(routines):
    routines = list(routines)
    while routines:
        alive = []
        for routine in routines:
            try:
                next(routine)
                alive.append(routine)
            except StopIteration:
                pass
        routines = alive


def add_rows(target, first, second):
    count = target.shape[0]
    step = 16 if count % 16 == 0 else 8

    def one(index, carry):
        rows = pl.ds(pl.multiple_of(index * step, step), step)
        total = first[rows, :].astype(jnp.float32) + second[rows, :].astype(jnp.float32)
        target[rows, :] = total.astype(target.dtype)
        return carry

    lax.fori_loop(0, count // step, one, 0)


def widen_rows(target, source):
    count = target.shape[0]
    step = 16 if count % 16 == 0 else 8

    def one(index, carry):
        rows = pl.ds(pl.multiple_of(index * step, step), step)
        target[rows, :] = source[rows, :].astype(target.dtype)
        return carry

    lax.fori_loop(0, count // step, one, 0)


class Chain:
    def __init__(self, net, at, own, place):
        depth = at.depth
        self.up, self.down = {}, {}
        for step in range(1, depth):
            low, high = at.z - step + 1, at.z + step - 1
            self.up[step] = Transfer(
                net,
                own if step == 1 else (lambda low=low: place(low)),
                lambda low=low: place(low),
                at.device(z=at.z + 1),
                sends=(at.z + 1 < depth) & (low >= 0),
                gets=at.z - step >= 0,
            )
            self.down[step] = Transfer(
                net,
                own if step == 1 else (lambda high=high: place(high)),
                lambda high=high: place(high),
                at.device(z=at.z - 1),
                sends=(at.z > 0) & (high < depth),
                gets=at.z + step < depth,
            )


def tags_of(at, chained):
    tags = [("own", at.z, None)]
    if chained:
        for step in range(1, at.depth):
            tags.append((("up", step), at.z - step, at.z - step >= 0))
            tags.append((("down", step), at.z + step, at.z + step < at.depth))
    return tags


def spread(net, at, shards, outs, chained):
    if chained:
        place = lambda out, z, x, k: out.at[z, x, k]
    else:
        place = lambda out, z, x, k: out.at[x, k]
    tags = tags_of(at, chained)
    chains, across, partner, locals_ = [], {}, {}, []
    for i, (shard, out) in enumerate(zip(shards, outs)):
        own = lambda shard=shard: shard
        if chained:
            chains.append(
                Chain(net, at, own, lambda z, out=out: place(out, z, at.x, at.k))
            )
        locals_.append(Local(net, own, lambda out=out: place(out, at.z, at.x, at.k)))
        for name, z, condition in tags:
            held = own if name == "own" else (lambda out=out, z=z: place(out, z, at.x, at.k))
            target = lambda out=out, z=z: place(out, z, at.x, at.k)
            partner[i, name, 0] = Transfer(
                net, held, target, at.device(k=1 - at.k), condition, condition
            )
            for step in range(1, at.breadth):
                across[i, name, step] = Transfer(
                    net, held, target, at.device(x=at.later_x(step)), condition, condition
                )
                other = at.later_x(at.breadth - step)
                arrived = lambda out=out, z=z, other=other: place(out, z, other, at.k)
                partner[i, name, step] = Transfer(
                    net, arrived, arrived, at.device(k=1 - at.k), condition, condition
                )
    count = len(shards)

    def launch(name):
        for i in range(count):
            for step in range(1, at.breadth):
                across[i, name, step].start()
        for i in range(count):
            partner[i, name, 0].start()

    def forward(name):
        for i in range(count):
            for step in range(1, at.breadth):
                across[i, name, step].got()
                partner[i, name, step].start()

    for chain in chains:
        chain.up[1].start()
        chain.down[1].start()
    launch("own")
    for move in locals_:
        move.start()
    yield
    previous = ["own"]
    if chained:
        for step in range(1, at.depth):
            for chain in chains:
                chain.up[step].got()
                if step + 1 < at.depth:
                    chain.up[step + 1].start()
            launch(("up", step))
            yield
            for chain in chains:
                chain.down[step].got()
                if step + 1 < at.depth:
                    chain.down[step + 1].start()
            launch(("down", step))
            yield
            for name in previous:
                forward(name)
            previous = [("up", step), ("down", step)]
    for name in previous:
        yield
        forward(name)
    yield
    for transfer in partner.values():
        transfer.got()
    for move in locals_:
        move.wait()


def fan(net, at, packs, outs):
    members = 2 * at.breadth
    swap, chains, across, locals_ = {}, [], {}, []
    mine = at.x * 2 + at.k
    for i, (pack, out) in enumerate(zip(packs, outs)):
        slot = lambda out=out: out.at[at.z, at.y, mine]
        locals_.append(Local(net, lambda pack=pack: pack.at[mine], slot))
        for step in range(at.breadth):
            for flip in (0, 1):
                if step == 0 and flip == 0:
                    continue
                x = at.later_x(step)
                k = 1 - at.k if flip else at.k
                swap[i, step, flip] = Transfer(
                    net,
                    lambda pack=pack, x=x, k=k: pack.at[x * 2 + k],
                    slot,
                    at.device(x=x, k=k),
                )
        block = lambda z, out=out: out.at[z, at.y]
        chains.append(Chain(net, at, lambda block=block: block(at.z), block))
        for name, z, condition in tags_of(at, True):
            held = lambda block=block, z=z: block(z)
            across[i, name] = Transfer(
                net, held, held, at.device(y=1 - at.y), condition, condition
            )
    for transfer in swap.values():
        transfer.start()
    for move in locals_:
        move.start()
    yield
    for transfer in swap.values():
        transfer.got()
    for move in locals_:
        move.wait()
    count = len(packs)
    for chain in chains:
        chain.up[1].start()
        chain.down[1].start()
    for i in range(count):
        across[i, "own"].start()
    for step in range(1, at.depth):
        yield
        for chain in chains:
            chain.up[step].got()
            if step + 1 < at.depth:
                chain.up[step + 1].start()
        for i in range(count):
            across[i, ("up", step)].start()
        yield
        for chain in chains:
            chain.down[step].got()
            if step + 1 < at.depth:
                chain.down[step + 1].start()
        for i in range(count):
            across[i, ("down", step)].start()
    yield
    for transfer in across.values():
        transfer.got()


def deal(net, at, sources, outs, stages):
    moves, across, loads, stores = {}, {}, [], []
    for i, (source, out, stage) in enumerate(zip(sources, outs, stages)):
        slot = lambda out=out: out.at[at.z, at.y]
        held = lambda stage=stage: stage
        loads.append(Local(net, lambda source=source: source(at.z), held))
        stores.append(Local(net, held, slot))
        across[i, 0] = Transfer(net, held, slot, at.device(y=1 - at.y))
        for step in range(1, at.depth):
            z = at.later_z(step)
            moves[i, step] = Transfer(
                net, lambda source=source, z=z: source(z), slot, at.device(z=z)
            )
            origin = at.later_z(at.depth - step)
            arrived = lambda out=out, origin=origin: out.at[origin, at.y]
            across[i, step] = Transfer(net, arrived, arrived, at.device(y=1 - at.y))
    for load in loads:
        load.start()
    count = len(loads)
    for i in range(count):
        for step in range(1, at.depth):
            moves[i, step].start()
    yield
    for i in range(count):
        loads[i].wait()
        stores[i].start()
        across[i, 0].start()
    for i in range(count):
        for step in range(1, at.depth):
            yield
            moves[i, step].got()
            across[i, step].start()
    yield
    for transfer in across.values():
        transfer.got()
    for store in stores:
        store.wait()


def chain_sum(net, at, own, up, down):
    rise, fall = {}, {}
    for t in range(at.depth):
        rise[t] = Transfer(
            net,
            lambda t=t: own(t),
            lambda t=t: up(t),
            at.device(z=at.z + 1),
            sends=at.z < t,
            gets=(at.z > 0) & (at.z <= t),
        )
        fall[t] = Transfer(
            net,
            lambda t=t: own(t),
            lambda t=t: down(t),
            at.device(z=at.z - 1),
            sends=at.z > t,
            gets=(at.z < at.depth - 1) & (at.z >= t),
        )
    return rise, fall


def edges_first(depth):
    order = []
    for i in range((depth + 1) // 2):
        order.append(depth - 1 - i)
        if i != depth - 1 - i:
            order.append(i)
    return order


def collect(net, at, parts, outs, buffers, chained):
    depth = at.depth if chained else 1
    order = edges_first(depth)
    part_of = (
        (lambda part, t, x, k: part.at[t, x, k]) if chained else (lambda part, t, x, k: part.at[x, k])
    )
    loads, partner, across, chains = {}, {}, {}, []
    for i, (part, buffer) in enumerate(zip(parts, buffers)):
        own, core, wide = buffer["own"], buffer["core"], buffer["wide"]
        for t in order:
            for step in range(at.breadth):
                x = at.later_x(step)
                loads[i, t, step] = Local(
                    net,
                    lambda part=part, t=t, x=x: part_of(part, t, x, at.k),
                    lambda own=own, t=t, x=x: own.at[t, x],
                )
                partner[i, t, step] = Transfer(
                    net,
                    lambda part=part, t=t, x=x: part_of(part, t, x, 1 - at.k),
                    lambda core=core, t=t, x=x: core.at[t, x],
                    at.device(k=1 - at.k),
                )
                if step > 0:
                    across[i, t, step] = Transfer(
                        net,
                        lambda own=own, t=t, x=x: own.at[t, x],
                        lambda wide=wide, t=t, step=step: wide.at[step - 1, t],
                        at.device(x=x),
                    )
        if chained:
            chains.append(
                chain_sum(
                    net,
                    at,
                    lambda t, own=own: own.at[t, at.x],
                    lambda t, buffer=buffer: buffer["up"].at[t],
                    lambda t, buffer=buffer: buffer["down"].at[t],
                )
            )
    steps = list(range(1, at.breadth)) + [0]
    count = len(parts)
    for i in range(count):
        for t in order:
            for step in steps:
                partner[i, t, step].start()
                loads[i, t, step].start()
    for i in range(count):
        own, core = buffers[i]["own"], buffers[i]["core"]
        for t in order:
            yield
            for step in steps:
                x = at.later_x(step)
                loads[i, t, step].wait()
                partner[i, t, step].got()
                add_rows(own.at[t, x], own.at[t, x], core.at[t, x])
            for step in steps[:-1]:
                across[i, t, step].start()
    for i in range(count):
        buffer = buffers[i]
        own, wide = buffer["own"], buffer["wide"]
        for t in order:
            yield
            for step in steps[:-1]:
                across[i, t, step].got()
                last = not chained and step == steps[-2]
                target = outs[i] if last else own.at[t, at.x]
                add_rows(target, own.at[t, at.x], wide.at[step - 1, t])
            if chained:
                rise, fall = chains[i]
                yield

                def finish(i=i, t=t, buffer=buffer, rise=rise, fall=fall):
                    widen_rows(outs[i], buffer["own"].at[t, at.x])
                    for moves, name in ((rise, "up"), (fall, "down")):

                        def more(moves=moves, name=name):
                            moves[t].describe().wait_recv()
                            add_rows(outs[i], outs[i], buffer[name].at[t])

                        pl.when(moves[t].gets)(more)

                def passing(t=t, buffer=buffer, rise=rise, fall=fall):
                    for moves, name in ((rise, "up"), (fall, "down")):

                        def more(moves=moves, name=name):
                            moves[t].describe().wait_recv()
                            held = buffer["own"].at[t, at.x]
                            add_rows(held, held, buffer[name].at[t])

                        pl.when(moves[t].gets)(more)

                pl.when(at.z == t)(finish)
                pl.when(at.z != t)(passing)
                rise[t].start()
                fall[t].start()


def give_back(net, at, parts, slots, buffers):
    loads, across, moves, stores = {}, {}, {}, []
    for i, (part, buffer) in enumerate(zip(parts, buffers)):
        own, core = buffer["own"], buffer["core"]
        for step in range(at.depth):
            z = at.later_z(step)
            loads[i, step] = Local(
                net,
                lambda part=part, z=z: part.at[z, at.y],
                lambda own=own, z=z: own.at[z],
            )
            across[i, step] = Transfer(
                net,
                lambda part=part, z=z: part.at[z, 1 - at.y],
                lambda core=core, z=z: core.at[z],
                at.device(y=1 - at.y),
            )
            if step > 0:
                moves[i, step] = Transfer(
                    net,
                    lambda own=own, z=z: own.at[z],
                    lambda i=i: slots[i](at.z),
                    at.device(z=z),
                )
            else:
                stores.append(
                    Local(net, lambda own=own: own.at[at.z], lambda i=i: slots[i](at.z))
                )
    count = len(parts)
    steps = list(range(1, at.depth)) + [0]
    for i in range(count):
        for step in steps:
            loads[i, step].start()
            across[i, step].start()
    for i in range(count):
        own, core = buffers[i]["own"], buffers[i]["core"]
        for step in steps:
            yield
            z = at.later_z(step)
            loads[i, step].wait()
            across[i, step].got()
            add_rows(own.at[z], own.at[z], core.at[z])
            if step > 0:
                moves[i, step].start()
            else:
                stores[i].start()
    for transfer in moves.values():
        yield
        transfer.got()
    for store in stores:
        store.wait()


def fold(net, at, parts, outs, buffers):
    mine = at.x * 2 + at.k
    members = 2 * at.breadth
    order = edges_first(at.depth)
    loads, across, chains, swap, stores = {}, {}, [], {}, []
    for i, (part, buffer) in enumerate(zip(parts, buffers)):
        own, core = buffer["own"], buffer["core"]
        for t in order:
            loads[i, t] = Local(
                net, lambda part=part, t=t: part.at[t, at.y], lambda own=own, t=t: own.at[t]
            )
            across[i, t] = Transfer(
                net,
                lambda part=part, t=t: part.at[t, 1 - at.y],
                lambda core=core, t=t: core.at[t],
                at.device(y=1 - at.y),
            )
        chains.append(
            chain_sum(
                net,
                at,
                lambda t, own=own: own.at[t],
                lambda t, buffer=buffer: buffer["up"].at[t],
                lambda t, buffer=buffer: buffer["down"].at[t],
            )
        )
        slot = lambda i=i: outs[i].at[mine]
        stores.append(Local(net, lambda own=own: own.at[at.z, mine], slot))
        for step in range(at.breadth):
            for flip in (0, 1):
                if step == 0 and flip == 0:
                    continue
                x = at.later_x(step)
                k = 1 - at.k if flip else at.k
                swap[i, step, flip] = Transfer(
                    net,
                    lambda own=own, x=x, k=k: own.at[at.z, x * 2 + k],
                    slot,
                    at.device(x=x, k=k),
                )
    count = len(parts)
    for i in range(count):
        for t in order:
            across[i, t].start()
            loads[i, t].start()
    for i in range(count):
        buffer = buffers[i]
        own, core = buffer["own"], buffer["core"]
        rise, fall = chains[i]
        for t in order:
            yield
            loads[i, t].wait()
            across[i, t].got()
            for member in range(members):
                add_rows(own.at[t, member], own.at[t, member], core.at[t, member])
            yield
            for moves, name in ((rise, "up"), (fall, "down")):

                def more(moves=moves, name=name, t=t, own=own, buffer=buffer):
                    moves[t].describe().wait_recv()
                    for member in range(members):
                        held = own.at[t, member]
                        add_rows(held, held, buffer[name].at[t, member])

                pl.when(moves[t].gets)(more)
            rise[t].start()
            fall[t].start()
        stores[i].start()
        for (j, step, flip), transfer in swap.items():
            if j == i:
                transfer.start()
    yield
    for transfer in swap.values():
        transfer.got()
    for store in stores:
        store.wait()


def exchange(label, ident, sizes, kinds, inputs, outputs, scratch, routines):
    space = lambda inside: pltpu.VMEM if inside else pl.ANY

    def kernel(*refs):
        sources = refs[: len(inputs)]
        targets = refs[len(inputs) : len(inputs) + len(outputs)]
        held = refs[len(inputs) + len(outputs) : -3]
        at, net = Place(*sizes), Net(*refs[-3:])
        greet(at, kinds)
        run_all(routines(net, at, sources, targets, held))
        net.settle()

    slots = 48 * sizes[0]
    return pl.pallas_call(
        kernel,
        name=label,
        out_shape=[shape for shape, _ in outputs],
        in_specs=[pl.BlockSpec(memory_space=space(inside)) for _, inside in inputs],
        out_specs=[pl.BlockSpec(memory_space=space(inside)) for _, inside in outputs],
        scratch_shapes=list(scratch)
        + [pltpu.SemaphoreType.DMA((slots,))] * 2
        + [pltpu.SemaphoreType.DMA((slots,))],
        compiler_params=pltpu.CompilerParams(
            collective_id=ident, has_side_effects=True, vmem_limit_bytes=60 << 20
        ),
    )(*[array for array, _ in inputs])


def shape_of(dims, kind=jnp.bfloat16):
    return jax.ShapeDtypeStruct(tuple(dims), kind)


def multiply(operand, matrix):
    return jnp.dot(operand, matrix, preferred_element_type=jnp.float32)


def against(operand, matrix):
    return lax.dot_general(
        operand, matrix, (((1,), (1,)), ((), ())), preferred_element_type=jnp.float32
    )


def outer_sum(operand, matrix):
    return lax.dot_general(
        operand, matrix, (((0,), (0,)), ((), ())), preferred_element_type=jnp.float32
    )


def norm_forward(values):
    scaling = lax.rsqrt(jnp.mean(values * values, axis=-1, keepdims=True) + epsilon)
    return (values * scaling, scaling)


def norm_backward(upstream, normed_unit, scaling, gain_vector):
    weighted = upstream * gain_vector
    average = jnp.mean(weighted * normed_unit, axis=-1, keepdims=True)
    return (scaling * (weighted - normed_unit * average), jnp.sum(upstream * normed_unit, axis=0))


def visible(query_ids, query_codes, key_ids, key_codes):
    matches = query_ids[:, None] == key_ids[None, :]
    return jnp.logical_and(matches, key_codes[None, :] <= query_codes[:, None])


def gated(gate_value, expand_value):
    return jax.nn.gelu(gate_value, approximate=True) * expand_value


def low(values):
    return values.astype(jnp.bfloat16)


def feed_forward(normed_rows, cotangent, gate_weight, expand_weight, down_weight):
    gate_value = multiply(normed_rows, gate_weight)
    expand_value = multiply(normed_rows, expand_weight)
    inside, pullback = jax.vjp(gated, gate_value, expand_value)
    inside_low = low(inside)
    part = low(against(inside_low, down_weight))
    inside_grad = multiply(cotangent, down_weight)
    gate_grad, expand_grad = pullback(inside_grad)
    gate_low, expand_low = low(gate_grad), low(expand_grad)
    normed_grad = low(against(gate_low, gate_weight) + against(expand_low, expand_weight))
    weight_grads = (
        outer_sum(normed_rows, gate_low),
        outer_sum(normed_rows, expand_low),
        outer_sum(cotangent, inside_low),
    )
    return (part, normed_grad, weight_grads)


def by_member(parts, members):
    rows = parts[0].shape[0]
    columns = jnp.concatenate([part.reshape(rows, members, -1) for part in parts], 2)
    return jnp.swapaxes(columns, 0, 1)


def body(
    prefix_tokens,
    action_tokens,
    prefix_cotangent,
    action_cotangent,
    prefix_segments,
    action_codes,
    prefix_query,
    prefix_key,
    prefix_value,
    prefix_mixer,
    action_query,
    action_key,
    action_value,
    action_mixer,
    prefix_prenorm,
    prefix_midnorm,
    action_prenorm,
    action_midnorm,
    prefix_gate,
    prefix_expand,
    prefix_down,
    action_gate,
    action_expand,
    action_down,
):
    members = lax.axis_size("cam")
    row_count = lax.axis_size("rows")
    depth, breadth = row_count // 2, members // 2
    sizes = (depth, breadth)
    head_size = prefix_key.shape[1]
    width = prefix_query.shape[1] // members
    heads = width // head_size
    pair = 2 * head_size // members
    inverse = float(head_size) ** (-0.5)
    lead_count, lead_width = prefix_tokens.shape
    tail_count, tail_width = action_tokens.shape
    idents = iter(range(100))

    def cam_spread(label, shards):
        return exchange(
            label,
            next(idents),
            sizes,
            ("cam",),
            [(shard, True) for shard in shards],
            [(shape_of((breadth, 2) + shard.shape), False) for shard in shards],
            [],
            lambda net, at, ins, outs, held: [spread(net, at, ins, outs, False)],
        )

    def cam_collect(label, parts):
        blocks = [part.shape[-2:] for part in parts]
        scratch = []
        for block in blocks:
            scratch += [
                pltpu.VMEM((1, breadth) + block, jnp.bfloat16),
                pltpu.VMEM((1, breadth) + block, jnp.bfloat16),
                pltpu.VMEM((breadth - 1, 1) + block, jnp.bfloat16),
            ]

        def routines(net, at, ins, outs, held):
            buffers = [
                dict(own=held[3 * i], core=held[3 * i + 1], wide=held[3 * i + 2])
                for i in range(len(parts))
            ]
            return [collect(net, at, ins, outs, buffers, False)]

        return exchange(
            label,
            next(idents),
            sizes,
            ("cam",),
            [(part, False) for part in parts],
            [(shape_of(block, jnp.float32), True) for block in blocks],
            scratch,
            routines,
        )

    lead_float = prefix_tokens.astype(jnp.float32)
    tail_float = action_tokens.astype(jnp.float32)
    lead_unit, lead_scale = norm_forward(lead_float)
    tail_unit, tail_scale = norm_forward(tail_float)
    lead_low = low(lead_unit * prefix_prenorm)
    tail_low = low(tail_unit * action_prenorm)
    lead_pack = by_member([prefix_query, jnp.concatenate([prefix_key, prefix_value], 1)], members)
    tail_pack = by_member([action_query, jnp.concatenate([action_key, action_value], 1)], members)
    first = [lead_low, tail_low, lead_pack, tail_pack]
    fanned = lambda pack: (shape_of((depth, 2) + pack.shape), False)
    lead_normed, tail_normed, lead_in, tail_in = exchange(
        "first",
        next(idents),
        sizes,
        ("z", "y", "cam"),
        [(array, True) for array in first],
        [(shape_of((breadth, 2) + array.shape), False) for array in first[:2]]
        + [fanned(lead_pack), fanned(tail_pack)],
        [],
        lambda net, at, ins, outs, held: [
            fan(net, at, ins[2:], outs[2:]),
            spread(net, at, ins[:2], outs[:2], False),
        ],
    )
    lead_normed = lead_normed.reshape(-1, lead_width)
    tail_normed = tail_normed.reshape(-1, tail_width)
    member_place = lax.axis_index("cam")
    lead_in = lead_in.reshape(lead_width, -1)
    tail_in = tail_in.reshape(tail_width, -1)
    lead_total, tail_total = lead_normed.shape[0], tail_normed.shape[0]

    projected = low(
        jnp.concatenate([multiply(lead_normed, lead_in), multiply(tail_normed, tail_in)], 0)
    )
    (pairs,) = cam_spread("pairs", [projected[:, width:]])
    pairs = jnp.swapaxes(pairs.reshape(members, -1, pair), 0, 1).reshape(-1, 2 * head_size)

    lead_mixers = by_member([prefix_mixer], members)
    tail_mixers = by_member([action_mixer], members)
    lead_slice = prefix_gate.shape[1] // depth
    tail_slice = action_gate.shape[1] // depth
    lead_block, tail_block = prefix_gate.shape[0], action_gate.shape[0]
    tail_weights = [
        jnp.swapaxes(weight.reshape(tail_block, depth, tail_slice), 0, 1)
        for weight in (action_gate, action_expand, action_down)
    ]
    second = (
        [(prefix_gate, False), (prefix_expand, False), (prefix_down, False)]
        + [(weight, False) for weight in tail_weights]
        + [(lead_mixers, True), (tail_mixers, True)]
    )

    def second_routines(net, at, ins, outs, held):
        def columns(ref):
            return lambda z: ref.at[
                :, pl.ds(pl.multiple_of(z * lead_slice, lead_slice), lead_slice)
            ]

        def planes(ref):
            return lambda z: ref.at[z]

        sources = [columns(ref) for ref in ins[:3]] + [planes(ref) for ref in ins[3:6]]
        return [
            fan(net, at, ins[6:8], outs[6:8]),
            deal(net, at, sources, outs[:6], held),
        ]

    dealt = exchange(
        "second",
        next(idents),
        sizes,
        ("z", "deal", "y", "cam"),
        second,
        [(shape_of((depth, 2, lead_block, lead_slice)), False)] * 3
        + [(shape_of((depth, 2, tail_block, tail_slice)), False)] * 3
        + [fanned(lead_mixers), fanned(tail_mixers)],
        [pltpu.VMEM((lead_block, lead_slice), jnp.bfloat16)] * 3
        + [pltpu.VMEM((tail_block, tail_slice), jnp.bfloat16)] * 3,
        second_routines,
    )
    lead_gate, lead_expand, lead_down = [w.reshape(lead_width, lead_slice) for w in dealt[:3]]
    tail_gate, tail_expand, tail_down = [w.reshape(tail_width, tail_slice) for w in dealt[3:6]]
    mine = lambda fans, total: fans.reshape(total, width)
    lead_mix, tail_mix = mine(dealt[6], lead_width), mine(dealt[7], tail_width)

    segment_row = prefix_segments[0]
    code_row = action_codes[0]
    token_ids = jnp.concatenate(
        [segment_row, jnp.arange(code_row.shape[0], dtype=jnp.int32) // ACTT]
    )
    token_codes = jnp.concatenate([jnp.zeros(segment_row.shape, jnp.int32), code_row])
    queries = projected[:, :width].reshape(-1, heads, head_size)
    keys, values = pairs[:, :head_size], pairs[:, head_size:]
    allowed = visible(token_ids, token_codes, token_ids, token_codes)
    logits = jnp.einsum("qhd,kd->hqk", queries, keys, preferred_element_type=jnp.float32) * inverse
    scores = jnp.where(allowed[None], logits, masked_score)
    exponent = jnp.exp(scores - jnp.max(scores, axis=2, keepdims=True))
    totals = jnp.transpose(jnp.sum(exponent, axis=2))[:, :, None]
    probs = low(exponent)
    attention = (
        jnp.einsum("hqk,kd->qhd", probs, values, preferred_element_type=jnp.float32) / totals
    )
    mixed = low(attention.reshape(-1, width))
    cam_blocks = lambda rows: low(rows).reshape(breadth, 2, -1, rows.shape[1])
    lead_sum, tail_sum = cam_collect(
        "mixing",
        [
            cam_blocks(against(mixed[:lead_total], lead_mix)),
            cam_blocks(against(mixed[lead_total:], tail_mix)),
        ],
    )
    lead_hidden = lead_float + lead_sum
    tail_hidden = tail_float + tail_sum
    lead_center, lead_factor = norm_forward(lead_hidden)
    tail_center, tail_factor = norm_forward(tail_hidden)
    lead_second = low(lead_center * prefix_midnorm)
    tail_second = low(tail_center * action_midnorm)

    chunks = max(1, depth // 4)
    lead_rows, tail_rows = lead_count // chunks, tail_count // chunks
    sums, grads = [], None
    for chunk in range(chunks):
        cut = lambda array: array.reshape(chunks, -1, array.shape[1])[chunk]
        shards = [cut(prefix_cotangent), cut(action_cotangent), cut(lead_second), cut(tail_second)]
        if chunk > 0:
            shards, sums = lax.optimization_barrier((shards, sums))
        gathered = exchange(
            "gather" + str(chunk),
            next(idents),
            sizes,
            ("z", "cam"),
            [(shard, True) for shard in shards],
            [(shape_of((depth, breadth, 2) + shard.shape), False) for shard in shards],
            [],
            lambda net, at, ins, outs, held: [
                spread(net, at, ins[2:], outs[2:], True),
                spread(net, at, ins[:2], outs[:2], True),
            ],
        )
        lead_upper, tail_upper, lead_all, tail_all = [
            array.reshape(-1, array.shape[-1]) for array in gathered
        ]
        lead_out, lead_back, lead_ffgrads = feed_forward(
            lead_all, lead_upper, lead_gate, lead_expand, lead_down
        )
        tail_out, tail_back, tail_ffgrads = feed_forward(
            tail_all, tail_upper, tail_gate, tail_expand, tail_down
        )
        fresh = list(lead_ffgrads) + list(tail_ffgrads)
        grads = fresh if grads is None else [one + other for one, other in zip(grads, fresh)]
        last = chunk + 1 == chunks
        parts = [
            rows.reshape(depth, breadth, 2, -1, rows.shape[1])
            for rows in (lead_back, tail_back, lead_out, tail_out)
        ]
        blocks = [part.shape[3:] for part in parts]
        scratch = []
        for block in blocks:
            scratch += [
                pltpu.VMEM((depth, breadth) + block, jnp.bfloat16),
                pltpu.VMEM((depth, breadth) + block, jnp.bfloat16),
                pltpu.VMEM((breadth - 1, depth) + block, jnp.bfloat16),
                pltpu.VMEM((depth,) + block, jnp.bfloat16),
                pltpu.VMEM((depth,) + block, jnp.bfloat16),
            ]

        def routines(net, at, ins, outs, held):
            names = ("own", "core", "wide", "up", "down")
            buffers = [dict(zip(names, held[5 * i : 5 * i + 5])) for i in range(len(parts))]
            return [collect(net, at, ins, outs, buffers, True)]

        sums.append(
            exchange(
                "collect" + str(chunk),
                next(idents),
                sizes,
                ("z", "cam"),
                [(part, False) for part in parts],
                [(shape_of(block, jnp.float32), True) for block in blocks],
                scratch,
                routines,
            )
        )
    lead_summed, tail_summed, lead_branch, tail_branch = [
        parts[0] if chunks == 1 else jnp.concatenate(parts, 0) for parts in zip(*sums)
    ]
    lead_result = low(lead_hidden + lead_branch)
    tail_result = low(tail_hidden + tail_branch)

    grads = [low(grad) for grad in grads]
    lead_returns = [grad.reshape(depth, 2, lead_block, lead_slice) for grad in grads[:3]]
    tail_returns = [grad.reshape(depth, 2, tail_block, tail_slice) for grad in grads[3:]]

    def return_routines(net, at, ins, outs, held):
        def columns(ref):
            return lambda z: ref.at[
                :, pl.ds(pl.multiple_of(z * lead_slice, lead_slice), lead_slice)
            ]

        def planes(ref):
            return lambda z: ref.at[z]

        slots = [columns(ref) for ref in outs[:3]] + [planes(ref) for ref in outs[3:]]
        buffers = [dict(own=held[2 * i], core=held[2 * i + 1]) for i in range(6)]
        return [give_back(net, at, ins, slots, buffers)]

    returned = exchange(
        "returns",
        next(idents),
        sizes,
        ("deal", "y"),
        [(part, False) for part in lead_returns + tail_returns],
        [(shape_of(prefix_gate.shape), False)] * 3
        + [(shape_of((depth, tail_block, tail_slice)), False)] * 3,
        [pltpu.VMEM((depth, lead_block, lead_slice), jnp.bfloat16)] * 6
        + [pltpu.VMEM((depth, tail_block, tail_slice), jnp.bfloat16)] * 6,
        return_routines,
    )
    ff_grads = [part.astype(jnp.float32) for part in returned[:3]] + [
        jnp.swapaxes(part, 0, 1).reshape(tail_block, -1).astype(jnp.float32)
        for part in returned[3:]
    ]

    lead_residual, lead_middle = norm_backward(
        lead_summed, lead_center, lead_factor, prefix_midnorm
    )
    tail_residual, tail_middle = norm_backward(
        tail_summed, tail_center, tail_factor, action_midnorm
    )
    lead_upstream = prefix_cotangent.astype(jnp.float32) + lead_residual
    tail_upstream = action_cotangent.astype(jnp.float32) + tail_residual
    lead_sent, tail_sent = cam_spread("sent", [low(lead_upstream), low(tail_upstream)])
    lead_sent = lead_sent.reshape(-1, lead_width)
    tail_sent = tail_sent.reshape(-1, tail_width)
    lead_mixing = outer_sum(lead_sent, mixed[:lead_total])
    tail_mixing = outer_sum(tail_sent, mixed[lead_total:])
    attention_grad = jnp.concatenate(
        [multiply(lead_sent, lead_mix), multiply(tail_sent, tail_mix)], 0
    ).reshape(-1, heads, head_size)
    scaled_grad = low(attention_grad / totals)
    deltas = jnp.sum(attention_grad * attention, axis=2, keepdims=True) / totals
    value_grad = jnp.einsum("hqk,qhd->kd", probs, scaled_grad, preferred_element_type=jnp.float32)
    prob_grad = jnp.einsum("qhd,kd->hqk", scaled_grad, values, preferred_element_type=jnp.float32)
    score_grad = low(exponent * (prob_grad - jnp.transpose(deltas, (1, 0, 2))))
    key_grad = (
        jnp.einsum("hqk,qhd->kd", score_grad, queries, preferred_element_type=jnp.float32) * inverse
    )
    query_grad = (
        jnp.einsum("hqk,kd->qhd", score_grad, keys, preferred_element_type=jnp.float32) * inverse
    )
    pair_parts = low(jnp.concatenate([key_grad, value_grad], 1)).reshape(-1, members, pair)
    (pair_grad,) = cam_collect(
        "pair_grads", [jnp.swapaxes(pair_parts, 0, 1).reshape(breadth, 2, -1, pair)]
    )
    low_grad = jnp.concatenate([low(query_grad.reshape(-1, width)), low(pair_grad)], 1)
    lead_part, tail_part = low_grad[:lead_total], low_grad[lead_total:]
    lead_back, tail_back = cam_collect(
        "backs",
        [cam_blocks(against(lead_part, lead_in)), cam_blocks(against(tail_part, tail_in))],
    )
    lead_back, lead_first = norm_backward(lead_back, lead_unit, lead_scale, prefix_prenorm)
    tail_back, tail_first = norm_backward(tail_back, tail_unit, tail_scale, action_prenorm)
    lead_input = low(lead_upstream + lead_back)
    tail_input = low(tail_upstream + tail_back)

    owned_lead, owned_tail = prefix_query.shape[0], action_query.shape[0]
    split_rows = lambda grad, rows: low(grad).reshape(depth, 2, members, rows, grad.shape[1])
    attention_parts = [
        split_rows(outer_sum(lead_normed, lead_part), owned_lead),
        split_rows(outer_sum(tail_normed, tail_part), owned_tail),
        split_rows(lead_mixing, owned_lead),
        split_rows(tail_mixing, owned_tail),
    ]
    scratch = []
    for part in attention_parts:
        block = part.shape[2:]
        scratch += [pltpu.VMEM((depth,) + block, jnp.bfloat16)] * 4

    def fold_routines(net, at, ins, outs, held):
        names = ("own", "core", "up", "down")
        buffers = [dict(zip(names, held[4 * i : 4 * i + 4])) for i in range(4)]
        return [fold(net, at, ins, outs, buffers)]

    folded = exchange(
        "fold",
        next(idents),
        sizes,
        ("z", "y", "cam"),
        [(part, False) for part in attention_parts],
        [(shape_of(part.shape[2:]), False) for part in attention_parts],
        scratch,
        fold_routines,
    )

    def split(projection, mixer):
        projection = jnp.swapaxes(projection, 0, 1).astype(jnp.float32)
        rows = projection.shape[0]
        query = projection[:, :, :width].reshape(rows, -1)
        pairs = projection[:, :, width:].reshape(rows, -1)
        mixer = jnp.swapaxes(mixer, 0, 1).reshape(rows, -1).astype(jnp.float32)
        return (query, pairs[:, :head_size], pairs[:, head_size:], mixer)

    lead_grads = split(folded[0], folded[2])
    tail_grads = split(folded[1], folded[3])

    gains = [lead_first, lead_middle, tail_first, tail_middle]
    total = lax.psum(jnp.concatenate(gains), ("rows", "cam"))
    place = lax.axis_index("rows") * members + member_place
    gain_grads = []
    offset = 0
    for gain in gains:
        share = gain.shape[0] // (row_count * members)
        gain_grads.append(lax.dynamic_slice_in_dim(total, offset + place * share, share))
        offset += gain.shape[0]

    return (
        (lead_result, tail_result, lead_input, tail_input)
        + lead_grads
        + tail_grads
        + tuple(gain_grads)
        + tuple(ff_grads)
    )


def solution(mesh):
    in_specs = (
        P(("rows", "cam"), None),
        P(("rows", "cam"), None),
        P(("rows", "cam"), None),
        P(("rows", "cam"), None),
        P("rows", None),
        P("rows", None),
        P(("rows", "cam"), None),
        P(("rows", "cam"), None),
        P(("rows", "cam"), None),
        P(("rows", "cam"), None),
        P(("rows", "cam"), None),
        P(("rows", "cam"), None),
        P(("rows", "cam"), None),
        P(("rows", "cam"), None),
        P(),
        P(),
        P(),
        P(),
        P("rows", "cam"),
        P("rows", "cam"),
        P("rows", "cam"),
        P("rows", "cam"),
        P("rows", "cam"),
        P("rows", "cam"),
    )
    out_specs = (
        P(("rows", "cam"), None),
        P(("rows", "cam"), None),
        P(("rows", "cam"), None),
        P(("rows", "cam"), None),
        P(("rows", "cam"), None),
        P(("rows", "cam"), None),
        P(("rows", "cam"), None),
        P(("rows", "cam"), None),
        P(("rows", "cam"), None),
        P(("rows", "cam"), None),
        P(("rows", "cam"), None),
        P(("rows", "cam"), None),
        P(("rows", "cam")),
        P(("rows", "cam")),
        P(("rows", "cam")),
        P(("rows", "cam")),
        P("rows", "cam"),
        P("rows", "cam"),
        P("rows", "cam"),
        P("rows", "cam"),
        P("rows", "cam"),
        P("rows", "cam"),
    )
    return jax.shard_map(body, mesh=mesh, in_specs=in_specs, out_specs=out_specs, check_vma=False)
```

time: 3850 us -> 1480 us (0.38)
  waiting for transfers between devices: 3370 us -> 0 us
  Pallas kernels: 0 us -> 1180 us
  blocking collectives: 149 us -> 45.9 us
  matrix products: 247 us -> 165 us
    reduce_scatter x19 -> x0, waiting for transfers between devices: 2200 us -> none  [the longest x1 279 us: body(): lax.psum_scatter(lead_ffgrads[2].astype(jnp.bfloat16), 'rows', scatter_di...]
    pallas_call x0 -> x11, Pallas kernels: none -> 1180 us  [exchange(): pl.pallas_call(kernel, name=label, out_shape=[shape for shape, _ in outpu...]
    all_gather x16 -> x0, waiting for transfers between devices: 1160 us -> none  [the longest x1 229 us: body(): lax.all_gather(prefix_gate, 'rows', axis=0, tiled=True)]
    all_gather x7 -> x0, blocking collectives: 106 us -> none  [the longest x1 40.8 us: body(): lax.all_gather(action_key, ('rows', 'cam'), axis=0, tiled=True)]
    psum x0 -> x1, blocking collectives: none -> 45.9 us  [body(): total = lax.psum(jnp.concatenate(gains), ('rows', 'cam'))]
    unnamed x1 -> x0, blocking collectives: 42.9 us -> none
    dot_general x14 -> x10, matrix products: 82.4 us -> 48.3 us  [outer_sum(): lax.dot_general(operand, matrix, (((0,), (0,)), ((), ())), preferred_elem...]
    dot_general x14 -> x10, matrix products: 79.6 us -> 58.1 us  [multiply(): return jnp.dot(operand, matrix, preferred_element_type=jnp.float32)]
  transfers between devices with their start and end apart: 36 -> 0, of which waited for: 32 -> 0; matrix products, arithmetic and copies ran while one was open for 7% -> 0% of each run, Pallas kernels for 0% -> 0%
where the time goes in v1:
time: 1480 us; the launch traced here: 1460 us
  Pallas kernels  1180 us (80%)
  matrix products  165 us (11%)
  blocking collectives  45.9 us (3%)
  other arithmetic  41.6 us (3%)
  local copies, waits for them, and re-layouts  24.2 us (2%)
    pallas_call x11, Pallas kernels, exchange(): pl.pallas_call(kernel, name=label, out_shape=[shape for shape, _ in outpu...  1180 us
    dot_general x10, matrix products, multiply(): return jnp.dot(operand, matrix, preferred_element_type=jnp.float32)  58.1 us
    dot_general x10, matrix products, against(): lax.dot_general(operand, matrix, (((1,), (1,)), ((), ())), preferred_elem...  52.2 us
    dot_general x10, matrix products, outer_sum(): lax.dot_general(operand, matrix, (((0,), (0,)), ((), ())), preferred_elem...  48.3 us
    psum x1, blocking collectives, body(): total = lax.psum(jnp.concatenate(gains), ('rows', 'cam'))  45.9 us

profile of v1, /device:TPU:0, one launch (start us, length us, event | category | flops | bytes accessed | tf_op | source)
XLA Modules:
  0.0 1458.9 jit_solution(9644248119020574237)
XLA Ops:
  17.4 66.5 %first.1 = (bf16[2,2,128,2048]{3,2,1,0:T(8,128)(2,1)}, bf16[2,2,16,1024]{3,2,1,0:T(8,128)(2,1)}, bf16[4,2,4,64,640]{4,3,2,1,0:T(8,128)(2,1)}, bf16[4,2,4,32,640]{4,3,2,1,0:T(8,128)(2,1)}) custom-call(bf16[128,2048]{1,0:T(8,128)(2,1)} %fusion.33.refs_0_, bf16[16,1024]{1,0:T(8,128)(2,1)} %fusion.60.refs_1_, bf16[4,64,640]{2,1,0:T(8,128)(2,1)} %maximum_bitcast_fusion.refs_2_, ...), custom_call_target="tpu_custom_call" | custom-call | tf_op jit(solution)/shard_map/first/pallas_call | solution.py:654
  85.7 4.2 convolution_convert_fusion.10
  90.6 13.8 pairs.1
  109.6 274.6 %second.1 = (bf16[4,2,256,1024]{3,2,1,0:T(8,128)(2,1)}, bf16[4,2,256,1024]{3,2,1,0:T(8,128)(2,1)}, bf16[4,2,256,1024]{3,2,1,0:T(8,128)(2,1)}, bf16[4,2,128,256]{...) custom-call(bf16[256,4096]{1,0:T(8,128)(2,1)} %refs_0_.2, ...), custom_call_target="tpu_custom_call" | custom-call | tf_op jit(solution)/shard_map/second/pallas_call | solution.py:654
  384.2 2.3 convolution_convert_fusion.15
  386.6 4.2 convolution_convert_fusion.6
  390.8 24.1 %mixing.1 = (f32[128,2048]{1,0:T(8,128)}, f32[16,1024]{1,0:T(8,128)}) custom-call(bf16[2,2,128,2048]{3,2,1,0:T(8,128)(2,1)} %bitcast.323, bf16[2,2,16,1024]{3,2,1,0:T(8,128)(2,1)} %bitcast.358), custom_call_target="tpu_custom_call" | custom-call | tf_op jit(solution)/shard_map/mixing/pallas_call | solution.py:654
  419.4 130.1 %gather0.1 = (bf16[4,2,2,128,2048]{4,3,2,1,0:T(8,128)(2,1)}, bf16[4,2,2,16,1024]{4,3,2,1,0:T(8,128)(2,1)}, bf16[4,2,2,128,2048]{4,3,2,1,0:T(8,128)(2,1)}, bf16[4,2,2,16,1024]{4,3,2,1,0:T(8,128)(2,1)}) custom-call(bf16[128,2048]{1,0:T(8,128)(2,1)} %refs_0_.3, bf16[16,1024]{1,0:T(8,128)(2,1)} %refs_1_.3, bf16[128,2048]{1,0:T(8,128)(2,1)} %multiply_convert_fusion.2.refs_2_, ...), custom_call_target="tpu_custom_call" | custom-call | tf_op jit(solution)/shard_map/gather0/pallas_call | solution.py:654
  560.1 11.0 fusion.81
  571.1 11.0 fusion.82
  582.1 22.0 %multiply_convert_fusion = (bf16[2048,1024]{1,0:T(8,128)(2,1)}, bf16[2048,1024]{1,0:T(8,128)(2,1)}, bf16[2048,1024]{1,0:T(8,128)(2,1)}) fusion(f32[2048,1024]{1,0:T(8,128)} %fusion.82, f32[2048,1024]{1,0:T(8,128)} %fusion.81, bf16[2048,2048]{1,0:T(8,128)(2,1)} %bitcast.375, bf16[2048,1024]{1,0:T(8,128)(2,1)S(1)} %bitcast.385), kind=kOutput, calls=%fused_computation.10 | convolution fusion | flops 8644460544 | bytes 41943040 | tf_op jit(solution)/shard_map/dot_general | solution.py:674
  604.1 14.3 convolution_convert_fusion.1
  618.4 10.9 convolution_convert_fusion
  629.4 10.5 convolution_convert_fusion.3
  639.9 11.0 convolution_convert_fusion.2
  651.0 185.4 %returns.1 = (bf16[256,4096]{1,0:T(8,128)(2,1)}, bf16[256,4096]{1,0:T(8,128)(2,1)}, bf16[256,4096]{1,0:T(8,128)(2,1)}, bf16[4,128,256]{2,1,0:T(8,128)(2,1)}, bf1...) custom-call(bf16[4,2,256,1024]{3,2,1,0:T(8,128)(2,1)} %bitcast.305, bf16[4,2,256,1024]{3,2,1,0:T(8,128)(2,1)} %bitcast.306, ...), custom_call_target="tpu_custom_call" | custom-call | tf_op jit(solution)/shard_map/returns/pallas_call | solution.py:654
  844.0 2.5 convert_element_type.264
  846.5 2.6 convert_element_type.265
  849.2 2.6 convert_element_type.266
  853.7 11.7 fusion.83
  865.4 14.2 add_convert_fusion
  879.7 234.1 %collect0.1 = (f32[128,2048]{1,0:T(8,128)}, f32[16,1024]{1,0:T(8,128)}, f32[128,2048]{1,0:T(8,128)}, f32[16,1024]{1,0:T(8,128)}) custom-call(bf16[4,2,2,128,2048]{4,3,2,1,0:T(8,128)(2,1)} %bitcast.294, bf16[4,2,2,16,1024]{4,3,2,1,0:T(8,128)(2,1)} %bitcast.320, bf16[4,2,2,128,2048]{4,3,2,1,0:T(8,128)(2,1)} %bitcast.293, bf16[4,2,2,16,1024]{4,3,2,1,0:T(8,128)(2,1)} %bitcast.321), custom_call_target="tpu_custom_call" | custom-call | tf_op jit(solution)/shard_map/collect0/pallas_call | solution.py:654
  1119.3 22.8 %sent.1 = (bf16[2,2,128,2048]{3,2,1,0:T(8,128)(2,1)}, bf16[2,2,16,1024]{3,2,1,0:T(8,128)(2,1)}) custom-call(bf16[128,2048]{1,0:T(8,128)(2,1)} %fusion.73.refs_0_, bf16[16,1024]{1,0:T(8,128)(2,1)} %fusion.68.refs_1_), custom_call_target="tpu_custom_call" | custom-call | tf_op jit(solution)/shard_map/sent/pallas_call | solution.py:654
  1142.1 3.6 fusion.87
  1145.8 2.7 convolution_convert_fusion.5
  1155.5 14.4 pair_grads.1
  1170.9 5.0 convolution_convert_fusion.7
  1177.2 3.3 convolution_convert_fusion.4
  1180.5 24.1 %backs.1 = (f32[128,2048]{1,0:T(8,128)}, f32[16,1024]{1,0:T(8,128)}) custom-call(bf16[2,2,128,2048]{3,2,1,0:T(8,128)(2,1)} %bitcast.322, bf16[2,2,16,1024]{3,2,1,0:T(8,128)(2,1)} %bitcast.357), custom_call_target="tpu_custom_call" | custom-call | tf_op jit(solution)/shard_map/backs/pallas_call | solution.py:654
  1208.9 45.9 %psum.7 = f32[6144]{0:T(1024)S(1)} all-reduce(f32[6144]{0:T(1024)S(1)} %pad_maximum_fusion.5), channel_id=1, replica_groups=mesh['rows'=8,'cam'=4] {'rows','cam'}, use_global_device_ids=true, to_apply=%region_15.16 | all-reduce | flops 6144 | bytes 49152 | tf_op jit(solution)/shard_map/psum | solution.py:1122
  1255.9 3.0 fusion.38
  1262.0 189.9 %fold.1 = (bf16[4,64,640]{2,1,0:T(8,128)(2,1)}, bf16[4,32,640]{2,1,0:T(8,128)(2,1)}, bf16[4,64,512]{2,1,0:T(8,128)(2,1)}, bf16[4,32,512]{2,1,0:T(8,128)(2,1)}) custom-call(bf16[4,2,4,64,640]{4,3,2,1,0:T(8,128)(2,1)} %bitcast.310, bf16[4,2,4,32,640]{4,3,2,1,0:T(8,128)(2,1)} %bitcast.295, bf16[4,2,4,64,512]{4,3,2,1,0:T(8,128)(2,1)} %bitcast.319, ...), custom_call_target="tpu_custom_call" | custom-call | tf_op jit(solution)/shard_map/fold/pallas_call | solution.py:654
  (268 shorter events, 78.1 us)
Async XLA Ops:
  0.7 14.3 copy-start.41
  2.0 14.4 copy-start.60
  16.4 90.7 %copy-start.19 = (pred[576,576]{0,1:T(8,128)(4,1)}, pred[576,576]{0,1:T(8,128)(4,1)S(1)}, u32[]{:S(2)}) copy-start(pred[576,576]{0,1:T(8,128)(4,1)S(1)} %compare_and_fusion) | copy-start | bytes 995332
  90.5 15.8 %copy-start.29 = (bf16[576,512]{1,0:T(8,128)(2,1)}, bf16[576,512]{1,0:T(8,128)(2,1)S(1)}, u32[]{:S(2)}) copy-start(bf16[576,512]{1,0:T(8,128)(2,1)S(1)} %pad_maximum_fusion.1) | copy-start | bytes 1769476
  109.5 277.0 %copy-start.34 = (bf16[512,2,256]{0,2,1:T(8,128)(2,1)}, bf16[512,2,256]{0,2,1:T(8,128)(2,1)S(1)}, u32[]{:S(2)}) copy-start(bf16[512,2,256]{0,2,1:T(8,128)(2,1)S(1)} %copy.60) | copy-start | bytes 1572868
  109.6 274.7 %copy-start.24 = (bf16[2,8,8,256]{3,2,0,1:T(8,128)(2,1)}, bf16[2,8,8,256]{3,2,0,1:T(8,128)(2,1)S(1)}, u32[]{:S(2)}) copy-start(bf16[2,8,8,256]{3,2,0,1:T(8,128)(2,1)S(1)} %copy.103) | copy-start | bytes 196612
  390.8 25.7 %copy-start.22 = (bf16[16,1024]{1,0:T(8,128)(2,1)S(1)}, bf16[16,1024]{1,0:T(8,128)(2,1)}, u32[]{:S(2)}) copy-start(bf16[16,1024]{1,0:T(8,128)(2,1)} %param.25) | copy-start | bytes 98308
  390.8 26.9 %copy-start.48 = (f32[1024]{0:T(1024)S(1)}, f32[1024]{0:T(1024)}, u32[]{:S(2)}) copy-start(f32[1024]{0:T(1024)} %param.41) | copy-start | bytes 12292
  390.8 27.7 %copy-start.44 = (f32[2048]{0:T(1024)S(1)}, f32[2048]{0:T(1024)}, u32[]{:S(2)}) copy-start(f32[2048]{0:T(1024)} %param.39) | copy-start | bytes 24580
  414.9 134.7 %copy-start.15 = (bf16[4,2,128,256]{3,2,1,0:T(8,128)(2,1)S(1)}, bf16[4,2,128,256]{3,2,1,0:T(8,128)(2,1)}, u32[]{:S(2)}) copy-start(bf16[4,2,128,256]{3,2,1,0:T(8,128)(2,1)} %get-tuple-element.72) | copy-start | bytes 1572868
  414.9 136.2 %copy-start.14 = (bf16[4,2,128,256]{3,2,1,0:T(8,128)(2,1)S(1)}, bf16[4,2,128,256]{3,2,1,0:T(8,128)(2,1)}, u32[]{:S(2)}) copy-start(bf16[4,2,128,256]{3,2,1,0:T(8,128)(2,1)} %get-tuple-element.75) | copy-start | bytes 1572868
  416.4 136.1 %copy-start.31 = (bf16[4,2,128,256]{3,2,1,0:T(8,128)(2,1)S(1)}, bf16[4,2,128,256]{3,2,1,0:T(8,128)(2,1)}, u32[]{:S(2)}) copy-start(bf16[4,2,128,256]{3,2,1,0:T(8,128)(2,1)} %get-tuple-element.74) | copy-start | bytes 1572868
  417.7 136.2 %copy-start.54 = (f32[16]{0:T(128)}, f32[16]{0:T(128)S(1)}, u32[]{:S(2)}) copy-start(f32[16]{0:T(128)S(1)} %add_rsqrt_fusion) | copy-start | bytes 196
  604.1 14.3 copy-start.70
  604.1 14.3 copy-start.77
  604.1 25.3 %slice-start.2 = ((s8[8388608]{0:T(1024)(128)(4,1)}), s8[4194304]{0:T(1024)(128)(4,1)S(1)}, s32[]{:S(2)}) async-start(s8[8388608]{0:T(1024)(128)(4,1)} %bitcast.379), calls=%async_computation.2 | async-start | bytes 8388608
  879.6 234.2 %copy-start.18 = (f32[16,1024]{1,0:T(8,128)S(1)}, f32[16,1024]{1,0:T(8,128)}, u32[]{:S(2)}) copy-start(f32[16,1024]{1,0:T(8,128)} %copy-done.17) | copy-start | bytes 196612
  879.6 234.2 %copy-start.49 = (f32[1024]{0:T(1024)S(1)}, f32[1024]{0:T(1024)}, u32[]{:S(2)}) copy-start(f32[1024]{0:T(1024)} %param.41) | copy-start | bytes 12292
  879.6 234.2 %copy-start.55 = (f32[16]{0:T(128)S(1)}, f32[16]{0:T(128)}, u32[]{:S(2)}) copy-start(f32[16]{0:T(128)} %copy-done.54) | copy-start | bytes 196
  879.6 235.4 %copy-start.1 = (f32[128,2048]{1,0:T(8,128)S(1)}, f32[128,2048]{1,0:T(8,128)}, u32[]{:S(2)}) copy-start(f32[128,2048]{1,0:T(8,128)} %copy-done) | copy-start | bytes 3145732
  879.6 235.4 %copy-start.45 = (f32[2048]{0:T(1024)S(1)}, f32[2048]{0:T(1024)}, u32[]{:S(2)}) copy-start(f32[2048]{0:T(1024)} %param.39) | copy-start | bytes 24580
  879.7 235.4 %copy-start.57 = (f32[128]{0:T(128)S(1)}, f32[128]{0:T(128)}, u32[]{:S(2)}) copy-start(f32[128]{0:T(128)} %copy-done.56) | copy-start | bytes 1540
  879.7 236.9 %copy-start.36 = (bf16[16,1024]{1,0:T(8,128)(2,1)S(1)}, bf16[16,1024]{1,0:T(8,128)(2,1)}, u32[]{:S(2)}) copy-start(bf16[16,1024]{1,0:T(8,128)(2,1)} %refs_1_.3) | copy-start | bytes 98308
  879.7 238.5 %copy-start.6 = (bf16[128,2048]{1,0:T(8,128)(2,1)S(1)}, bf16[128,2048]{1,0:T(8,128)(2,1)}, u32[]{:S(2)}) copy-start(bf16[128,2048]{1,0:T(8,128)(2,1)} %refs_0_.3) | copy-start | bytes 1572868
  1177.1 27.4 %copy-start.23 = (bf16[16,1024]{1,0:T(8,128)(2,1)S(1)}, bf16[16,1024]{1,0:T(8,128)(2,1)}, u32[]{:S(2)}) copy-start(bf16[16,1024]{1,0:T(8,128)(2,1)} %param.25) | copy-start | bytes 98308
  1177.2 27.5 %copy-start.53 = (f32[1024]{0:T(1024)S(1)}, f32[1024]{0:T(1024)}, u32[]{:S(2)}) copy-start(f32[1024]{0:T(1024)} %param.40) | copy-start | bytes 12292
  1177.2 27.5 %copy-start.63 = (f32[16]{0:T(128)S(1)}, f32[16]{0:T(128)}, u32[]{:S(2)}) copy-start(f32[16]{0:T(128)} %copy-done.62) | copy-start | bytes 196
  1177.2 28.5 %copy-start.26 = (f32[16,1024]{1,0:T(8,128)S(1)}, f32[16,1024]{1,0:T(8,128)}, u32[]{:S(2)}) copy-start(f32[16,1024]{1,0:T(8,128)} %get-tuple-element.79) | copy-start | bytes 196612
  1177.2 28.5 %copy-start.50 = (f32[16,1024]{1,0:T(8,128)S(1)}, f32[16,1024]{1,0:T(8,128)}, u32[]{:S(2)}) copy-start(f32[16,1024]{1,0:T(8,128)} %get-tuple-element.77) | copy-start | bytes 196612
  1177.2 30.1 %copy-start.47 = (f32[2048]{0:T(1024)S(1)}, f32[2048]{0:T(1024)}, u32[]{:S(2)}) copy-start(f32[2048]{0:T(1024)} %param.38) | copy-start | bytes 24580
  1177.2 30.1 %copy-start.61 = (f32[128]{0:T(128)S(1)}, f32[128]{0:T(128)}, u32[]{:S(2)}) copy-start(f32[128]{0:T(128)} %copy-done.60) | copy-start | bytes 1540
  1180.5 26.7 %copy-start.3 = (bf16[128,2048]{1,0:T(8,128)(2,1)S(1)}, bf16[128,2048]{1,0:T(8,128)(2,1)}, u32[]{:S(2)}) copy-start(bf16[128,2048]{1,0:T(8,128)(2,1)} %param.24) | copy-start | bytes 1572868
  (50 other events, 279.6 us)

commit v2 on v1

--- a/solution.py
+++ b/solution.py
@@ -103,6 +103,19 @@
 def greet(at, kinds):
     peers = []
     count = 0
+    if "all" in kinds:
+        for s, flip, step, turn in everyone(at):
+            peers.append(
+                (
+                    None,
+                    at.device(
+                        at.later_z(s),
+                        1 - at.y if flip else at.y,
+                        at.later_x(step),
+                        1 - at.k if turn else at.k,
+                    ),
+                )
+            )
     if "z" in kinds and "deal" not in kinds:
         count = count + (at.z > 0).astype(jnp.int32) + (at.z < at.depth - 1).astype(jnp.int32)
         peers.append((at.z > 0, at.device(z=at.z - 1)))
@@ -339,255 +352,124 @@
         transfer.got()
 
 
-def deal(net, at, sources, outs, stages):
-    moves, across, loads, stores = {}, {}, [], []
-    for i, (source, out, stage) in enumerate(zip(sources, outs, stages)):
-        slot = lambda out=out: out.at[at.z, at.y]
-        held = lambda stage=stage: stage
-        loads.append(Local(net, lambda source=source: source(at.z), held))
-        stores.append(Local(net, held, slot))
-        across[i, 0] = Transfer(net, held, slot, at.device(y=1 - at.y))
-        for step in range(1, at.depth):
-            z = at.later_z(step)
-            moves[i, step] = Transfer(
-                net, lambda source=source, z=z: source(z), slot, at.device(z=z)
-            )
-            origin = at.later_z(at.depth - step)
-            arrived = lambda out=out, origin=origin: out.at[origin, at.y]
-            across[i, step] = Transfer(net, arrived, arrived, at.device(y=1 - at.y))
-    for load in loads:
-        load.start()
-    count = len(loads)
-    for i in range(count):
-        for step in range(1, at.depth):
-            moves[i, step].start()
-    yield
-    for i in range(count):
-        loads[i].wait()
-        stores[i].start()
-        across[i, 0].start()
-    for i in range(count):
-        for step in range(1, at.depth):
-            yield
-            moves[i, step].got()
-            across[i, step].start()
-    yield
-    for transfer in across.values():
-        transfer.got()
-    for store in stores:
-        store.wait()
-
-
-def chain_sum(net, at, own, up, down):
-    rise, fall = {}, {}
-    for t in range(at.depth):
-        rise[t] = Transfer(
-            net,
-            lambda t=t: own(t),
-            lambda t=t: up(t),
-            at.device(z=at.z + 1),
-            sends=at.z < t,
-            gets=(at.z > 0) & (at.z <= t),
-        )
-        fall[t] = Transfer(
-            net,
-            lambda t=t: own(t),
-            lambda t=t: down(t),
-            at.device(z=at.z - 1),
-            sends=at.z > t,
-            gets=(at.z < at.depth - 1) & (at.z >= t),
-        )
-    return rise, fall
-
-
-def edges_first(depth):
-    order = []
-    for i in range((depth + 1) // 2):
-        order.append(depth - 1 - i)
-        if i != depth - 1 - i:
-            order.append(i)
-    return order
+def add_all(target, sources):
+    count = target.shape[0]
+    step = 16 if count % 16 == 0 else 8
+
+    def one(index, carry):
+        rows = pl.ds(pl.multiple_of(index * step, step), step)
+        total = sources[0][rows, :].astype(jnp.float32)
+        for source in sources[1:]:
+            total = total + source[rows, :].astype(jnp.float32)
+        target[rows, :] = total.astype(target.dtype)
+        return carry
+
+    lax.fori_loop(0, count // step, one, 0)
 
 
 def collect(net, at, parts, outs, buffers, chained):
     depth = at.depth if chained else 1
-    order = edges_first(depth)
     part_of = (
         (lambda part, t, x, k: part.at[t, x, k]) if chained else (lambda part, t, x, k: part.at[x, k])
     )
-    loads, partner, across, chains = {}, {}, {}, []
+    loads, partner, across, beyond = {}, {}, {}, {}
     for i, (part, buffer) in enumerate(zip(parts, buffers)):
         own, core, wide = buffer["own"], buffer["core"], buffer["wide"]
-        for t in order:
+        for s in range(depth):
+            t = at.later_z(s) if chained else 0
             for step in range(at.breadth):
                 x = at.later_x(step)
-                loads[i, t, step] = Local(
+                loads[i, s, step] = Local(
                     net,
                     lambda part=part, t=t, x=x: part_of(part, t, x, at.k),
-                    lambda own=own, t=t, x=x: own.at[t, x],
+                    lambda own=own, s=s, step=step: own.at[s, step],
                 )
-                partner[i, t, step] = Transfer(
+                partner[i, s, step] = Transfer(
                     net,
                     lambda part=part, t=t, x=x: part_of(part, t, x, 1 - at.k),
-                    lambda core=core, t=t, x=x: core.at[t, x],
+                    lambda core=core, s=s, step=step: core.at[s, step],
                     at.device(k=1 - at.k),
                 )
                 if step > 0:
-                    across[i, t, step] = Transfer(
+                    across[i, s, step] = Transfer(
                         net,
-                        lambda own=own, t=t, x=x: own.at[t, x],
-                        lambda wide=wide, t=t, step=step: wide.at[step - 1, t],
+                        lambda own=own, s=s, step=step: own.at[s, step],
+                        lambda wide=wide, s=s, step=step: wide.at[step - 1, s],
                         at.device(x=x),
                     )
-        if chained:
-            chains.append(
-                chain_sum(
+            if s > 0:
+                beyond[i, s] = Transfer(
                     net,
-                    at,
-                    lambda t, own=own: own.at[t, at.x],
-                    lambda t, buffer=buffer: buffer["up"].at[t],
-                    lambda t, buffer=buffer: buffer["down"].at[t],
+                    lambda own=own, s=s: own.at[s, 0],
+                    lambda buffer=buffer, s=s: buffer["far"].at[s - 1],
+                    at.device(z=t),
                 )
-            )
     steps = list(range(1, at.breadth)) + [0]
+    spans = list(range(1, depth)) + [0]
     count = len(parts)
     for i in range(count):
-        for t in order:
+        for s in spans:
             for step in steps:
-                partner[i, t, step].start()
-                loads[i, t, step].start()
+                partner[i, s, step].start()
+                loads[i, s, step].start()
     for i in range(count):
         own, core = buffers[i]["own"], buffers[i]["core"]
-        for t in order:
+        for s in spans:
             yield
             for step in steps:
-                x = at.later_x(step)
-                loads[i, t, step].wait()
-                partner[i, t, step].got()
-                add_rows(own.at[t, x], own.at[t, x], core.at[t, x])
-            for step in steps[:-1]:
-                across[i, t, step].start()
+                loads[i, s, step].wait()
+                partner[i, s, step].got()
+                if step > 0:
+                    add_rows(own.at[s, step], own.at[s, step], core.at[s, step])
+                    across[i, s, step].start()
     for i in range(count):
-        buffer = buffers[i]
-        own, wide = buffer["own"], buffer["wide"]
-        for t in order:
+        own, core, wide = buffers[i]["own"], buffers[i]["core"], buffers[i]["wide"]
+        for s in spans:
             yield
             for step in steps[:-1]:
-                across[i, t, step].got()
-                last = not chained and step == steps[-2]
-                target = outs[i] if last else own.at[t, at.x]
-                add_rows(target, own.at[t, at.x], wide.at[step - 1, t])
-            if chained:
-                rise, fall = chains[i]
-                yield
-
-                def finish(i=i, t=t, buffer=buffer, rise=rise, fall=fall):
-                    widen_rows(outs[i], buffer["own"].at[t, at.x])
-                    for moves, name in ((rise, "up"), (fall, "down")):
-
-                        def more(moves=moves, name=name):
-                            moves[t].describe().wait_recv()
-                            add_rows(outs[i], outs[i], buffer[name].at[t])
-
-                        pl.when(moves[t].gets)(more)
-
-                def passing(t=t, buffer=buffer, rise=rise, fall=fall):
-                    for moves, name in ((rise, "up"), (fall, "down")):
-
-                        def more(moves=moves, name=name):
-                            moves[t].describe().wait_recv()
-                            held = buffer["own"].at[t, at.x]
-                            add_rows(held, held, buffer[name].at[t])
-
-                        pl.when(moves[t].gets)(more)
-
-                pl.when(at.z == t)(finish)
-                pl.when(at.z != t)(passing)
-                rise[t].start()
-                fall[t].start()
-
-
-def give_back(net, at, parts, slots, buffers):
-    loads, across, moves, stores = {}, {}, {}, []
-    for i, (part, buffer) in enumerate(zip(parts, buffers)):
-        own, core = buffer["own"], buffer["core"]
-        for step in range(at.depth):
-            z = at.later_z(step)
-            loads[i, step] = Local(
-                net,
-                lambda part=part, z=z: part.at[z, at.y],
-                lambda own=own, z=z: own.at[z],
-            )
-            across[i, step] = Transfer(
-                net,
-                lambda part=part, z=z: part.at[z, 1 - at.y],
-                lambda core=core, z=z: core.at[z],
-                at.device(y=1 - at.y),
-            )
-            if step > 0:
-                moves[i, step] = Transfer(
-                    net,
-                    lambda own=own, z=z: own.at[z],
-                    lambda i=i: slots[i](at.z),
-                    at.device(z=z),
-                )
+                across[i, s, step].got()
+            terms = [own.at[s, 0], core.at[s, 0]] + [wide.at[step - 1, s] for step in steps[:-1]]
+            if s > 0:
+                add_all(own.at[s, 0], terms)
+                beyond[i, s].start()
             else:
-                stores.append(
-                    Local(net, lambda own=own: own.at[at.z], lambda i=i: slots[i](at.z))
-                )
-    count = len(parts)
-    steps = list(range(1, at.depth)) + [0]
+                add_all(outs[i], terms)
     for i in range(count):
-        for step in steps:
-            loads[i, step].start()
-            across[i, step].start()
-    for i in range(count):
-        own, core = buffers[i]["own"], buffers[i]["core"]
-        for step in steps:
+        if depth > 1:
             yield
-            z = at.later_z(step)
-            loads[i, step].wait()
-            across[i, step].got()
-            add_rows(own.at[z], own.at[z], core.at[z])
-            if step > 0:
-                moves[i, step].start()
-            else:
-                stores[i].start()
-    for transfer in moves.values():
-        yield
-        transfer.got()
-    for store in stores:
-        store.wait()
+            for s in spans[:-1]:
+                beyond[i, s].got()
+            add_all(outs[i], [outs[i]] + [buffers[i]["far"].at[s - 1] for s in spans[:-1]])
 
 
 def fold(net, at, parts, outs, buffers):
     mine = at.x * 2 + at.k
     members = 2 * at.breadth
-    order = edges_first(at.depth)
-    loads, across, chains, swap, stores = {}, {}, [], {}, []
+    loads, across, beyond, swap, stores = {}, {}, {}, {}, []
     for i, (part, buffer) in enumerate(zip(parts, buffers)):
-        own, core = buffer["own"], buffer["core"]
-        for t in order:
-            loads[i, t] = Local(
-                net, lambda part=part, t=t: part.at[t, at.y], lambda own=own, t=t: own.at[t]
+        own, core, far = buffer["own"], buffer["core"], buffer["far"]
+        for s in range(at.depth):
+            t = at.later_z(s)
+            loads[i, s] = Local(
+                net,
+                lambda part=part, t=t: part.at[t, at.y],
+                lambda own=own, s=s: own.at[s],
             )
-            across[i, t] = Transfer(
+            across[i, s] = Transfer(
                 net,
                 lambda part=part, t=t: part.at[t, 1 - at.y],
-                lambda core=core, t=t: core.at[t],
+                lambda core=core, s=s: core.at[s],
                 at.device(y=1 - at.y),
             )
-        chains.append(
-            chain_sum(
-                net,
-                at,
-                lambda t, own=own: own.at[t],
-                lambda t, buffer=buffer: buffer["up"].at[t],
-                lambda t, buffer=buffer: buffer["down"].at[t],
-            )
-        )
+            if s > 0:
+                beyond[i, s] = Transfer(
+                    net,
+                    lambda own=own, s=s: own.at[s],
+                    lambda far=far, s=s: far.at[s - 1],
+                    at.device(z=t),
+                )
         slot = lambda i=i: outs[i].at[mine]
-        stores.append(Local(net, lambda own=own: own.at[at.z, mine], slot))
+        stores.append(Local(net, lambda own=own: own.at[0, mine], slot))
         for step in range(at.breadth):
             for flip in (0, 1):
                 if step == 0 and flip == 0:
@@ -596,37 +478,37 @@
                 k = 1 - at.k if flip else at.k
                 swap[i, step, flip] = Transfer(
                     net,
-                    lambda own=own, x=x, k=k: own.at[at.z, x * 2 + k],
+                    lambda own=own, x=x, k=k: own.at[0, x * 2 + k],
                     slot,
                     at.device(x=x, k=k),
                 )
     count = len(parts)
+    spans = list(range(1, at.depth)) + [0]
     for i in range(count):
-        for t in order:
-            across[i, t].start()
-            loads[i, t].start()
+        for s in spans:
+            across[i, s].start()
+            loads[i, s].start()
     for i in range(count):
-        buffer = buffers[i]
-        own, core = buffer["own"], buffer["core"]
-        rise, fall = chains[i]
-        for t in order:
+        own, core = buffers[i]["own"], buffers[i]["core"]
+        for s in spans:
             yield
-            loads[i, t].wait()
-            across[i, t].got()
-            for member in range(members):
-                add_rows(own.at[t, member], own.at[t, member], core.at[t, member])
-            yield
-            for moves, name in ((rise, "up"), (fall, "down")):
-
-                def more(moves=moves, name=name, t=t, own=own, buffer=buffer):
-                    moves[t].describe().wait_recv()
-                    for member in range(members):
-                        held = own.at[t, member]
-                        add_rows(held, held, buffer[name].at[t, member])
-
-                pl.when(moves[t].gets)(more)
-            rise[t].start()
-            fall[t].start()
+            loads[i, s].wait()
+            across[i, s].got()
+            if s > 0:
+                for member in range(members):
+                    add_rows(own.at[s, member], own.at[s, member], core.at[s, member])
+                beyond[i, s].start()
+    for i in range(count):
+        yield
+        own, core, far = buffers[i]["own"], buffers[i]["core"], buffers[i]["far"]
+        for s in spans[:-1]:
+            beyond[i, s].got()
+        for member in range(members):
+            add_all(
+                own.at[0, member],
+                [own.at[0, member], core.at[0, member]]
+                + [far.at[s - 1, member] for s in spans[:-1]],
+            )
         stores[i].start()
         for (j, step, flip), transfer in swap.items():
             if j == i:
@@ -638,7 +520,46 @@
         store.wait()
 
 
-def exchange(label, ident, sizes, kinds, inputs, outputs, scratch, routines):
+def everyone(at):
+    return [
+        (s, flip, step, turn)
+        for s in range(at.depth)
+        for flip in (0, 1)
+        for step in range(at.breadth)
+        for turn in (0, 1)
+        if (s, flip, step, turn) != (0, 0, 0, 0)
+    ]
+
+
+def hand_out(net, at, table, out):
+    members = 2 * at.breadth
+    number = lambda z, y, x, k: (z * 2 + y) * members + x * 2 + k
+    mine = number(at.z, at.y, at.x, at.k)
+    transfers = []
+    for s, flip, step, turn in everyone(at):
+        z, x = at.later_z(s), at.later_x(step)
+        y = 1 - at.y if flip else at.y
+        k = 1 - at.k if turn else at.k
+        transfers.append(
+            Transfer(
+                net,
+                lambda z=z, y=y, x=x, k=k: table.at[number(z, y, x, k)],
+                lambda: out.at[mine],
+                at.device(z, y, x, k),
+            )
+        )
+    kept = Local(net, lambda: table.at[mine], lambda: out.at[mine])
+    for transfer in transfers:
+        transfer.start()
+    kept.start()
+    for _ in range(64):
+        yield
+    kept.wait()
+    for transfer in transfers:
+        transfer.got()
+
+
+def exchange(label, ident, sizes, kinds, inputs, outputs, scratch, routines, micros=1):
     space = lambda inside: pltpu.VMEM if inside else pl.ANY
 
     def kernel(*refs):
@@ -650,7 +571,7 @@
         run_all(routines(net, at, sources, targets, held))
         net.settle()
 
-    slots = 48 * sizes[0]
+    slots = 40 * sizes[0]
     return pl.pallas_call(
         kernel,
         name=label,
@@ -660,10 +581,118 @@
         scratch_shapes=list(scratch)
         + [pltpu.SemaphoreType.DMA((slots,))] * 2
         + [pltpu.SemaphoreType.DMA((slots,))],
+        cost_estimate=pl.CostEstimate(
+            flops=0, bytes_accessed=micros * 3000000, transcendentals=0
+        ),
         compiler_params=pltpu.CompilerParams(
-            collective_id=ident, has_side_effects=True, vmem_limit_bytes=60 << 20
+            collective_id=ident,
+            has_side_effects=True,
+            vmem_limit_bytes=(60 if sizes[0] <= 4 else 63) << 20,
         ),
     )(*[array for array, _ in inputs])
+
+
+def permute(array, depth, step, flip):
+    pairs = [
+        (z * 2 + y, ((z + step) % depth) * 2 + (1 - y if flip else y))
+        for z in range(depth)
+        for y in range(2)
+    ]
+    return lax.ppermute(array, "rows", pairs)
+
+
+def shuffle(label, sizes, arrays, stages, outs, moves, most):
+    def kernel(*refs):
+        ins, targets = refs[: len(arrays)], refs[len(arrays) : len(arrays) + len(outs)]
+        held = refs[len(arrays) + len(outs) : -2]
+        loaded, stored = refs[-2:]
+        started, copies = [], []
+        plan = moves(Place(*sizes), ins, held, targets)
+        for loads, _ in plan:
+            for source, target in loads:
+                copy = pltpu.make_async_copy(source, target, loaded.at[len(started)])
+                copy.start()
+                started.append(copy)
+        pending = iter(started)
+        for loads, stores in plan:
+            for _ in loads:
+                next(pending).wait()
+            for source, target in stores:
+                copy = pltpu.make_async_copy(source, target, stored.at[len(copies)])
+                copy.start()
+                copies.append(copy)
+        for copy in copies:
+            copy.wait()
+
+    size = sum(stage.size * stage.dtype.itemsize for stage in stages)
+    slots = most * len(stages)
+    return pl.pallas_call(
+        kernel,
+        name=label,
+        out_shape=outs,
+        in_specs=[pl.BlockSpec(memory_space=pl.ANY)] * len(arrays),
+        out_specs=[pl.BlockSpec(memory_space=pl.ANY)] * len(outs),
+        scratch_shapes=[pltpu.VMEM(stage.shape, stage.dtype) for stage in stages]
+        + [pltpu.SemaphoreType.DMA((slots,)), pltpu.SemaphoreType.DMA((slots,))],
+        cost_estimate=pl.CostEstimate(flops=0, bytes_accessed=2 * size, transcendentals=0),
+        compiler_params=pltpu.CompilerParams(vmem_limit_bytes=60 << 20),
+    )(*arrays)
+
+
+def widen(label, sizes, blocks, outs, parts):
+    shares = sorted({(outs[out].shape[-2], share) for _, _, out, share, _ in parts})
+
+    def kernel(*refs):
+        ins, targets = refs[: len(blocks)], refs[len(blocks) : len(blocks) + len(outs)]
+        held = refs[len(blocks) + len(outs) : -len(shares) - 2]
+        wide = refs[-len(shares) - 2 : -2]
+        loaded, stored = refs[-2:]
+        at = Place(*sizes)
+        loads = [
+            pltpu.make_async_copy(source, held[i], loaded.at[i]) for i, source in enumerate(ins)
+        ]
+        for load in loads:
+            load.start()
+        waited, turns, previous = set(), {}, {}
+        for block, distance, out, share, pieces in parts:
+            if block not in waited:
+                loads[block].wait()
+                waited.add(block)
+            kind = shares.index((outs[out].shape[-2], share))
+            turn = turns.get(kind, 0) % 2
+            turns[kind] = turns.get(kind, 0) + 1
+            if (kind, turn) in previous:
+                previous[kind, turn].wait()
+            buffer = wide[kind].at[turn]
+            for row, column, count, place in pieces:
+                widen_rows(
+                    buffer.at[pl.ds(place, count), :],
+                    held[block].at[pl.ds(row, count), pl.ds(column, share)],
+                )
+            z = at.later_z((sizes[0] - distance) % sizes[0])
+            if len(outs[out].shape) == 3:
+                target = targets[out].at[z]
+            else:
+                target = targets[out].at[:, pl.ds(pl.multiple_of(z * share, share), share)]
+            copy = pltpu.make_async_copy(buffer, target, stored.at[2 * kind + turn])
+            copy.start()
+            previous[kind, turn] = copy
+        for copy in previous.values():
+            copy.wait()
+
+    size = sum(block.size for block in blocks)
+    return pl.pallas_call(
+        kernel,
+        name=label,
+        out_shape=outs,
+        in_specs=[pl.BlockSpec(memory_space=pl.ANY)] * len(blocks),
+        out_specs=[pl.BlockSpec(memory_space=pl.ANY)] * len(outs),
+        scratch_shapes=[pltpu.VMEM(block.shape, block.dtype) for block in blocks]
+        + [pltpu.VMEM((2,) + share, jnp.float32) for share in shares]
+        + [pltpu.SemaphoreType.DMA((len(blocks),)), pltpu.SemaphoreType.DMA((2 * len(shares),))],
+        cost_estimate=pl.CostEstimate(flops=0, bytes_accessed=6 * size, transcendentals=0),
+        compiler_params=pltpu.CompilerParams(vmem_limit_bytes=60 << 20),
+    )(*blocks)
 
 
 def shape_of(dims, kind=jnp.bfloat16):
@@ -813,6 +842,82 @@
             routines,
         )
 
+    lead_slice = prefix_gate.shape[1] // depth
+    tail_slice = action_gate.shape[1] // depth
+    lead_block, tail_block = prefix_gate.shape[0], action_gate.shape[0]
+    floor = lax.axis_index("rows") // 2
+    side = lax.rem(lax.axis_index("rows"), 2)
+    ratio = lead_slice // tail_slice
+    strip = tail_block // ratio
+    packed = tail_slice % 128 == 0 and strip % 16 == 0
+    high = 3 * lead_block + (3 * strip if packed else 0)
+    cut_shapes = [shape_of((high, lead_slice))] * depth
+    if not packed:
+        cut_shapes += [shape_of((3, tail_block, tail_slice))] * depth
+
+    def strips(i, start):
+        return [(start + i * strip, j * tail_slice, j * strip) for j in range(ratio)]
+
+    def cut_moves(at, ins, held, outs):
+        lists = []
+        for step in range(depth):
+            z = at.later_z(step)
+            columns = pl.ds(pl.multiple_of(z * lead_slice, lead_slice), lead_slice)
+            loads = [
+                (ins[i].at[:, columns], held[step].at[pl.ds(i * lead_block, lead_block), :])
+                for i in range(3)
+            ]
+            if packed:
+                narrow = pl.ds(pl.multiple_of(z * tail_slice, tail_slice), tail_slice)
+                loads += [
+                    (
+                        ins[3 + i].at[pl.ds(place, strip), narrow],
+                        held[step].at[pl.ds(row, strip), pl.ds(column, tail_slice)],
+                    )
+                    for i in range(3)
+                    for row, column, place in strips(i, 3 * lead_block)
+                ]
+            lists.append((loads, [(held[step], outs[step])]))
+        return lists
+
+    lead_weights = [prefix_gate, prefix_expand, prefix_down]
+    tail_weights = [action_gate, action_expand, action_down]
+    cuts = list(
+        shuffle(
+            "cut",
+            sizes,
+            lead_weights + (tail_weights if packed else []),
+            cut_shapes[:depth],
+            cut_shapes[:depth],
+            cut_moves,
+            3 + 3 * ratio if packed else 3,
+        )
+    )
+    if not packed:
+        cuts += [
+            jnp.stack(
+                [
+                    lax.dynamic_slice_in_dim(
+                        weight, lax.rem(floor + step, depth) * tail_slice, tail_slice, 1
+                    )
+                    for weight in tail_weights
+                ]
+            )
+            for step in range(depth)
+        ]
+    groups = len(cuts) // depth
+    dealt, mirrored = {}, {}
+
+    def mirror(step):
+        for group in range(groups):
+            mirrored[group, step] = permute(dealt[group, step], depth, 0, True)
+
+    def tied(arrays, steps):
+        keys = [(group, step) for group in range(groups) for step in steps]
+        arrays, blocks = lax.optimization_barrier((arrays, [dealt[key] for key in keys]))
+        dealt.update(zip(keys, blocks))
+        return arrays
+
     lead_float = prefix_tokens.astype(jnp.float32)
     tail_float = action_tokens.astype(jnp.float32)
     lead_unit, lead_scale = norm_forward(lead_float)
@@ -821,25 +926,41 @@
     tail_low = low(tail_unit * action_prenorm)
     lead_pack = by_member([prefix_query, jnp.concatenate([prefix_key, prefix_value], 1)], members)
     tail_pack = by_member([action_query, jnp.concatenate([action_key, action_value], 1)], members)
-    first = [lead_low, tail_low, lead_pack, tail_pack]
+    lead_mixers = by_member([prefix_mixer], members)
+    tail_mixers = by_member([action_mixer], members)
+    packs = [lead_pack, tail_pack, lead_mixers, tail_mixers]
+    shards = [prefix_cotangent, action_cotangent]
+    first = [lead_low, tail_low] + packs + shards
     fanned = lambda pack: (shape_of((depth, 2) + pack.shape), False)
-    lead_normed, tail_normed, lead_in, tail_in = exchange(
+    gathered = lambda shard: (shape_of((depth, breadth, 2) + shard.shape), False)
+    started = exchange(
         "first",
         next(idents),
         sizes,
         ("z", "y", "cam"),
         [(array, True) for array in first],
         [(shape_of((breadth, 2) + array.shape), False) for array in first[:2]]
-        + [fanned(lead_pack), fanned(tail_pack)],
+        + [fanned(pack) for pack in packs]
+        + [gathered(shard) for shard in shards],
         [],
         lambda net, at, ins, outs, held: [
-            fan(net, at, ins[2:], outs[2:]),
+            fan(net, at, ins[2:4], outs[2:4]),
             spread(net, at, ins[:2], outs[:2], False),
+            fan(net, at, ins[4:6], outs[4:6]),
+            spread(net, at, ins[6:], outs[6:], True),
         ],
     )
+    started, cuts = lax.optimization_barrier((started, cuts))
+    for group in range(groups):
+        for step in range(depth):
+            cut = cuts[group * depth + step]
+            dealt[group, step] = permute(cut, depth, step, False) if step > 0 else cut
+    lead_normed, tail_normed, lead_in, tail_in, lead_mix, tail_mix, *uppers = started
+    lead_upper, tail_upper = [array.reshape(-1, array.shape[-1]) for array in uppers]
+    lead_mix, tail_mix = lead_mix.reshape(lead_width, width), tail_mix.reshape(tail_width, width)
+    mirror(0)
     lead_normed = lead_normed.reshape(-1, lead_width)
     tail_normed = tail_normed.reshape(-1, tail_width)
-    member_place = lax.axis_index("cam")
     lead_in = lead_in.reshape(lead_width, -1)
     tail_in = tail_in.reshape(tail_width, -1)
     lead_total, tail_total = lead_normed.shape[0], tail_normed.shape[0]
@@ -849,54 +970,6 @@
     )
     (pairs,) = cam_spread("pairs", [projected[:, width:]])
     pairs = jnp.swapaxes(pairs.reshape(members, -1, pair), 0, 1).reshape(-1, 2 * head_size)
-
-    lead_mixers = by_member([prefix_mixer], members)
-    tail_mixers = by_member([action_mixer], members)
-    lead_slice = prefix_gate.shape[1] // depth
-    tail_slice = action_gate.shape[1] // depth
-    lead_block, tail_block = prefix_gate.shape[0], action_gate.shape[0]
-    tail_weights = [
-        jnp.swapaxes(weight.reshape(tail_block, depth, tail_slice), 0, 1)
-        for weight in (action_gate, action_expand, action_down)
-    ]
-    second = (
-        [(prefix_gate, False), (prefix_expand, False), (prefix_down, False)]
-        + [(weight, False) for weight in tail_weights]
-        + [(lead_mixers, True), (tail_mixers, True)]
-    )
-
-    def second_routines(net, at, ins, outs, held):
-        def columns(ref):
-            return lambda z: ref.at[
-                :, pl.ds(pl.multiple_of(z * lead_slice, lead_slice), lead_slice)
-            ]
-
-        def planes(ref):
-            return lambda z: ref.at[z]
-
-        sources = [columns(ref) for ref in ins[:3]] + [planes(ref) for ref in ins[3:6]]
-        return [
-            fan(net, at, ins[6:8], outs[6:8]),
-            deal(net, at, sources, outs[:6], held),
-        ]
-
-    dealt = exchange(
-        "second",
-        next(idents),
-        sizes,
-        ("z", "deal", "y", "cam"),
-        second,
-        [(shape_of((depth, 2, lead_block, lead_slice)), False)] * 3
-        + [(shape_of((depth, 2, tail_block, tail_slice)), False)] * 3
-        + [fanned(lead_mixers), fanned(tail_mixers)],
-        [pltpu.VMEM((lead_block, lead_slice), jnp.bfloat16)] * 3
-        + [pltpu.VMEM((tail_block, tail_slice), jnp.bfloat16)] * 3,
-        second_routines,
-    )
-    lead_gate, lead_expand, lead_down = [w.reshape(lead_width, lead_slice) for w in dealt[:3]]
-    tail_gate, tail_expand, tail_down = [w.reshape(tail_width, tail_slice) for w in dealt[3:6]]
-    mine = lambda fans, total: fans.reshape(total, width)
-    lead_mix, tail_mix = mine(dealt[6], lead_width), mine(dealt[7], tail_width)
 
     segment_row = prefix_segments[0]
     code_row = action_codes[0]
@@ -924,6 +997,8 @@
             cam_blocks(against(mixed[lead_total:], tail_mix)),
         ],
     )
+    lead_sum, tail_sum = tied([lead_sum, tail_sum], [1])
+    mirror(1)
     lead_hidden = lead_float + lead_sum
     tail_hidden = tail_float + tail_sum
     lead_center, lead_factor = norm_forward(lead_hidden)
@@ -931,111 +1006,158 @@
     lead_second = low(lead_center * prefix_midnorm)
     tail_second = low(tail_center * action_midnorm)
 
-    chunks = max(1, depth // 4)
-    lead_rows, tail_rows = lead_count // chunks, tail_count // chunks
-    sums, grads = [], None
-    for chunk in range(chunks):
-        cut = lambda array: array.reshape(chunks, -1, array.shape[1])[chunk]
-        shards = [cut(prefix_cotangent), cut(action_cotangent), cut(lead_second), cut(tail_second)]
-        if chunk > 0:
-            shards, sums = lax.optimization_barrier((shards, sums))
-        gathered = exchange(
-            "gather" + str(chunk),
+    for step in range(2, depth):
+        lead_second, tail_second = tied([lead_second, tail_second], [step])
+        mirror(step)
+
+    def place_moves(at, ins, held, outs):
+        lists = []
+        for number, (group, step, flip) in enumerate(marks):
+            z = at.later_z((depth - step) % depth)
+            y = 1 - at.y if flip else at.y
+            block = held[number]
+            stores = []
+            if group == 0:
+                stores += [
+                    (block.at[pl.ds(i * lead_block, lead_block), :], outs[i].at[z, y])
+                    for i in range(3)
+                ]
+                if packed:
+                    stores += [
+                        (
+                            block.at[pl.ds(row, strip), pl.ds(column, tail_slice)],
+                            outs[3 + i].at[z, y, pl.ds(place, strip), :],
+                        )
+                        for i in range(3)
+                        for row, column, place in strips(i, 3 * lead_block)
+                    ]
+            else:
+                stores += [(block.at[i], outs[3 + i].at[z, y]) for i in range(3)]
+            lists.append(([(ins[number], block)], stores))
+        return lists
+
+    marks = [
+        (group, step, flip) for group in range(groups) for step in range(depth) for flip in (0, 1)
+    ]
+    blocks = [
+        (mirrored if flip else dealt)[group, step] for group, step, flip in marks
+    ]
+    lead_gate, lead_expand, lead_down, tail_gate, tail_expand, tail_down = [
+        weight.reshape(-1, weight.shape[-1])
+        for weight in shuffle(
+            "place",
+            sizes,
+            blocks,
+            blocks,
+            [shape_of((depth, 2, lead_block, lead_slice))] * 3
+            + [shape_of((depth, 2, tail_block, tail_slice))] * 3,
+            place_moves,
+            3 + 3 * ratio if packed else 3,
+        )
+    ]
+
+    def send_across(packs):
+        sent = []
+        for pack in packs:
+            pack = [low(grad).reshape(depth, 2, -1, grad.shape[1]) for grad in pack]
+            if len(pack) > 1 and packed:
+                pack[1:] = [
+                    jnp.concatenate(jnp.split(grad, ratio, axis=2), axis=3) for grad in pack[1:]
+                ]
+            tables = [pack] if packed or len(pack) == 1 else [pack[:1], pack[1:]]
+            for table in tables:
+                take = lambda y: jnp.concatenate(
+                    [lax.dynamic_index_in_dim(part, y, 1, False) for part in table], 1
+                )
+                own, other = take(side), permute(take(1 - side), depth, 0, True)
+                sent.append((own, other))
+        return sent
+
+    def pass_on(pairs):
+        summed = jnp.concatenate(
+            [low(own.astype(jnp.float32) + other.astype(jnp.float32)) for own, other in pairs], 1
+        )
+        blocks = []
+        for step in range(depth):
+            block = lax.dynamic_index_in_dim(summed, lax.rem(floor + step, depth), 0, False)
+            blocks.append(permute(block, depth, step, False) if step > 0 else block)
+        return blocks
+
+    shards = [lead_second, tail_second]
+    lead_all, tail_all = [
+        array.reshape(-1, array.shape[-1])
+        for array in exchange(
+            "gather",
             next(idents),
             sizes,
             ("z", "cam"),
             [(shard, True) for shard in shards],
-            [(shape_of((depth, breadth, 2) + shard.shape), False) for shard in shards],
+            [gathered(shard) for shard in shards],
             [],
-            lambda net, at, ins, outs, held: [
-                spread(net, at, ins[2:], outs[2:], True),
-                spread(net, at, ins[:2], outs[:2], True),
-            ],
+            lambda net, at, ins, outs, held: [spread(net, at, ins, outs, True)],
         )
-        lead_upper, tail_upper, lead_all, tail_all = [
-            array.reshape(-1, array.shape[-1]) for array in gathered
-        ]
-        lead_out, lead_back, lead_ffgrads = feed_forward(
-            lead_all, lead_upper, lead_gate, lead_expand, lead_down
-        )
-        tail_out, tail_back, tail_ffgrads = feed_forward(
-            tail_all, tail_upper, tail_gate, tail_expand, tail_down
-        )
-        fresh = list(lead_ffgrads) + list(tail_ffgrads)
-        grads = fresh if grads is None else [one + other for one, other in zip(grads, fresh)]
-        last = chunk + 1 == chunks
-        parts = [
-            rows.reshape(depth, breadth, 2, -1, rows.shape[1])
-            for rows in (lead_back, tail_back, lead_out, tail_out)
-        ]
-        blocks = [part.shape[3:] for part in parts]
+    ]
+    tail_out, tail_back, tail_ffgrads = feed_forward(
+        tail_all, tail_upper, tail_gate, tail_expand, tail_down
+    )
+    gate_value = multiply(lead_all, lead_gate)
+    expand_value = multiply(lead_all, lead_expand)
+    inside, pullback = jax.vjp(gated, gate_value, expand_value)
+    inside_low = low(inside)
+    down_grad = low(outer_sum(lead_upper, inside_low))
+    down_grad, lead_upper = lax.optimization_barrier((down_grad, lead_upper))
+    returns = send_across([[down_grad] + list(tail_ffgrads)])
+    inside_grad = multiply(lead_upper, lead_down)
+    gate_grad, expand_grad = pullback(inside_grad)
+    gate_low, expand_low = low(gate_grad), low(expand_grad)
+    returns += send_across(
+        [[outer_sum(lead_all, gate_low)], [outer_sum(lead_all, expand_low)]]
+    )
+    lead_out = low(against(inside_low, lead_down))
+    lead_back = low(against(gate_low, lead_gate) + against(expand_low, lead_expand))
+    (lead_out, lead_back), returns[:-2] = lax.optimization_barrier(
+        ((lead_out, lead_back), returns[:-2])
+    )
+    blocks_back = [pass_on(returns[:1])]
+    if not packed:
+        blocks_back.append(pass_on(returns[1:2]))
+
+    def token_blocks(rows):
+        return rows.reshape(depth, breadth, 2, -1, rows.shape[1])
+
+    def sum_scratch(parts):
         scratch = []
-        for block in blocks:
+        for part in parts:
+            block = part.shape[3:]
             scratch += [
                 pltpu.VMEM((depth, breadth) + block, jnp.bfloat16),
                 pltpu.VMEM((depth, breadth) + block, jnp.bfloat16),
                 pltpu.VMEM((breadth - 1, depth) + block, jnp.bfloat16),
-                pltpu.VMEM((depth,) + block, jnp.bfloat16),
-                pltpu.VMEM((depth,) + block, jnp.bfloat16),
+                pltpu.VMEM((depth - 1,) + block, jnp.bfloat16),
             ]
-
-        def routines(net, at, ins, outs, held):
-            names = ("own", "core", "wide", "up", "down")
-            buffers = [dict(zip(names, held[5 * i : 5 * i + 5])) for i in range(len(parts))]
-            return [collect(net, at, ins, outs, buffers, True)]
-
-        sums.append(
-            exchange(
-                "collect" + str(chunk),
-                next(idents),
-                sizes,
-                ("z", "cam"),
-                [(part, False) for part in parts],
-                [(shape_of(block, jnp.float32), True) for block in blocks],
-                scratch,
-                routines,
-            )
-        )
-    lead_summed, tail_summed, lead_branch, tail_branch = [
-        parts[0] if chunks == 1 else jnp.concatenate(parts, 0) for parts in zip(*sums)
-    ]
-    lead_result = low(lead_hidden + lead_branch)
-    tail_result = low(tail_hidden + tail_branch)
-
-    grads = [low(grad) for grad in grads]
-    lead_returns = [grad.reshape(depth, 2, lead_block, lead_slice) for grad in grads[:3]]
-    tail_returns = [grad.reshape(depth, 2, tail_block, tail_slice) for grad in grads[3:]]
-
-    def return_routines(net, at, ins, outs, held):
-        def columns(ref):
-            return lambda z: ref.at[
-                :, pl.ds(pl.multiple_of(z * lead_slice, lead_slice), lead_slice)
-            ]
-
-        def planes(ref):
-            return lambda z: ref.at[z]
-
-        slots = [columns(ref) for ref in outs[:3]] + [planes(ref) for ref in outs[3:]]
-        buffers = [dict(own=held[2 * i], core=held[2 * i + 1]) for i in range(6)]
-        return [give_back(net, at, ins, slots, buffers)]
-
-    returned = exchange(
-        "returns",
+        return scratch
+
+    def sum_routine(net, at, ins, outs, held):
+        names = ("own", "core", "wide", "far")
+        buffers = [dict(zip(names, held[4 * i : 4 * i + 4])) for i in range(len(ins))]
+        return collect(net, at, ins, outs, buffers, True)
+
+    backs = [token_blocks(lead_back), token_blocks(tail_back)]
+    lead_summed, tail_summed = exchange(
+        "collect",
         next(idents),
         sizes,
-        ("deal", "y"),
-        [(part, False) for part in lead_returns + tail_returns],
-        [(shape_of(prefix_gate.shape), False)] * 3
-        + [(shape_of((depth, tail_block, tail_slice)), False)] * 3,
-        [pltpu.VMEM((depth, lead_block, lead_slice), jnp.bfloat16)] * 6
-        + [pltpu.VMEM((depth, tail_block, tail_slice), jnp.bfloat16)] * 6,
-        return_routines,
-    )
-    ff_grads = [part.astype(jnp.float32) for part in returned[:3]] + [
-        jnp.swapaxes(part, 0, 1).reshape(tail_block, -1).astype(jnp.float32)
-        for part in returned[3:]
-    ]
-
+        ("deal", "cam"),
+        [(part, False) for part in backs],
+        [(shape_of(part.shape[3:], jnp.float32), True) for part in backs],
+        sum_scratch(backs),
+        lambda net, at, ins, outs, held: [sum_routine(net, at, ins, outs, held)],
+    )
+
+    (lead_summed, tail_summed), rest, blocks_back = lax.optimization_barrier(
+        ((lead_summed, tail_summed), returns[-2:], blocks_back)
+    )
+    blocks_back.insert(1, pass_on(rest))
     lead_residual, lead_middle = norm_backward(
         lead_summed, lead_center, lead_factor, prefix_midnorm
     )
@@ -1073,6 +1195,12 @@
         "backs",
         [cam_blocks(against(lead_part, lead_in)), cam_blocks(against(tail_part, tail_in))],
     )
+    (lead_back, tail_back, low_grad, lead_mixing, tail_mixing), blocks_back = (
+        lax.optimization_barrier(
+            ((lead_back, tail_back, low_grad, lead_mixing, tail_mixing), blocks_back)
+        )
+    )
+    lead_part, tail_part = low_grad[:lead_total], low_grad[lead_total:]
     lead_back, lead_first = norm_backward(lead_back, lead_unit, lead_scale, prefix_prenorm)
     tail_back, tail_first = norm_backward(tail_back, tail_unit, tail_scale, action_prenorm)
     lead_input = low(lead_upstream + lead_back)
@@ -1089,23 +1217,41 @@
     scratch = []
     for part in attention_parts:
         block = part.shape[2:]
-        scratch += [pltpu.VMEM((depth,) + block, jnp.bfloat16)] * 4
+        scratch += [pltpu.VMEM((depth,) + block, jnp.bfloat16)] * 2
+        scratch += [pltpu.VMEM((depth - 1,) + block, jnp.bfloat16)]
+    gains = [lead_first, lead_middle, tail_first, tail_middle]
+    device_count = row_count * members
+    table = jnp.concatenate([gain.reshape(device_count, -1) for gain in gains], 1)
+    owned = table.shape[1]
+    span = -(-owned // 128) * 128
+    table = jnp.pad(table, ((0, 0), (0, span - owned)))[:, None, :]
+    branches = [token_blocks(lead_out), token_blocks(tail_out)]
 
     def fold_routines(net, at, ins, outs, held):
-        names = ("own", "core", "up", "down")
-        buffers = [dict(zip(names, held[4 * i : 4 * i + 4])) for i in range(4)]
-        return [fold(net, at, ins, outs, buffers)]
+        names = ("own", "core", "far")
+        buffers = [dict(zip(names, held[3 * i : 3 * i + 3])) for i in range(4)]
+        return [
+            hand_out(net, at, ins[4], outs[4]),
+            fold(net, at, ins[:4], outs[:4], buffers),
+            sum_routine(net, at, ins[5:], outs[5:], held[12:]),
+        ]
 
     folded = exchange(
         "fold",
         next(idents),
         sizes,
-        ("z", "y", "cam"),
-        [(part, False) for part in attention_parts],
-        [(shape_of(part.shape[2:]), False) for part in attention_parts],
-        scratch,
+        ("all",),
+        [(part, False) for part in attention_parts]
+        + [(table, True)]
+        + [(branch, False) for branch in branches],
+        [(shape_of(part.shape[2:]), False) for part in attention_parts]
+        + [(shape_of(table.shape, jnp.float32), True)]
+        + [(shape_of(branch.shape[3:], jnp.float32), True) for branch in branches],
+        scratch + sum_scratch(branches),
         fold_routines,
     )
+    lead_result = low(lead_hidden + folded[5])
+    tail_result = low(tail_hidden + folded[6])
 
     def split(projection, mixer):
         projection = jnp.swapaxes(projection, 0, 1).astype(jnp.float32)
@@ -1118,15 +1264,46 @@
     lead_grads = split(folded[0], folded[2])
     tail_grads = split(folded[1], folded[3])
 
-    gains = [lead_first, lead_middle, tail_first, tail_middle]
-    total = lax.psum(jnp.concatenate(gains), ("rows", "cam"))
-    place = lax.axis_index("rows") * members + member_place
+    whole_block = [(0, 0, lead_block, 0)]
+    parts = []
+    for step in range(depth):
+        parts.append((step, step, 2, lead_slice, whole_block))
+        for i in range(3):
+            if packed:
+                pieces = [(row, column, strip, place) for row, column, place in strips(i, lead_block)]
+                parts.append((step, step, 3 + i, tail_slice, pieces))
+            else:
+                pieces = [(i * tail_block, 0, tail_block, 0)]
+                parts.append((2 * depth + step, step, 3 + i, tail_slice, pieces))
+    for step in range(depth):
+        for i in range(2):
+            pieces = [(i * lead_block, 0, lead_block, 0)]
+            parts.append((depth + step, step, i, lead_slice, pieces))
+    ff_grads = widen(
+        "returns",
+        sizes,
+        sum(blocks_back, []),
+        [shape_of(weight.shape, jnp.float32) for weight in lead_weights]
+        + [
+            shape_of(
+                weight.shape if packed else (depth, tail_block, tail_slice), jnp.float32
+            )
+            for weight in tail_weights
+        ],
+        parts,
+    )
+    if not packed:
+        ff_grads = list(ff_grads[:3]) + [
+            jnp.swapaxes(grad, 0, 1).reshape(tail_block, -1) for grad in ff_grads[3:]
+        ]
+
+    total = jnp.sum(folded[4][:, 0], axis=0)
     gain_grads = []
     offset = 0
     for gain in gains:
-        share = gain.shape[0] // (row_count * members)
-        gain_grads.append(lax.dynamic_slice_in_dim(total, offset + place * share, share))
-        offset += gain.shape[0]
+        share = gain.shape[0] // device_count
+        gain_grads.append(total[offset : offset + share])
+        offset += share
 
     return (
         (lead_result, tail_result, lead_input, tail_input)

time: 1480 us -> 1040 us (0.70)
  Pallas kernels: 1180 us -> 599 us
  waiting for transfers between devices: 0 us -> 143 us
  starting transfers between devices: 0 us -> 52 us
  blocking collectives: 45.9 us -> 0 us
    pallas_call x11 -> x9, Pallas kernels: 1180 us -> 569 us  [exchange(): pl.pallas_call(kernel, name=label, out_shape=[shape for shape, _ in outpu...]
    ppermute x0 -> x16, waiting for transfers between devices: none -> 143 us  [permute(): return lax.ppermute(array, 'rows', pairs)]
    ppermute x0 -> x16, starting transfers between devices: none -> 52 us  [permute(): return lax.ppermute(array, 'rows', pairs)]
    psum x1 -> x0, blocking collectives: 45.9 us -> none  [body(): total = lax.psum(jnp.concatenate(gains), ('rows', 'cam'))]
    pallas_call x0 -> x3, Pallas kernels: none -> 30 us  [the longest x2 19.6 us: shuffle(): pl.pallas_call(kernel, name=label, out_shape=outs, in_specs=[pl.BlockSpec...]
  transfers between devices with their start and end apart: 0 -> 16, of which waited for: 0 -> 6; matrix products, arithmetic and copies ran while one was open for 0% -> 8% of each run, Pallas kernels for 0% -> 25%
where the time goes in v2:
time: 1040 us; the launch traced here: 1030 us
  Pallas kernels  599 us (58%)
  matrix products  172 us (17%)
  waiting for transfers between devices  143 us (14%)
  starting transfers between devices  52 us (5%)
  other arithmetic  38.4 us (4%)
  local copies, waits for them, and re-layouts  25.3 us (2%)
    pallas_call x9, Pallas kernels, exchange(): pl.pallas_call(kernel, name=label, out_shape=[shape for shape, _ in outpu...  569 us
    ppermute x16, waiting for transfers between devices, permute(): return lax.ppermute(array, 'rows', pairs)  143 us
    dot_general x10, matrix products, multiply(): return jnp.dot(operand, matrix, preferred_element_type=jnp.float32)  61.3 us
    dot_general x10, matrix products, against(): lax.dot_general(operand, matrix, (((1,), (1,)), ((), ())), preferred_elem...  56.3 us
    ppermute x16, starting transfers between devices, permute(): return lax.ppermute(array, 'rows', pairs)  52 us
    dot_general x10, matrix products, outer_sum(): lax.dot_general(operand, matrix, (((0,), (0,)), ((), ())), preferred_elem...  48.3 us
  transfers between devices with their start and end apart: 16, of which 6 were waited for; matrix products, arithmetic and copies ran while one was open for 8% of the time, Pallas kernels for 25%

profile of v2, /device:TPU:0, one launch (start us, length us, event | category | flops | bytes accessed | tf_op | source)
XLA Modules:
  0.0 1032.2 jit_solution(12842248887801889756)
XLA Ops:
  13.4 7.3 cut.1
  20.7 122.9 %first.1 = (bf16[2,2,128,2048]{3,2,1,0:T(8,128)(2,1)}, bf16[2,2,16,1024]{3,2,1,0:T(8,128)(2,1)}, bf16[4,2,4,64,640]{4,3,2,1,0:T(8,128)(2,1)}, bf16[4,2,4,32,640]...) custom-call(bf16[128,2048]{1,0:T(8,128)(2,1)} %fusion.33.refs_0_, ...), custom_call_target="tpu_custom_call" | custom-call | bytes 3000000 | tf_op jit(solution)/shard_map/first/pallas_call | solution.py:575
  150.0 4.2 convolution_convert_fusion.8
  154.9 13.0 %pairs.1 = bf16[2,2,576,128]{3,2,1,0:T(8,128)(2,1)} custom-call(bf16[576,128]{1,0:T(8,128)(2,1)} %pad_maximum_fusion.9.refs_0_), custom_call_target="tpu_custom_call" | custom-call | bytes 3000000 | tf_op jit(solution)/shard_map/pairs/pallas_call | solution.py:575
  173.5 4.4 convolution_convert_fusion.5
  179.1 22.4 %mixing.1 = (f32[128,2048]{1,0:T(8,128)}, f32[16,1024]{1,0:T(8,128)}) custom-call(bf16[2,2,128,2048]{3,2,1,0:T(8,128)(2,1)} %bitcast.343, bf16[2,2,16,1024]{3,2,1,0:T(8,128)(2,1)} %bitcast.371), custom_call_target="tpu_custom_call" | custom-call | bytes 3000000 | tf_op jit(solution)/shard_map/mixing/pallas_call | solution.py:575
  205.7 56.7 %collective-permute-done.1.refs_4_ = bf16[864,1024]{1,0:T(8,128)(2,1)} collective-permute-done((bf16[864,1024]{1,0:T(8,128)(2,1)}, bf16[864,1024]{1,0:T(8,128)(2,1)}, u32[]{:S(2)}, u32[]{:S(2)}) %collective-permute-start.1) | collective-permute-done | bytes 1769504 | tf_op jit(solution)/shard_map/ppermute | solution.py:601
  265.0 96.6 %gather.1 = (bf16[4,2,2,128,2048]{4,3,2,1,0:T(8,128)(2,1)}, bf16[4,2,2,16,1024]{4,3,2,1,0:T(8,128)(2,1)}) custom-call(bf16[128,2048]{1,0:T(8,128)(2,1)} %multiply_convert_fusion.2.refs_0_, bf16[16,1024]{1,0:T(8,128)(2,1)} %multiply_convert_fusion.5.refs_1_), custom_call_target="tpu_custom_call" | custom-call | bytes 3000000 | tf_op jit(solution)/shard_map/gather/pallas_call | solution.py:575
  361.7 16.7 %collective-permute-done.4.refs_3_ = bf16[864,1024]{1,0:T(8,128)(2,1)} collective-permute-done((bf16[864,1024]{1,0:T(8,128)(2,1)}, bf16[864,1024]{1,0:T(8,128)(2,1)}, u32[]{:S(2)}, u32[]{:S(2)}) %collective-permute-start.4) | collective-permute-done | bytes 1769504 | tf_op jit(solution)/shard_map/ppermute | solution.py:601
  378.3 12.3 %place.1 = (bf16[4,2,256,1024]{3,2,1,0:T(8,128)(2,1)}, bf16[4,2,256,1024]{3,2,1,0:T(8,128)(2,1)}, bf16[4,2,256,1024]{3,2,1,0:T(8,128)(2,1)}, bf16[4,2,128,256]{3...) custom-call(bf16[864,1024]{1,0:T(8,128)(2,1)} %get-tuple-element.143.refs_0_, ...), custom_call_target="tpu_custom_call" | custom-call | bytes 28311552 | tf_op jit(solution)/shard_map/place/pallas_call | solution.py:629
  390.6 14.5 %fusion.97 = f32[2048,1024]{1,0:T(8,128)} fusion(bf16[2048,2048]{1,0:T(8,128)(2,1)} %bitcast.391, bf16[2048,1024]{1,0:T(8,128)(2,1)} %bitcast.399), kind=kOutput, calls=%fused_computation.227 | convolution fusion | flops 8589934592 | bytes 20971520 | tf_op jit(solution)/shard_map/dot_general | solution.py:703
  405.2 14.2 %multiply_convert_fusion.1 = (bf16[2048,1024]{1,0:T(8,128)(2,1)}, f32[2048,1024]{1,0:T(8,128)}) fusion(f32[2048,1024]{1,0:T(8,128)} %fusion.97, bf16[2048,2048]{1,0:T(8,128)(2,1)S(1)} %bitcast.393, bf16[2048,1024]{1,0:T(8,128)(2,1)S(1)} %bitcast.401), kind=kOutput, calls=%fused_computation.11 | convolution fusion | flops 8610906112 | bytes 33554432 | tf_op jit(solution)/shard_map/dot_general | solution.py:703
  419.4 12.8 %convolution_convert_fusion.3 = bf16[2048,1024]{1,0:T(8,128)(2,1)S(1)} fusion(bf16[2048,2048]{1,0:T(8,128)(2,1)} %bitcast.389, bf16[2048,1024]{1,0:T(8,128)(2,1)} %get-tuple-element.271), kind=kOutput, calls=%fused_computation.27 | convolution fusion | flops 8592031744 | bytes 16777216 | tf_op jit(solution)/shard_map/dot_general | solution.py:713
  432.2 21.8 %fusion.6 = (bf16[2048,1024]{1,0:T(8,128)(2,1)}, bf16[2048,1024]{1,0:T(8,128)(2,1)}) fusion(f32[2048,1024]{1,0:T(8,128)} %fusion.97, f32[2048,1024]{1,0:T(8,128)} %get-tuple-element.272, bf16[2048,2048]{1,0:T(8,128)(2,1)} %bitcast.390, bf16[2048,1024]{1,0:T(8,128)(2,1)S(1)} %bitcast.398), kind=kOutput, calls=%fused_computation.9 | convolution fusion | flops 8640266240 | bytes 37748736 | tf_op jit(solution)/shard_map/dot_general | solution.py:703
  454.0 12.8 %convolution_convert_fusion.1 = bf16[2048,1024]{1,0:T(8,128)(2,1)S(1)} fusion(bf16[2048,2048]{1,0:T(8,128)(2,1)} %bitcast.392, bf16[2048,1024]{1,0:T(8,128)(2,1)} %get-tuple-element.217), kind=kOutput, calls=%fused_computation.25 | convolution fusion | flops 8592031744 | bytes 16777216 | tf_op jit(solution)/shard_map/dot_general | solution.py:713
  466.9 11.9 %fusion.98 = f32[2048,2048]{1,0:T(8,128)} fusion(bf16[2048,1024]{1,0:T(8,128)(2,1)S(1)} %copy-done.85, bf16[2048,1024]{1,0:T(8,128)(2,1)S(1)} %bitcast.402), kind=kOutput, calls=%fused_computation.228 | convolution fusion | flops 8589934592 | bytes 25165824 | tf_op jit(solution)/shard_map/dot_general | solution.py:707
  484.8 10.8 %convolution_convert_fusion.2 = bf16[2048,1024]{1,0:T(8,128)(2,1)S(1)} fusion(bf16[2048,2048]{1,0:T(8,128)(2,1)S(1)} %bitcast.396, bf16[2048,1024]{1,0:T(8,128)(2,1)} %get-tuple-element.216), kind=kOutput, calls=%fused_computation.26 | convolution fusion | flops 8592031744 | bytes 16777216 | tf_op jit(solution)/shard_map/dot_general | solution.py:713
  502.8 16.6 %add_convert_fusion = bf16[2048,2048]{1,0:T(8,128)(2,1)} fusion(f32[2048,2048]{1,0:T(8,128)} %fusion.98, bf16[2048,1024]{1,0:T(8,128)(2,1)} %get-tuple-element.216, bf16[2048,1024]{1,0:T(8,128)(2,1)} %bitcast.400), kind=kOutput, calls=%fused_computation | convolution fusion | flops 8598323200 | bytes 33554432 | tf_op jit(solution)/shard_map/dot_general | solution.py:707
  519.4 14.0 %convolution_convert_fusion = bf16[2048,2048]{1,0:T(8,128)(2,1)} fusion(bf16[2048,1024]{1,0:T(8,128)(2,1)} %get-tuple-element.271, bf16[2048,1024]{1,0:T(8,128)(2,1)} %bitcast.397), kind=kOutput, calls=%fused_computation.13 | convolution fusion | flops 8594128896 | bytes 16777216 | tf_op jit(solution)/shard_map/dot_general | solution.py:707
  533.7 14.0 %collective-permute-done.7 = bf16[4,352,1024]{2,1,0:T(8,128)(2,1)S(1)} collective-permute-done((bf16[4,352,1024]{2,1,0:T(8,128)(2,1)S(1)}, bf16[4,352,1024]{2,1,0:T(8,128)(2,1)S(1)}, u32[]{:S(2)}, u32[]{:S(2)}) %collective-permute-start.7) | collective-permute-done | bytes 2883616 | tf_op jit(solution)/shard_map/ppermute | solution.py:601
  550.8 21.0 %collective-permute-start.12 = (bf16[352,1024]{1,0:T(8,128)(2,1)}, bf16[352,1024]{1,0:T(8,128)(2,1)}, u32[]{:S(2)}, u32[]{:S(2)}) collective-permute-start(bf16[352,1024]{1,0:T(8,128)(2,1)} %get-tuple-element.228), channel_id=1, source_target_pairs={{0,24},{4,28},{8,0},{12,4},{16,8},{20,12},{24,16},{28,20},{1,25},{... | collective-permute-start | bytes 2162696 | tf_op jit(solution)/shard_map/ppermute | solution.py:601
  571.8 18.9 %collective-permute-start.11 = (bf16[352,1024]{1,0:T(8,128)(2,1)}, bf16[352,1024]{1,0:T(8,128)(2,1)}, u32[]{:S(2)}, u32[]{:S(2)}) collective-permute-start(bf16[352,1024]{1,0:T(8,128)(2,1)} %get-tuple-element.229), channel_id=1, source_target_pairs={{0,16},{4,20},{8,24},{12,28},{16,0},{20,4},{24,8},{28,12},{1,17},{... | collective-permute-start | bytes 2162696 | tf_op jit(solution)/shard_map/ppermute | solution.py:601
  593.4 108.4 %collect.1 = (f32[128,2048]{1,0:T(8,128)}, f32[16,1024]{1,0:T(8,128)}) custom-call(bf16[4,2,2,128,2048]{4,3,2,1,0:T(8,128)(2,1)} %bitcast.317, bf16[4,2,2,16,1024]{4,3,2,1,0:T(8,128)(2,1)} %bitcast.340), custom_call_target="tpu_custom_call" | custom-call | bytes 3000000 | tf_op jit(solution)/shard_map/collect/pallas_call | solution.py:575
  707.3 21.9 %sent.1 = (bf16[2,2,128,2048]{3,2,1,0:T(8,128)(2,1)}, bf16[2,2,16,1024]{3,2,1,0:T(8,128)(2,1)}) custom-call(bf16[128,2048]{1,0:T(8,128)(2,1)} %fusion.86.refs_0_, bf16[16,1024]{1,0:T(8,128)(2,1)} %fusion.83.refs_1_), custom_call_target="tpu_custom_call" | custom-call | bytes 3000000 | tf_op jit(solution)/shard_map/sent/pallas_call | solution.py:575
  729.3 3.6 fusion.102
  740.0 13.1 %pair_grads.1 = f32[576,128]{1,0:T(8,128)} custom-call(bf16[2,2,576,128]{3,2,1,0:T(8,128)(2,1)} %bitcast.337), custom_call_target="tpu_custom_call" | custom-call | bytes 3000000 | tf_op jit(solution)/shard_map/pair_grads/pallas_call | solution.py:575
  771.1 22.6 %backs.1 = (f32[128,2048]{1,0:T(8,128)}, f32[16,1024]{1,0:T(8,128)}) custom-call(bf16[2,2,128,2048]{3,2,1,0:T(8,128)(2,1)} %bitcast.342, bf16[2,2,16,1024]{3,2,1,0:T(8,128)(2,1)} %bitcast.370), custom_call_target="tpu_custom_call" | custom-call | bytes 3000000 | tf_op jit(solution)/shard_map/backs/pallas_call | solution.py:575
  795.2 4.5 fusion.104
  799.6 9.9 collective-permute-done.15.refs_7_
  810.5 44.8 %collective-permute-done.14.refs_6_ = bf16[512,1024]{1,0:T(8,128)(2,1)} collective-permute-done((bf16[512,1024]{1,0:T(8,128)(2,1)}, bf16[512,1024]{1,0:T(8,128)(2,1)}, u32[]{:S(2)}, u32[]{:S(2)}) %collective-permute-start.14) | collective-permute-done | bytes 1048608 | tf_op jit(solution)/shard_map/ppermute | solution.py:601
  862.8 147.6 %fold.1 = (bf16[4,64,640]{2,1,0:T(8,128)(2,1)}, bf16[4,32,640]{2,1,0:T(8,128)(2,1)}, bf16[4,64,512]{2,1,0:T(8,128)(2,1)}, bf16[4,32,512]{2,1,0:T(8,128)(2,1)}, f...) custom-call(bf16[4,2,4,64,640]{4,3,2,1,0:T(8,128)(2,1)} %bitcast.336, ...), custom_call_target="tpu_custom_call" | custom-call | bytes 3000000 | tf_op jit(solution)/shard_map/fold/pallas_call | solution.py:575
  1021.5 10.5 %returns.1 = (f32[256,4096]{1,0:T(8,128)}, f32[256,4096]{1,0:T(8,128)}, f32[256,4096]{1,0:T(8,128)}, f32[128,1024]{1,0:T(8,128)}, f32[128,1024]{1,0:T(8,128)}, /*index=5*/f32[128,1024]{1,0:T(8,128)}) custom-call(bf16[352,1024]{1,0:T(8,128)(2,1)} %get-tuple-element.190.refs_0_, bf16[352,1024]{1,0:T(8,128)(2,1)} %collective-permute-done.10.refs_1_, ...), custom_call_target="tpu_custom_call" | custom-call | bytes 21233664 | tf_op jit(solution)/shard_map/returns/pallas_call | solution.py:684
  (318 shorter events, 103.2 us)
Async XLA Ops:
  143.7 57.8 %collective-permute-start = (bf16[864,1024]{1,0:T(8,128)(2,1)}, bf16[864,1024]{1,0:T(8,128)(2,1)}, u32[]{:S(2)}, u32[]{:S(2)}) collective-permute-start(bf16[864,1024]{1,0:T(8,128)(2,1)} %get-tuple-element.133), channel_id=1, source_target_pairs={{0,8},{4,12},{8,16},{12,20},{16,24},{20,28},{24,0},{28,4},{1,9},{5... | collective-permute-start | bytes 5308424 | tf_op jit(solution)/shard_map/ppermute | solution.py:601
  143.8 118.6 %collective-permute-start.1 = (bf16[864,1024]{1,0:T(8,128)(2,1)}, bf16[864,1024]{1,0:T(8,128)(2,1)}, u32[]{:S(2)}, u32[]{:S(2)}) collective-permute-start(bf16[864,1024]{1,0:T(8,128)(2,1)} %get-tuple-element.136), channel_id=1, source_target_pairs={{0,16},{4,20},{8,24},{12,28},{16,0},{20,4},{24,8},{28,12},{1,17},{... | collective-permute-start | bytes 5308424 | tf_op jit(solution)/shard_map/ppermute | solution.py:601
  145.6 116.8 %collective-permute-start.2 = (bf16[864,1024]{1,0:T(8,128)(2,1)}, bf16[864,1024]{1,0:T(8,128)(2,1)}, u32[]{:S(2)}, u32[]{:S(2)}) collective-permute-start(bf16[864,1024]{1,0:T(8,128)(2,1)} %get-tuple-element.139), channel_id=1, source_target_pairs={{0,24},{4,28},{8,0},{12,4},{16,8},{20,12},{24,16},{28,20},{1,25},{... | collective-permute-start | bytes 5308424 | tf_op jit(solution)/shard_map/ppermute | solution.py:601
  147.7 213.9 %collective-permute-start.3 = (bf16[864,1024]{1,0:T(8,128)(2,1)}, bf16[864,1024]{1,0:T(8,128)(2,1)}, u32[]{:S(2)}, u32[]{:S(2)}) collective-permute-start(bf16[864,1024]{1,0:T(8,128)(2,1)} %get-tuple-element.143.refs_0_), channel_id=1, source_target_pairs={{0,4},{4,0},{8,12},{12,8},{16,20},{20,16},{24,28},{28,24},{1,5},{5... | collective-permute-start | bytes 5308424 | tf_op jit(solution)/shard_map/ppermute | solution.py:601
  173.5 188.1 %copy-start.40 = (bf16[512,2,256]{0,2,1:T(8,128)(2,1)}, bf16[512,2,256]{0,2,1:T(8,128)(2,1)S(1)}, u32[]{:S(2)}) copy-start(bf16[512,2,256]{0,2,1:T(8,128)(2,1)S(1)} %copy.62) | copy-start | bytes 1572868
  203.0 59.4 %copy-start.61 = (f32[128]{0:T(128)}, f32[128]{0:T(128)S(1)}, u32[]{:S(2)}) copy-start(f32[128]{0:T(128)S(1)} %add_rsqrt_fusion.1) | copy-start | bytes 1540
  204.0 58.4 %copy-start.18 = (f32[16,1024]{1,0:T(8,128)}, f32[16,1024]{1,0:T(8,128)S(1)}, u32[]{:S(2)}) copy-start(f32[16,1024]{1,0:T(8,128)S(1)} %get-tuple-element.213) | copy-start | bytes 196612
  204.1 58.3 %copy-start.58 = (f32[16]{0:T(128)}, f32[16]{0:T(128)S(1)}, u32[]{:S(2)}) copy-start(f32[16]{0:T(128)S(1)} %add_rsqrt_fusion) | copy-start | bytes 196
  262.4 99.2 %collective-permute-start.6 = (bf16[864,1024]{1,0:T(8,128)(2,1)}, bf16[864,1024]{1,0:T(8,128)(2,1)S(1)}, u32[]{:S(2)}, u32[]{:S(2)}) collective-permute-start(bf16[864,1024]{1,0:T(8,128)(2,1)} %collective-permute-done.2.refs_6_), channel_id=1, source_target_pairs={{0,4},{4,0},{8,12},{12,8},{16,20},{20,16},{24,28},{28,24},{1,5},{5... | collective-permute-start | bytes 5308424 | tf_op jit(solution)/shard_map/ppermute | solution.py:601
  263.0 98.7 %collective-permute-start.5 = (bf16[864,1024]{1,0:T(8,128)(2,1)}, bf16[864,1024]{1,0:T(8,128)(2,1)}, u32[]{:S(2)}, u32[]{:S(2)}) collective-permute-start(bf16[864,1024]{1,0:T(8,128)(2,1)} %collective-permute-done.1.refs_4_), channel_id=1, source_target_pairs={{0,4},{4,0},{8,12},{12,8},{16,20},{20,16},{24,28},{28,24},{1,5},{5... | collective-permute-start | bytes 5308424 | tf_op jit(solution)/shard_map/ppermute | solution.py:601
  264.5 113.8 %collective-permute-start.4 = (bf16[864,1024]{1,0:T(8,128)(2,1)}, bf16[864,1024]{1,0:T(8,128)(2,1)}, u32[]{:S(2)}, u32[]{:S(2)}) collective-permute-start(bf16[864,1024]{1,0:T(8,128)(2,1)} %collective-permute-done.refs_2_), channel_id=1, source_target_pairs={{0,4},{4,0},{8,12},{12,8},{16,20},{20,16},{24,28},{28,24},{1,5},{5... | collective-permute-start | bytes 5308424 | tf_op jit(solution)/shard_map/ppermute | solution.py:601
  482.3 65.4 %collective-permute-start.7 = (bf16[4,352,1024]{2,1,0:T(8,128)(2,1)S(1)}, bf16[4,352,1024]{2,1,0:T(8,128)(2,1)S(1)}, u32[]{:S(2)}, u32[]{:S(2)}) collective-permute-start(bf16[4,352,1024]{2,1,0:T(8,128)(2,1)S(1)} %pad_maximum_fusion.1), channel_id=1, source_target_pairs={{0,4},{4,0},{8,12},{12,8},{16,20},{20,16},{24,28},{28,24},{1,5},{5... | collective-permute-start | bytes 8650760 | tf_op jit(solution)/shard_map/ppermute | solution.py:601
  500.8 201.0 %collective-permute-start.8 = (bf16[4,256,1024]{2,1,0:T(8,128)(2,1)}, bf16[4,256,1024]{2,1,0:T(8,128)(2,1)}, u32[]{:S(2)}, u32[]{:S(2)}) collective-permute-start(bf16[4,256,1024]{2,1,0:T(8,128)(2,1)} %get-tuple-element.224), channel_id=1, source_target_pairs={{0,4},{4,0},{8,12},{12,8},{16,20},{20,16},{24,28},{28,24},{1,5},{5... | collective-permute-start | bytes 6291464 | tf_op jit(solution)/shard_map/ppermute | solution.py:601
  501.3 200.5 %collective-permute-start.9 = (bf16[4,256,1024]{2,1,0:T(8,128)(2,1)}, bf16[4,256,1024]{2,1,0:T(8,128)(2,1)}, u32[]{:S(2)}, u32[]{:S(2)}) collective-permute-start(bf16[4,256,1024]{2,1,0:T(8,128)(2,1)} %get-tuple-element.222), channel_id=1, source_target_pairs={{0,4},{4,0},{8,12},{12,8},{16,20},{20,16},{24,28},{28,24},{1,5},{5... | collective-permute-start | bytes 6291464 | tf_op jit(solution)/shard_map/ppermute | solution.py:601
  549.2 41.5 %copy-start.37 = (bf16[256,256]{1,0:T(8,128)(2,1)S(1)}, bf16[256,256]{1,0:T(8,128)(2,1)}, u32[]{:S(2)}) copy-start(bf16[256,256]{1,0:T(8,128)(2,1)} %copy-done.36) | copy-start | bytes 393220
  549.2 42.6 %copy-start.42 = (bf16[256,256]{1,0:T(8,128)(2,1)S(1)}, bf16[256,256]{1,0:T(8,128)(2,1)}, u32[]{:S(2)}) copy-start(bf16[256,256]{1,0:T(8,128)(2,1)} %copy-done.41) | copy-start | bytes 393220
  549.2 43.0 %copy-start.34 = (bf16[4,2,128,256]{3,2,1,0:T(8,128)(2,1)S(1)}, bf16[4,2,128,256]{3,2,1,0:T(8,128)(2,1)}, u32[]{:S(2)}) copy-start(bf16[4,2,128,256]{3,2,1,0:T(8,128)(2,1)} %get-tuple-element.157) | copy-start | bytes 1572868
  550.8 151.0 %collective-permute-start.12 = (bf16[352,1024]{1,0:T(8,128)(2,1)}, bf16[352,1024]{1,0:T(8,128)(2,1)}, u32[]{:S(2)}, u32[]{:S(2)}) collective-permute-start(bf16[352,1024]{1,0:T(8,128)(2,1)} %get-tuple-element.228), channel_id=1, source_target_pairs={{0,24},{4,28},{8,0},{12,4},{16,8},{20,12},{24,16},{28,20},{1,25},{... | collective-permute-start | bytes 2162696 | tf_op jit(solution)/shard_map/ppermute | solution.py:601
  571.8 130.0 %collective-permute-start.11 = (bf16[352,1024]{1,0:T(8,128)(2,1)}, bf16[352,1024]{1,0:T(8,128)(2,1)}, u32[]{:S(2)}, u32[]{:S(2)}) collective-permute-start(bf16[352,1024]{1,0:T(8,128)(2,1)} %get-tuple-element.229), channel_id=1, source_target_pairs={{0,16},{4,20},{8,24},{12,28},{16,0},{20,4},{24,8},{28,12},{1,17},{... | collective-permute-start | bytes 2162696 | tf_op jit(solution)/shard_map/ppermute | solution.py:601
  590.7 111.2 %collective-permute-start.10 = (bf16[352,1024]{1,0:T(8,128)(2,1)}, bf16[352,1024]{1,0:T(8,128)(2,1)}, u32[]{:S(2)}, u32[]{:S(2)}) collective-permute-start(bf16[352,1024]{1,0:T(8,128)(2,1)} %get-tuple-element.230), channel_id=1, source_target_pairs={{0,8},{4,12},{8,16},{12,20},{16,24},{20,28},{24,0},{28,4},{1,9},{5... | collective-permute-start | bytes 2162696 | tf_op jit(solution)/shard_map/ppermute | solution.py:601
  593.3 108.6 %copy-start.19 = (f32[16,1024]{1,0:T(8,128)S(1)}, f32[16,1024]{1,0:T(8,128)}, u32[]{:S(2)}) copy-start(f32[16,1024]{1,0:T(8,128)} %copy-done.18) | copy-start | bytes 196612
  593.3 108.6 %copy-start.52 = (f32[1024]{0:T(1024)S(1)}, f32[1024]{0:T(1024)}, u32[]{:S(2)}) copy-start(f32[1024]{0:T(1024)} %param.41) | copy-start | bytes 12292
  593.3 108.6 %copy-start.59 = (f32[16]{0:T(128)S(1)}, f32[16]{0:T(128)}, u32[]{:S(2)}) copy-start(f32[16]{0:T(128)} %copy-done.58) | copy-start | bytes 196
  593.3 109.7 %copy-start.1 = (f32[128,2048]{1,0:T(8,128)S(1)}, f32[128,2048]{1,0:T(8,128)}, u32[]{:S(2)}) copy-start(f32[128,2048]{1,0:T(8,128)} %copy-done) | copy-start | bytes 3145732
  593.3 109.7 %copy-start.47 = (f32[2048]{0:T(1024)S(1)}, f32[2048]{0:T(1024)}, u32[]{:S(2)}) copy-start(f32[2048]{0:T(1024)} %param.39) | copy-start | bytes 24580
  593.3 109.7 %copy-start.62 = (f32[128]{0:T(128)S(1)}, f32[128]{0:T(128)}, u32[]{:S(2)}) copy-start(f32[128]{0:T(128)} %copy-done.61) | copy-start | bytes 1540
  593.4 111.3 %copy-start.43 = (bf16[16,1024]{1,0:T(8,128)(2,1)S(1)}, bf16[16,1024]{1,0:T(8,128)(2,1)}, u32[]{:S(2)}) copy-start(bf16[16,1024]{1,0:T(8,128)(2,1)} %refs_7_.1) | copy-start | bytes 98308
  593.4 112.8 %copy-start.7 = (bf16[128,2048]{1,0:T(8,128)(2,1)S(1)}, bf16[128,2048]{1,0:T(8,128)(2,1)}, u32[]{:S(2)}) copy-start(bf16[128,2048]{1,0:T(8,128)(2,1)} %refs_6_.1) | copy-start | bytes 1572868
  762.3 47.3 %collective-permute-start.15 = (bf16[512,1024]{1,0:T(8,128)(2,1)}, bf16[512,1024]{1,0:T(8,128)(2,1)}, u32[]{:S(2)}, u32[]{:S(2)}) collective-permute-start(bf16[512,1024]{1,0:T(8,128)(2,1)} %get-tuple-element.218), channel_id=1, source_target_pairs={{0,24},{4,28},{8,0},{12,4},{16,8},{20,12},{24,16},{28,20},{1,25},{... | collective-permute-start | bytes 3145736 | tf_op jit(solution)/shard_map/ppermute | solution.py:601
  762.3 48.2 %collective-permute-start.13 = (bf16[512,1024]{1,0:T(8,128)(2,1)}, bf16[512,1024]{1,0:T(8,128)(2,1)}, u32[]{:S(2)}, u32[]{:S(2)}) collective-permute-start(bf16[512,1024]{1,0:T(8,128)(2,1)} %get-tuple-element.220), channel_id=1, source_target_pairs={{0,8},{4,12},{8,16},{12,20},{16,24},{20,28},{24,0},{28,4},{1,9},{5... | collective-permute-start | bytes 3145736 | tf_op jit(solution)/shard_map/ppermute | solution.py:601
  764.3 90.9 %collective-permute-start.14 = (bf16[512,1024]{1,0:T(8,128)(2,1)}, bf16[512,1024]{1,0:T(8,128)(2,1)}, u32[]{:S(2)}, u32[]{:S(2)}) collective-permute-start(bf16[512,1024]{1,0:T(8,128)(2,1)} %get-tuple-element.221), channel_id=1, source_target_pairs={{0,16},{4,20},{8,24},{12,28},{16,0},{20,4},{24,8},{28,12},{1,17},{... | collective-permute-start | bytes 3145736 | tf_op jit(solution)/shard_map/ppermute | solution.py:601
  795.2 60.0 %copy-start.84 = (bf16[2,2,128,2048]{3,2,1,0:T(8,128)(2,1)S(1)}, bf16[2,2,128,2048]{3,2,1,0:T(8,128)(2,1)}, u32[]{:S(2)}) copy-start(bf16[2,2,128,2048]{3,2,1,0:T(8,128)(2,1)} %get-tuple-element.125) | copy-start | bytes 6291460
  (72 other events, 596.0 us)

commit v3 on v2

--- a/solution.py
+++ b/solution.py
@@ -1,4 +1,4 @@
-import functools
+import math
 
 import jax
 import jax.numpy as jnp
@@ -33,6 +33,14 @@
 
     def later_z(self, step):
         return lax.rem(self.z + step, self.depth)
+
+    def flip_z(self, bits):
+        z, bit = self.z, 1
+        while bit < self.depth:
+            if bits & bit:
+                z = z + bit - 2 * bit * lax.rem(self.z // bit, 2)
+            bit *= 2
+        return z
 
 
 def guarded(condition, action):
@@ -352,6 +360,15 @@
         transfer.got()
 
 
+def halvings(depth):
+    return sorted(range(1, depth), key=lambda bits: (bits & -bits, -bits)) + [0]
+
+
+def merging(bits, depth):
+    limit = bits & -bits if bits else depth
+    return [bits + e for e in (1 << i for i in range(depth.bit_length())) if e < limit]
+
+
 def add_all(target, sources):
     count = target.shape[0]
     step = 16 if count % 16 == 0 else 8
@@ -376,7 +393,7 @@
     for i, (part, buffer) in enumerate(zip(parts, buffers)):
         own, core, wide = buffer["own"], buffer["core"], buffer["wide"]
         for s in range(depth):
-            t = at.later_z(s) if chained else 0
+            t = at.flip_z(s) if chained else 0
             for step in range(at.breadth):
                 x = at.later_x(step)
                 loads[i, s, step] = Local(
@@ -402,10 +419,10 @@
                     net,
                     lambda own=own, s=s: own.at[s, 0],
                     lambda buffer=buffer, s=s: buffer["far"].at[s - 1],
-                    at.device(z=t),
+                    at.device(z=at.flip_z(s & -s)),
                 )
     steps = list(range(1, at.breadth)) + [0]
-    spans = list(range(1, depth)) + [0]
+    spans = halvings(depth)
     count = len(parts)
     for i in range(count):
         for s in spans:
@@ -429,17 +446,14 @@
             for step in steps[:-1]:
                 across[i, s, step].got()
             terms = [own.at[s, 0], core.at[s, 0]] + [wide.at[step - 1, s] for step in steps[:-1]]
+            for other in merging(s, depth):
+                beyond[i, other].got()
+                terms.append(buffers[i]["far"].at[other - 1])
             if s > 0:
                 add_all(own.at[s, 0], terms)
                 beyond[i, s].start()
             else:
                 add_all(outs[i], terms)
-    for i in range(count):
-        if depth > 1:
-            yield
-            for s in spans[:-1]:
-                beyond[i, s].got()
-            add_all(outs[i], [outs[i]] + [buffers[i]["far"].at[s - 1] for s in spans[:-1]])
 
 
 def fold(net, at, parts, outs, buffers):
@@ -449,7 +463,7 @@
     for i, (part, buffer) in enumerate(zip(parts, buffers)):
         own, core, far = buffer["own"], buffer["core"], buffer["far"]
         for s in range(at.depth):
-            t = at.later_z(s)
+            t = at.flip_z(s)
             loads[i, s] = Local(
                 net,
                 lambda part=part, t=t: part.at[t, at.y],
@@ -466,7 +480,7 @@
                     net,
                     lambda own=own, s=s: own.at[s],
                     lambda far=far, s=s: far.at[s - 1],
-                    at.device(z=t),
+                    at.device(z=at.flip_z(s & -s)),
                 )
         slot = lambda i=i: outs[i].at[mine]
         stores.append(Local(net, lambda own=own: own.at[0, mine], slot))
@@ -483,36 +497,33 @@
                     at.device(x=x, k=k),
                 )
     count = len(parts)
-    spans = list(range(1, at.depth)) + [0]
-    for i in range(count):
-        for s in spans:
+    spans = halvings(at.depth)
+    for s in spans:
+        for i in range(count):
             across[i, s].start()
             loads[i, s].start()
-    for i in range(count):
-        own, core = buffers[i]["own"], buffers[i]["core"]
-        for s in spans:
+    for s in spans:
+        for i in range(count):
             yield
+            own, core, far = buffers[i]["own"], buffers[i]["core"], buffers[i]["far"]
             loads[i, s].wait()
             across[i, s].got()
+            others = merging(s, at.depth)
+            for other in others:
+                beyond[i, other].got()
+            for member in range(members):
+                add_all(
+                    own.at[s, member],
+                    [own.at[s, member], core.at[s, member]]
+                    + [far.at[other - 1, member] for other in others],
+                )
             if s > 0:
-                for member in range(members):
-                    add_rows(own.at[s, member], own.at[s, member], core.at[s, member])
                 beyond[i, s].start()
-    for i in range(count):
-        yield
-        own, core, far = buffers[i]["own"], buffers[i]["core"], buffers[i]["far"]
-        for s in spans[:-1]:
-            beyond[i, s].got()
-        for member in range(members):
-            add_all(
-                own.at[0, member],
-                [own.at[0, member], core.at[0, member]]
-                + [far.at[s - 1, member] for s in spans[:-1]],
-            )
-        stores[i].start()
-        for (j, step, flip), transfer in swap.items():
-            if j == i:
-                transfer.start()
+                continue
+            stores[i].start()
+            for (j, step, flip), transfer in swap.items():
+                if j == i:
+                    transfer.start()
     yield
     for transfer in swap.values():
         transfer.got()
@@ -739,15 +750,24 @@
     return values.astype(jnp.bfloat16)
 
 
+def gated_grads(gate_value, expand_value, inside_grad):
+    gate, expand = gate_value.astype(jnp.float32), expand_value.astype(jnp.float32)
+    upstream = inside_grad.astype(jnp.float32)
+    slope = float((2.0 / math.pi) ** 0.5)
+    square = gate * gate
+    bend = jnp.tanh(slope * gate * (1.0 + 0.044715 * square))
+    half = 0.5 * (1.0 + bend)
+    rise = half + 0.5 * gate * (1.0 - bend * bend) * slope * (1.0 + 3.0 * 0.044715 * square)
+    return (low(upstream * expand * rise), low(upstream * gate * half))
+
+
 def feed_forward(normed_rows, cotangent, gate_weight, expand_weight, down_weight):
     gate_value = multiply(normed_rows, gate_weight)
     expand_value = multiply(normed_rows, expand_weight)
-    inside, pullback = jax.vjp(gated, gate_value, expand_value)
-    inside_low = low(inside)
+    inside_low = low(gated(gate_value, expand_value))
     part = low(against(inside_low, down_weight))
     inside_grad = multiply(cotangent, down_weight)
-    gate_grad, expand_grad = pullback(inside_grad)
-    gate_low, expand_low = low(gate_grad), low(expand_grad)
+    gate_low, expand_low = gated_grads(gate_value, expand_value, inside_grad)
     normed_grad = low(against(gate_low, gate_weight) + against(expand_low, expand_weight))
     weight_grads = (
         outer_sum(normed_rows, gate_low),
@@ -850,73 +870,82 @@
     ratio = lead_slice // tail_slice
     strip = tail_block // ratio
     packed = tail_slice % 128 == 0 and strip % 16 == 0
-    high = 3 * lead_block + (3 * strip if packed else 0)
-    cut_shapes = [shape_of((high, lead_slice))] * depth
-    if not packed:
-        cut_shapes += [shape_of((3, tail_block, tail_slice))] * depth
+    upper = shape_of((2 * lead_block + (3 * strip if packed else 0), lead_slice))
+    lower = shape_of((lead_block, lead_slice))
 
     def strips(i, start):
         return [(start + i * strip, j * tail_slice, j * strip) for j in range(ratio)]
 
-    def cut_moves(at, ins, held, outs):
-        lists = []
+    def cut(net, at, ins, outs, held):
+        loads, stores = [], []
         for step in range(depth):
             z = at.later_z(step)
             columns = pl.ds(pl.multiple_of(z * lead_slice, lead_slice), lead_slice)
-            loads = [
-                (ins[i].at[:, columns], held[step].at[pl.ds(i * lead_block, lead_block), :])
-                for i in range(3)
+            high, down = held[step], held[depth + step]
+            pairs = [
+                (ins[i].at[:, columns], high.at[pl.ds(i * lead_block, lead_block), :])
+                for i in range(2)
             ]
             if packed:
                 narrow = pl.ds(pl.multiple_of(z * tail_slice, tail_slice), tail_slice)
-                loads += [
+                pairs += [
                     (
                         ins[3 + i].at[pl.ds(place, strip), narrow],
-                        held[step].at[pl.ds(row, strip), pl.ds(column, tail_slice)],
+                        high.at[pl.ds(row, strip), pl.ds(column, tail_slice)],
                     )
                     for i in range(3)
-                    for row, column, place in strips(i, 3 * lead_block)
+                    for row, column, place in strips(i, 2 * lead_block)
                 ]
-            lists.append((loads, [(held[step], outs[step])]))
-        return lists
+            pairs.append((ins[2].at[:, columns], down))
+            for source, target in pairs:
+                loads.append(Local(net, lambda source=source: source, lambda target=target: target))
+            for i in (step, depth + step):
+                stores.append(Local(net, lambda i=i: held[i], lambda i=i: outs[i]))
+        for load in loads:
+            load.start()
+        yield
+        yield
+        for load in loads:
+            load.wait()
+        for store in stores:
+            store.start()
+        for _ in range(8):
+            yield
+        for store in stores:
+            store.wait()
 
     lead_weights = [prefix_gate, prefix_expand, prefix_down]
     tail_weights = [action_gate, action_expand, action_down]
-    cuts = list(
-        shuffle(
-            "cut",
-            sizes,
-            lead_weights + (tail_weights if packed else []),
-            cut_shapes[:depth],
-            cut_shapes[:depth],
-            cut_moves,
-            3 + 3 * ratio if packed else 3,
+    cut_inputs = lead_weights + (tail_weights if packed else [])
+    groups = 2 if packed else 3
+    tails_cut = [
+        jnp.stack(
+            [
+                lax.dynamic_slice_in_dim(
+                    weight, lax.rem(floor + step, depth) * tail_slice, tail_slice, 1
+                )
+                for weight in tail_weights
+            ]
         )
-    )
-    if not packed:
-        cuts += [
-            jnp.stack(
-                [
-                    lax.dynamic_slice_in_dim(
-                        weight, lax.rem(floor + step, depth) * tail_slice, tail_slice, 1
-                    )
-                    for weight in tail_weights
-                ]
-            )
-            for step in range(depth)
-        ]
-    groups = len(cuts) // depth
+        for step in range(0 if packed else depth)
+    ]
     dealt, mirrored = {}, {}
 
-    def mirror(step):
-        for group in range(groups):
+    def deal(group, cuts):
+        for step, block in enumerate(cuts):
+            dealt[group, step] = permute(block, depth, step, False) if step > 0 else block
+
+    def mirror(kinds, step):
+        for group in kinds:
             mirrored[group, step] = permute(dealt[group, step], depth, 0, True)
 
-    def tied(arrays, steps):
-        keys = [(group, step) for group in range(groups) for step in steps]
+    def tied(arrays, kinds, step):
+        keys = [(group, step) for group in kinds]
         arrays, blocks = lax.optimization_barrier((arrays, [dealt[key] for key in keys]))
         dealt.update(zip(keys, blocks))
         return arrays
+
+    soon = [0] if packed else [0, 2]
 
     lead_float = prefix_tokens.astype(jnp.float32)
     tail_float = action_tokens.astype(jnp.float32)
@@ -938,27 +967,33 @@
         next(idents),
         sizes,
         ("z", "y", "cam"),
-        [(array, True) for array in first],
+        [(array, True) for array in first] + [(weight, False) for weight in cut_inputs],
         [(shape_of((breadth, 2) + array.shape), False) for array in first[:2]]
         + [fanned(pack) for pack in packs]
-        + [gathered(shard) for shard in shards],
-        [],
+        + [gathered(shard) for shard in shards]
+        + [(upper, False)] * depth
+        + [(lower, False)] * depth,
+        [pltpu.VMEM(upper.shape, upper.dtype)] * depth
+        + [pltpu.VMEM(lower.shape, lower.dtype)] * depth,
         lambda net, at, ins, outs, held: [
             fan(net, at, ins[2:4], outs[2:4]),
             spread(net, at, ins[:2], outs[:2], False),
             fan(net, at, ins[4:6], outs[4:6]),
-            spread(net, at, ins[6:], outs[6:], True),
+            spread(net, at, ins[6:8], outs[6:8], True),
+            cut(net, at, ins[8:], outs[8:], held),
         ],
     )
-    started, cuts = lax.optimization_barrier((started, cuts))
-    for group in range(groups):
-        for step in range(depth):
-            cut = cuts[group * depth + step]
-            dealt[group, step] = permute(cut, depth, step, False) if step > 0 else cut
+    started, tails_cut = lax.optimization_barrier((started, tails_cut))
+    started, high_cuts, low_cuts = started[:8], started[8 : 8 + depth], started[8 + depth :]
+    deal(0, high_cuts)
+    if not packed:
+        deal(2, tails_cut)
+    dealt[1, 0] = low_cuts[0]
     lead_normed, tail_normed, lead_in, tail_in, lead_mix, tail_mix, *uppers = started
     lead_upper, tail_upper = [array.reshape(-1, array.shape[-1]) for array in uppers]
     lead_mix, tail_mix = lead_mix.reshape(lead_width, width), tail_mix.reshape(tail_width, width)
-    mirror(0)
+    mirror(soon, 0)
+    mirror([1], 0)
     lead_normed = lead_normed.reshape(-1, lead_width)
     tail_normed = tail_normed.reshape(-1, tail_width)
     lead_in = lead_in.reshape(lead_width, -1)
@@ -997,8 +1032,8 @@
             cam_blocks(against(mixed[lead_total:], tail_mix)),
         ],
     )
-    lead_sum, tail_sum = tied([lead_sum, tail_sum], [1])
-    mirror(1)
+    lead_sum, tail_sum = tied([lead_sum, tail_sum], soon, 1)
+    mirror(soon, 1)
     lead_hidden = lead_float + lead_sum
     tail_hidden = tail_float + tail_sum
     lead_center, lead_factor = norm_forward(lead_hidden)
@@ -1007,54 +1042,51 @@
     tail_second = low(tail_center * action_midnorm)
 
     for step in range(2, depth):
-        lead_second, tail_second = tied([lead_second, tail_second], [step])
-        mirror(step)
-
-    def place_moves(at, ins, held, outs):
-        lists = []
-        for number, (group, step, flip) in enumerate(marks):
-            z = at.later_z((depth - step) % depth)
-            y = 1 - at.y if flip else at.y
-            block = held[number]
-            stores = []
-            if group == 0:
-                stores += [
-                    (block.at[pl.ds(i * lead_block, lead_block), :], outs[i].at[z, y])
-                    for i in range(3)
-                ]
-                if packed:
+        lead_second, tail_second = tied([lead_second, tail_second], soon, step)
+        mirror(soon, step)
+
+    def placed(label, kinds, firsts, outs):
+        marks = [
+            (group, step, flip) for group in kinds for step in range(depth) for flip in (0, 1)
+        ]
+        blocks = [(mirrored if flip else dealt)[group, step] for group, step, flip in marks]
+
+        def moves(at, ins, held, targets):
+            lists = []
+            for number, (group, step, flip) in enumerate(marks):
+                z = at.later_z((depth - step) % depth)
+                y = 1 - at.y if flip else at.y
+                block, slot = held[number], firsts[group]
+                if group == 2:
+                    stores = [(block.at[i], targets[slot + i].at[z, y]) for i in range(3)]
+                else:
+                    stores = [
+                        (
+                            block.at[pl.ds(i * lead_block, lead_block), :],
+                            targets[slot + i].at[z, y],
+                        )
+                        for i in range(1 if group == 1 else 2)
+                    ]
+                if group == 0 and packed:
                     stores += [
                         (
                             block.at[pl.ds(row, strip), pl.ds(column, tail_slice)],
-                            outs[3 + i].at[z, y, pl.ds(place, strip), :],
+                            targets[2 + i].at[z, y, pl.ds(place, strip), :],
                         )
                         for i in range(3)
-                        for row, column, place in strips(i, 3 * lead_block)
+                        for row, column, place in strips(i, 2 * lead_block)
                     ]
-            else:
-                stores += [(block.at[i], outs[3 + i].at[z, y]) for i in range(3)]
-            lists.append(([(ins[number], block)], stores))
-        return lists
-
-    marks = [
-        (group, step, flip) for group in range(groups) for step in range(depth) for flip in (0, 1)
-    ]
-    blocks = [
-        (mirrored if flip else dealt)[group, step] for group, step, flip in marks
-    ]
-    lead_gate, lead_expand, lead_down, tail_gate, tail_expand, tail_down = [
-        weight.reshape(-1, weight.shape[-1])
-        for weight in shuffle(
-            "place",
-            sizes,
-            blocks,
-            blocks,
-            [shape_of((depth, 2, lead_block, lead_slice))] * 3
-            + [shape_of((depth, 2, tail_block, tail_slice))] * 3,
-            place_moves,
-            3 + 3 * ratio if packed else 3,
-        )
-    ]
+                lists.append(([(ins[number], block)], stores))
+            return lists
+
+        most = 3 + 3 * ratio if packed else 3
+        return [
+            weight.reshape(-1, weight.shape[-1])
+            for weight in shuffle(label, sizes, blocks, blocks, outs, moves, most)
+        ]
+
+    lead_out_shape = shape_of((depth, 2, lead_block, lead_slice))
+    tail_out_shape = shape_of((depth, 2, tail_block, tail_slice))
 
     def send_across(packs):
         sent = []
@@ -1073,15 +1105,20 @@
                 sent.append((own, other))
         return sent
 
-    def pass_on(pairs):
+    def summed_blocks(pairs):
         summed = jnp.concatenate(
             [low(own.astype(jnp.float32) + other.astype(jnp.float32)) for own, other in pairs], 1
         )
-        blocks = []
-        for step in range(depth):
-            block = lax.dynamic_index_in_dim(summed, lax.rem(floor + step, depth), 0, False)
-            blocks.append(permute(block, depth, step, False) if step > 0 else block)
-        return blocks
+        return [
+            lax.dynamic_index_in_dim(summed, lax.rem(floor + step, depth), 0, False)
+            for step in range(depth)
+        ]
+
+    def pass_on(pairs):
+        blocks = summed_blocks(pairs)
+        return blocks[:1] + [
+            permute(block, depth, step + 1, False) for step, block in enumerate(blocks[1:])
+        ]
 
     shards = [lead_second, tail_second]
     lead_all, tail_all = [
@@ -1097,30 +1134,52 @@
             lambda net, at, ins, outs, held: [spread(net, at, ins, outs, True)],
         )
     ]
+    (lead_all, tail_all), low_cuts = lax.optimization_barrier(((lead_all, tail_all), low_cuts))
+    dealt_here = dealt[1, 0]
+    deal(1, low_cuts)
+    dealt[1, 0] = dealt_here
+    lead_gate, lead_expand, tail_gate, tail_expand, tail_down = placed(
+        "upper", soon, {0: 0, 2: 2}, [lead_out_shape] * 2 + [tail_out_shape] * 3
+    )
     tail_out, tail_back, tail_ffgrads = feed_forward(
         tail_all, tail_upper, tail_gate, tail_expand, tail_down
     )
-    gate_value = multiply(lead_all, lead_gate)
-    expand_value = multiply(lead_all, lead_expand)
-    inside, pullback = jax.vjp(gated, gate_value, expand_value)
-    inside_low = low(inside)
+    (lead_all, tail_out, tail_back), tail_ffgrads = lax.optimization_barrier(
+        ((lead_all, tail_out, tail_back), [low(grad) for grad in tail_ffgrads])
+    )
+    lead_all = tied(lead_all, [1], 1)
+    mirror([1], 1)
+    gate_value = low(multiply(lead_all, lead_gate))
+    gate_value, lead_all = tied((gate_value, lead_all), [1], 2)
+    mirror([1], 2)
+    expand_value = low(multiply(lead_all, lead_expand))
+    for step in range(3, depth):
+        gate_value, expand_value = tied((gate_value, expand_value), [1], step)
+        mirror([1], step)
+    inside_low = low(gated(gate_value.astype(jnp.float32), expand_value.astype(jnp.float32)))
     down_grad = low(outer_sum(lead_upper, inside_low))
     down_grad, lead_upper = lax.optimization_barrier((down_grad, lead_upper))
-    returns = send_across([[down_grad] + list(tail_ffgrads)])
-    inside_grad = multiply(lead_upper, lead_down)
-    gate_grad, expand_grad = pullback(inside_grad)
-    gate_low, expand_low = low(gate_grad), low(expand_grad)
+    returns = send_across([[down_grad] + tail_ffgrads])
+    (lead_down,) = placed("lower", [1], {1: 0}, [lead_out_shape])
+    inside_grad = low(multiply(lead_upper, lead_down))
+    gate_low, expand_low = gated_grads(gate_value, expand_value, inside_grad)
     returns += send_across(
         [[outer_sum(lead_all, gate_low)], [outer_sum(lead_all, expand_low)]]
     )
-    lead_out = low(against(inside_low, lead_down))
+    others = [other for _, other in returns[-2:]]
+    sources = [own for own, _ in returns[-2:]]
+    (inside_low, gate_low, expand_low), sources = lax.optimization_barrier(
+        ((inside_low, gate_low, expand_low), sources)
+    )
+    returns[-2:] = list(zip(sources, others))
     lead_back = low(against(gate_low, lead_gate) + against(expand_low, lead_expand))
-    (lead_out, lead_back), returns[:-2] = lax.optimization_barrier(
-        ((lead_out, lead_back), returns[:-2])
+    (inside_low, lead_back), returns[:-2] = lax.optimization_barrier(
+        ((inside_low, lead_back), returns[:-2])
     )
     blocks_back = [pass_on(returns[:1])]
     if not packed:
         blocks_back.append(pass_on(returns[1:2]))
+    lead_out = low(against(inside_low, lead_down))
 
     def token_blocks(rows):
         return rows.reshape(depth, breadth, 2, -1, rows.shape[1])
@@ -1157,7 +1216,26 @@
     (lead_summed, tail_summed), rest, blocks_back = lax.optimization_barrier(
         ((lead_summed, tail_summed), returns[-2:], blocks_back)
     )
-    blocks_back.insert(1, pass_on(rest))
+    back_blocks = {}
+    for i, both in enumerate(rest):
+        back_blocks.update({(i, s): block for s, block in enumerate(summed_blocks([both]))})
+    leaving = [(i, s) for s in [1] + list(range(3, depth)) + [2] for i in (0, 1)]
+    stops = [0, len(leaving) // 3, len(leaving) * 2 // 3, len(leaving)]
+    turns = [leaving[stops[i] : stops[i + 1]] for i in range(3)]
+
+    def leave(turn):
+        for i, s in turns[turn]:
+            back_blocks[i, s] = permute(back_blocks[i, s], depth, s, False)
+
+    def back_tied(arrays, turn):
+        marks = turns[turn] + (turns[turn + 1] if turn < 2 else [])
+        arrays, pieces = lax.optimization_barrier((arrays, [back_blocks[mark] for mark in marks]))
+        back_blocks.update(zip(marks, pieces))
+        if turn < 2:
+            leave(turn + 1)
+        return arrays
+
+    leave(0)
     lead_residual, lead_middle = norm_backward(
         lead_summed, lead_center, lead_factor, prefix_midnorm
     )
@@ -1167,6 +1245,7 @@
     lead_upstream = prefix_cotangent.astype(jnp.float32) + lead_residual
     tail_upstream = action_cotangent.astype(jnp.float32) + tail_residual
     lead_sent, tail_sent = cam_spread("sent", [low(lead_upstream), low(tail_upstream)])
+    lead_sent, tail_sent = back_tied((lead_sent, tail_sent), 0)
     lead_sent = lead_sent.reshape(-1, lead_width)
     tail_sent = tail_sent.reshape(-1, tail_width)
     lead_mixing = outer_sum(lead_sent, mixed[:lead_total])
@@ -1186,19 +1265,21 @@
         jnp.einsum("hqk,kd->qhd", score_grad, keys, preferred_element_type=jnp.float32) * inverse
     )
     pair_parts = low(jnp.concatenate([key_grad, value_grad], 1)).reshape(-1, members, pair)
+    pair_parts, query_low, lead_mixing, tail_mixing = lax.optimization_barrier(
+        (pair_parts, low(query_grad.reshape(-1, width)), low(lead_mixing), low(tail_mixing))
+    )
     (pair_grad,) = cam_collect(
         "pair_grads", [jnp.swapaxes(pair_parts, 0, 1).reshape(breadth, 2, -1, pair)]
     )
-    low_grad = jnp.concatenate([low(query_grad.reshape(-1, width)), low(pair_grad)], 1)
+    pair_grad = back_tied(pair_grad, 1)
+    low_grad = jnp.concatenate([query_low, low(pair_grad)], 1)
     lead_part, tail_part = low_grad[:lead_total], low_grad[lead_total:]
     lead_back, tail_back = cam_collect(
         "backs",
         [cam_blocks(against(lead_part, lead_in)), cam_blocks(against(tail_part, tail_in))],
     )
-    (lead_back, tail_back, low_grad, lead_mixing, tail_mixing), blocks_back = (
-        lax.optimization_barrier(
-            ((lead_back, tail_back, low_grad, lead_mixing, tail_mixing), blocks_back)
-        )
+    (lead_back, tail_back, low_grad, lead_mixing, tail_mixing) = back_tied(
+        (lead_back, tail_back, low_grad, lead_mixing, tail_mixing), 2
     )
     lead_part, tail_part = low_grad[:lead_total], low_grad[lead_total:]
     lead_back, lead_first = norm_backward(lead_back, lead_unit, lead_scale, prefix_prenorm)
@@ -1274,15 +1355,16 @@
                 parts.append((step, step, 3 + i, tail_slice, pieces))
             else:
                 pieces = [(i * tail_block, 0, tail_block, 0)]
-                parts.append((2 * depth + step, step, 3 + i, tail_slice, pieces))
-    for step in range(depth):
-        for i in range(2):
-            pieces = [(i * lead_block, 0, lead_block, 0)]
-            parts.append((depth + step, step, i, lead_slice, pieces))
+                parts.append((3 * depth + step, step, 3 + i, tail_slice, pieces))
+    for i in range(2):
+        for step in range(depth):
+            parts.append(((1 + i) * depth + step, step, i, lead_slice, whole_block))
     ff_grads = widen(
         "returns",
         sizes,
-        sum(blocks_back, []),
+        blocks_back[0]
+        + [back_blocks[i, s] for i in (0, 1) for s in range(depth)]
+        + sum(blocks_back[1:], []),
         [shape_of(weight.shape, jnp.float32) for weight in lead_weights]
         + [
             shape_of(

time: 1040 us -> 873 us (0.84)
  waiting for transfers between devices: 143 us -> 44.9 us
  Pallas kernels: 599 us -> 540 us
    ppermute x16 -> x26, waiting for transfers between devices: 143 us -> 44.9 us  [permute(): return lax.ppermute(array, 'rows', pairs)]
    pallas_call x9, Pallas kernels: 569 us -> 514 us  [exchange(): pl.pallas_call(kernel, name=label, out_shape=[shape for shape, _ in outpu...]
    ppermute x16 -> x26, starting transfers between devices: 52 us -> 44.8 us  [permute(): return lax.ppermute(array, 'rows', pairs)]
    convert_element_type x12 -> x13, other arithmetic: 17.3 us -> 21.8 us  [low(): return values.astype(jnp.bfloat16)]
  transfers between devices with their start and end apart: 16 -> 26, of which waited for: 6 -> 5; matrix products, arithmetic and copies ran while one was open for 8% -> 21% of each run, Pallas kernels for 25% -> 32%
where the time goes in v3:
time: 873 us; the launch traced here: 868 us
  Pallas kernels  540 us (62%)
  matrix products  165 us (19%)
  waiting for transfers between devices  44.9 us (5%)
  starting transfers between devices  44.8 us (5%)
  other arithmetic  40.5 us (5%)
  local copies, waits for them, and re-layouts  30.6 us (4%)
    pallas_call x9, Pallas kernels, exchange(): pl.pallas_call(kernel, name=label, out_shape=[shape for shape, _ in outpu...  514 us
    dot_general x10, matrix products, multiply(): return jnp.dot(operand, matrix, preferred_element_type=jnp.float32)  57.1 us
    dot_general x10, matrix products, against(): lax.dot_general(operand, matrix, (((1,), (1,)), ((), ())), preferred_elem...  54.5 us
    dot_general x10, matrix products, outer_sum(): lax.dot_general(operand, matrix, (((0,), (0,)), ((), ())), preferred_elem...  47 us
    ppermute x26, waiting for transfers between devices, permute(): return lax.ppermute(array, 'rows', pairs)  44.9 us
    ppermute x26, starting transfers between devices, permute(): return lax.ppermute(array, 'rows', pairs)  44.8 us
    convert_element_type x13, other arithmetic, low(): return values.astype(jnp.bfloat16)  21.8 us
  transfers between devices with their start and end apart: 26, of which 5 were waited for; matrix products, arithmetic and copies ran while one was open for 21% of the time, Pallas kernels for 32%

profile of v3, /device:TPU:0, one launch (start us, length us, event | category | flops | bytes accessed | tf_op | source)
XLA Modules:
  0.0 868.4 jit_solution(4973023586934101571)
XLA Ops:
  13.4 122.9 %first.1 = (bf16[2,2,128,2048]{3,2,1,0:T(8,128)(2,1)}, bf16[2,2,16,1024]{3,2,1,0:T(8,128)(2,1)}, bf16[4,2,4,64,640]{4,3,2,1,0:T(8,128)(2,1)}, bf16[4,2,4,32,640]...) custom-call(bf16[128,2048]{1,0:T(8,128)(2,1)} %fusion.46.refs_0_, ...), custom_call_target="tpu_custom_call" | custom-call | bytes 3000000 | tf_op jit(solution)/shard_map/first/pallas_call | solution.py:586
  142.7 4.2 convolution_convert_fusion.13
  147.6 13.0 %pairs.1 = bf16[2,2,576,128]{3,2,1,0:T(8,128)(2,1)} custom-call(bf16[576,128]{1,0:T(8,128)(2,1)} %pad_maximum_fusion.9.refs_0_), custom_call_target="tpu_custom_call" | custom-call | bytes 3000000 | tf_op jit(solution)/shard_map/pairs/pallas_call | solution.py:586
  169.7 4.4 convolution_convert_fusion.9
  174.1 22.4 %mixing.1 = (f32[128,2048]{1,0:T(8,128)}, f32[16,1024]{1,0:T(8,128)}) custom-call(bf16[2,2,128,2048]{3,2,1,0:T(8,128)(2,1)} %bitcast.353, bf16[2,2,16,1024]{3,2,1,0:T(8,128)(2,1)} %bitcast.382), custom_call_target="tpu_custom_call" | custom-call | bytes 3000000 | tf_op jit(solution)/shard_map/mixing/pallas_call | solution.py:586
  201.8 19.6 %collective-permute-done.1.refs_4_ = bf16[608,1024]{1,0:T(8,128)(2,1)} collective-permute-done((bf16[608,1024]{1,0:T(8,128)(2,1)}, bf16[608,1024]{1,0:T(8,128)(2,1)}, u32[]{:S(2)}, u32[]{:S(2)}) %collective-permute-start.1) | collective-permute-done | bytes 1245216 | tf_op jit(solution)/shard_map/ppermute | solution.py:612
  225.5 85.2 %gather.1 = (bf16[4,2,2,128,2048]{4,3,2,1,0:T(8,128)(2,1)}, bf16[4,2,2,16,1024]{4,3,2,1,0:T(8,128)(2,1)}) custom-call(bf16[128,2048]{1,0:T(8,128)(2,1)} %multiply_convert_fusion.refs_0_, bf16[16,1024]{1,0:T(8,128)(2,1)} %multiply_convert_fusion.2.refs_1_), custom_call_target="tpu_custom_call" | custom-call | bytes 3000000 | tf_op jit(solution)/shard_map/gather/pallas_call | solution.py:586
  315.6 9.7 %upper.1 = (bf16[4,2,256,1024]{3,2,1,0:T(8,128)(2,1)}, bf16[4,2,256,1024]{3,2,1,0:T(8,128)(2,1)}, bf16[4,2,128,256]{3,2,1,0:T(8,128)(2,1)}, bf16[4,2,128,256]{3,2,1,0:T(8,128)(2,1)}, bf16[4,2,128,256]{3,2,1,0:T(8,128)(2,1)}) custom-call(bf16[608,1024]{1,0:T(8,128)(2,1)} %get-tuple-element.162.refs_0_, bf16[608,1024]{1,0:T(8,128)(2,1)} %collective-permute-done.3.refs_1_, ...), custom_call_target="tpu_custom_call" | custom-call | bytes 19922944 | tf_op jit(solution)/shard_map/upper/pallas_call | solution.py:640
  334.0 11.1 %convolution_convert_fusion.3 = bf16[2048,1024]{1,0:T(8,128)(2,1)S(1)} fusion(bf16[2048,2048]{1,0:T(8,128)(2,1)S(1)} %bitcast.405, bf16[2048,1024]{1,0:T(8,128)(2,1)} %bitcast.409), kind=kOutput, calls=%fused_computation.37 | convolution fusion | flops 8592031744 | bytes 16777216 | tf_op jit(solution)/shard_map/dot_general | solution.py:714
  345.2 4.2 collective-permute-done.8.refs_4_
  349.9 11.1 %convolution_convert_fusion.2 = bf16[2048,1024]{1,0:T(8,128)(2,1)S(1)} fusion(bf16[2048,2048]{1,0:T(8,128)(2,1)S(1)} %bitcast.408, bf16[2048,1024]{1,0:T(8,128)(2,1)} %bitcast.411), kind=kOutput, calls=%fused_computation.36 | convolution fusion | flops 8592031744 | bytes 16777216 | tf_op jit(solution)/shard_map/dot_general | solution.py:714
  366.4 9.8 %convolution_convert_fusion.6 = bf16[2048,1024]{1,0:T(8,128)(2,1)S(1)} fusion(bf16[2048,2048]{1,0:T(8,128)(2,1)S(1)} %bitcast.402, bf16[2048,1024]{1,0:T(8,128)(2,1)S(1)} %fusion.2), kind=kOutput, calls=%fused_computation.40 | convolution fusion | flops 8592031744 | bytes 16777216 | tf_op jit(solution)/shard_map/dot_general | solution.py:724
  380.5 5.6 lower.1
  386.1 19.2 %fusion.19 = (bf16[2048,1024]{1,0:T(8,128)(2,1)S(1)}, bf16[2048,1024]{1,0:T(8,128)(2,1)S(1)}) fusion(bf16[2048,1024]{1,0:T(8,128)(2,1)} %copy-done.10, bf16[2048,1024]{1,0:T(8,128)(2,1)} %copy-done.11, bf16[2048,2048]{1,0:T(8,128)(2,1)} %bitcast.399, bf16[2048,1024]{1,0:T(8,128)(2,1)} %bitcast.340), kind=kOutput, calls=%fused_computation.29 | convolution fusion | flops 8644460544 | bytes 29360128 | tf_op jit(solution)/shard_map/dot_general | solution.py:714
  405.3 13.0 %convolution_convert_fusion.4 = bf16[2048,1024]{1,0:T(8,128)(2,1)S(1)} fusion(bf16[2048,2048]{1,0:T(8,128)(2,1)} %bitcast.403, bf16[2048,1024]{1,0:T(8,128)(2,1)S(1)} %get-tuple-element.188), kind=kOutput, calls=%fused_computation.38 | convolution fusion | flops 8592031744 | bytes 16777216 | tf_op jit(solution)/shard_map/dot_general | solution.py:724
  418.4 11.5 %convolution_convert_fusion.5 = bf16[2048,1024]{1,0:T(8,128)(2,1)S(1)} fusion(bf16[2048,2048]{1,0:T(8,128)(2,1)} %bitcast.404, bf16[2048,1024]{1,0:T(8,128)(2,1)S(1)} %get-tuple-element.187), kind=kOutput, calls=%fused_computation.39 | convolution fusion | flops 8592031744 | bytes 16777216 | tf_op jit(solution)/shard_map/dot_general | solution.py:724
  436.9 12.1 %fusion.115 = f32[2048,2048]{1,0:T(8,128)} fusion(bf16[2048,1024]{1,0:T(8,128)(2,1)S(1)} %get-tuple-element.188, bf16[2048,1024]{1,0:T(8,128)(2,1)S(1)} %bitcast.412), kind=kOutput, calls=%fused_computation.255 | convolution fusion | flops 8589934592 | bytes 25165824 | tf_op jit(solution)/shard_map/dot_general | solution.py:718
  449.0 15.9 %add_convert_fusion = bf16[2048,2048]{1,0:T(8,128)(2,1)} fusion(f32[2048,2048]{1,0:T(8,128)} %fusion.115, bf16[2048,1024]{1,0:T(8,128)(2,1)} %copy-done.80, bf16[2048,1024]{1,0:T(8,128)(2,1)S(1)} %bitcast.410), kind=kOutput, calls=%fused_computation.7 | convolution fusion | flops 8598323200 | bytes 33554432 | tf_op jit(solution)/shard_map/dot_general | solution.py:718
  469.9 12.0 %collective-permute-start.19 = (bf16[352,1024]{1,0:T(8,128)(2,1)}, bf16[352,1024]{1,0:T(8,128)(2,1)S(1)}, u32[]{:S(2)}, u32[]{:S(2)}) collective-permute-start(bf16[352,1024]{1,0:T(8,128)(2,1)} %get-tuple-element.272), channel_id=1, source_target_pairs={{0,24},{4,28},{8,0},{12,4},{16,8},{20,12},{24,16},{28,20},{1,25},{... | collective-permute-start | bytes 2162696 | tf_op jit(solution)/shard_map/ppermute | solution.py:612
  485.1 11.1 %convolution_convert_fusion = bf16[2048,2048]{1,0:T(8,128)(2,1)} fusion(bf16[2048,1024]{1,0:T(8,128)(2,1)S(1)} %copy-done.9, bf16[2048,1024]{1,0:T(8,128)(2,1)S(1)} %bitcast.341), kind=kOutput, calls=%fused_computation.31 | convolution fusion | flops 8594128896 | bytes 16777216 | tf_op jit(solution)/shard_map/dot_general | solution.py:718
  496.2 85.9 %collect.1 = (f32[128,2048]{1,0:T(8,128)}, f32[16,1024]{1,0:T(8,128)}) custom-call(bf16[4,2,2,128,2048]{4,3,2,1,0:T(8,128)(2,1)} %bitcast.325, bf16[4,2,2,16,1024]{4,3,2,1,0:T(8,128)(2,1)} %bitcast.350), custom_call_target="tpu_custom_call" | custom-call | bytes 3000000 | tf_op jit(solution)/shard_map/collect/pallas_call | solution.py:586
  599.2 21.9 %sent.1 = (bf16[2,2,128,2048]{3,2,1,0:T(8,128)(2,1)}, bf16[2,2,16,1024]{3,2,1,0:T(8,128)(2,1)}) custom-call(bf16[128,2048]{1,0:T(8,128)(2,1)} %fusion.101.refs_0_, bf16[16,1024]{1,0:T(8,128)(2,1)} %fusion.98.refs_1_), custom_call_target="tpu_custom_call" | custom-call | bytes 3000000 | tf_op jit(solution)/shard_map/sent/pallas_call | solution.py:586
  625.3 3.6 fusion.116
  642.0 13.3 %pair_grads.1 = f32[576,128]{1,0:T(8,128)} custom-call(bf16[2,2,576,128]{3,2,1,0:T(8,128)(2,1)} %bitcast.347), custom_call_target="tpu_custom_call" | custom-call | bytes 3000000 | tf_op jit(solution)/shard_map/pair_grads/pallas_call | solution.py:586
  655.4 5.4 collective-permute-done.23.refs_11_
  667.3 4.9 convolution_convert_fusion.10
  672.1 22.5 %backs.1 = (f32[128,2048]{1,0:T(8,128)}, f32[16,1024]{1,0:T(8,128)}) custom-call(bf16[2,2,128,2048]{3,2,1,0:T(8,128)(2,1)} %bitcast.352, bf16[2,2,16,1024]{3,2,1,0:T(8,128)(2,1)} %bitcast.381), custom_call_target="tpu_custom_call" | custom-call | bytes 3000000 | tf_op jit(solution)/shard_map/backs/pallas_call | solution.py:586
  694.7 5.4 collective-permute-done.24.refs_6_
  700.2 10.2 %collective-permute-done.25.refs_10_ = bf16[256,1024]{1,0:T(8,128)(2,1)} collective-permute-done((bf16[256,1024]{1,0:T(8,128)(2,1)}, bf16[256,1024]{1,0:T(8,128)(2,1)}, u32[]{:S(2)}, u32[]{:S(2)}) %collective-permute-start.25) | collective-permute-done | bytes 524320 | tf_op jit(solution)/shard_map/ppermute | solution.py:612
  710.5 5.1 convolution_convert_fusion.7
  719.6 127.0 %fold.1 = (bf16[4,64,640]{2,1,0:T(8,128)(2,1)}, bf16[4,32,640]{2,1,0:T(8,128)(2,1)}, bf16[4,64,512]{2,1,0:T(8,128)(2,1)}, bf16[4,32,512]{2,1,0:T(8,128)(2,1)}, f...) custom-call(bf16[4,2,4,64,640]{4,3,2,1,0:T(8,128)(2,1)} %bitcast.346, ...), custom_call_target="tpu_custom_call" | custom-call | bytes 3000000 | tf_op jit(solution)/shard_map/fold/pallas_call | solution.py:586
  857.6 10.5 %returns.1 = (f32[256,4096]{1,0:T(8,128)}, f32[256,4096]{1,0:T(8,128)}, f32[256,4096]{1,0:T(8,128)}, f32[128,1024]{1,0:T(8,128)}, f32[128,1024]{1,0:T(8,128)}, /*index=5*/f32[128,1024]{1,0:T(8,128)}) custom-call(bf16[352,1024]{1,0:T(8,128)(2,1)} %get-tuple-element.236.refs_0_, bf16[352,1024]{1,0:T(8,128)(2,1)} %collective-permute-done.17.refs_1_, ...), custom_call_target="tpu_custom_call" | custom-call | bytes 21233664 | tf_op jit(solution)/shard_map/returns/pallas_call | solution.py:695
  (335 shorter events, 132.2 us)
Async XLA Ops:
  136.4 60.2 %collective-permute-start = (bf16[608,1024]{1,0:T(8,128)(2,1)}, bf16[608,1024]{1,0:T(8,128)(2,1)S(1)}, u32[]{:S(2)}, u32[]{:S(2)}) collective-permute-start(bf16[608,1024]{1,0:T(8,128)(2,1)} %get-tuple-element.145), channel_id=1, source_target_pairs={{0,8},{4,12},{8,16},{12,20},{16,24},{20,28},{24,0},{28,4},{1,9},{5... | collective-permute-start | bytes 3735560 | tf_op jit(solution)/shard_map/ppermute | solution.py:612
  136.4 84.9 %collective-permute-start.1 = (bf16[608,1024]{1,0:T(8,128)(2,1)}, bf16[608,1024]{1,0:T(8,128)(2,1)}, u32[]{:S(2)}, u32[]{:S(2)}) collective-permute-start(bf16[608,1024]{1,0:T(8,128)(2,1)} %get-tuple-element.148), channel_id=1, source_target_pairs={{0,16},{4,20},{8,24},{12,28},{16,0},{20,4},{24,8},{28,12},{1,17},{... | collective-permute-start | bytes 3735560 | tf_op jit(solution)/shard_map/ppermute | solution.py:612
  138.3 83.1 %collective-permute-start.2 = (bf16[608,1024]{1,0:T(8,128)(2,1)}, bf16[608,1024]{1,0:T(8,128)(2,1)}, u32[]{:S(2)}, u32[]{:S(2)}) collective-permute-start(bf16[608,1024]{1,0:T(8,128)(2,1)} %get-tuple-element.151), channel_id=1, source_target_pairs={{0,24},{4,28},{8,0},{12,4},{16,8},{20,12},{24,16},{28,20},{1,25},{... | collective-permute-start | bytes 3735560 | tf_op jit(solution)/shard_map/ppermute | solution.py:612
  140.4 170.3 %collective-permute-start.3 = (bf16[608,1024]{1,0:T(8,128)(2,1)}, bf16[608,1024]{1,0:T(8,128)(2,1)}, u32[]{:S(2)}, u32[]{:S(2)}) collective-permute-start(bf16[608,1024]{1,0:T(8,128)(2,1)} %get-tuple-element.162.refs_0_), channel_id=1, source_target_pairs={{0,4},{4,0},{8,12},{12,8},{16,20},{20,16},{24,28},{28,24},{1,5},{5... | collective-permute-start | bytes 3735560 | tf_op jit(solution)/shard_map/ppermute | solution.py:612
  174.1 26.1 %copy-start.56 = (f32[1024]{0:T(1024)S(1)}, f32[1024]{0:T(1024)}, u32[]{:S(2)}) copy-start(f32[1024]{0:T(1024)} %param.41) | copy-start | bytes 12292
  174.1 26.8 %copy-start.51 = (f32[2048]{0:T(1024)S(1)}, f32[2048]{0:T(1024)}, u32[]{:S(2)}) copy-start(f32[2048]{0:T(1024)} %param.39) | copy-start | bytes 24580
  196.5 119.0 %copy-start.25 = (bf16[608,1024]{1,0:T(8,128)(2,1)}, bf16[608,1024]{1,0:T(8,128)(2,1)S(1)}, u32[]{:S(2)}) copy-start(bf16[608,1024]{1,0:T(8,128)(2,1)S(1)} %collective-permute-done.refs_2_) | copy-start | bytes 3735556
  221.4 89.4 %collective-permute-start.6 = (bf16[608,1024]{1,0:T(8,128)(2,1)}, bf16[608,1024]{1,0:T(8,128)(2,1)S(1)}, u32[]{:S(2)}, u32[]{:S(2)}) collective-permute-start(bf16[608,1024]{1,0:T(8,128)(2,1)} %collective-permute-done.2.refs_6_), channel_id=1, source_target_pairs={{0,4},{4,0},{8,12},{12,8},{16,20},{20,16},{24,28},{28,24},{1,5},{5... | collective-permute-start | bytes 3735560 | tf_op jit(solution)/shard_map/ppermute | solution.py:612
  222.0 91.4 %collective-permute-start.5 = (bf16[608,1024]{1,0:T(8,128)(2,1)}, bf16[608,1024]{1,0:T(8,128)(2,1)}, u32[]{:S(2)}, u32[]{:S(2)}) collective-permute-start(bf16[608,1024]{1,0:T(8,128)(2,1)} %collective-permute-done.1.refs_4_), channel_id=1, source_target_pairs={{0,4},{4,0},{8,12},{12,8},{16,20},{20,16},{24,28},{28,24},{1,5},{5... | collective-permute-start | bytes 3735560 | tf_op jit(solution)/shard_map/ppermute | solution.py:612
  223.5 92.1 %collective-permute-start.4 = (bf16[608,1024]{1,0:T(8,128)(2,1)S(1)}, bf16[608,1024]{1,0:T(8,128)(2,1)}, u32[]{:S(2)}, u32[]{:S(2)}) collective-permute-start(bf16[608,1024]{1,0:T(8,128)(2,1)S(1)} %collective-permute-done.refs_2_), channel_id=1, source_target_pairs={{0,4},{4,0},{8,12},{12,8},{16,20},{20,16},{24,28},{28,24},{1,5},{5... | collective-permute-start | bytes 3735560 | tf_op jit(solution)/shard_map/ppermute | solution.py:612
  224.0 155.5 %collective-permute-start.10 = (bf16[256,1024]{1,0:T(8,128)(2,1)}, bf16[256,1024]{1,0:T(8,128)(2,1)}, u32[]{:S(2)}, u32[]{:S(2)}) collective-permute-start(bf16[256,1024]{1,0:T(8,128)(2,1)} %get-tuple-element.156.refs_0_), channel_id=1, source_target_pairs={{0,4},{4,0},{8,12},{12,8},{16,20},{20,16},{24,28},{28,24},{1,5},{5... | collective-permute-start | bytes 1572872 | tf_op jit(solution)/shard_map/ppermute | solution.py:612
  310.7 22.8 %collective-permute-start.7 = (bf16[256,1024]{1,0:T(8,128)(2,1)}, bf16[256,1024]{1,0:T(8,128)(2,1)}, u32[]{:S(2)}, u32[]{:S(2)}) collective-permute-start(bf16[256,1024]{1,0:T(8,128)(2,1)} %get-tuple-element.171), channel_id=1, source_target_pairs={{0,8},{4,12},{8,16},{12,20},{16,24},{20,28},{24,0},{28,4},{1,9},{5... | collective-permute-start | bytes 1572872 | tf_op jit(solution)/shard_map/ppermute | solution.py:612
  310.8 38.6 %collective-permute-start.8 = (bf16[256,1024]{1,0:T(8,128)(2,1)}, bf16[256,1024]{1,0:T(8,128)(2,1)}, u32[]{:S(2)}, u32[]{:S(2)}) collective-permute-start(bf16[256,1024]{1,0:T(8,128)(2,1)} %get-tuple-element.174), channel_id=1, source_target_pairs={{0,16},{4,20},{8,24},{12,28},{16,0},{20,4},{24,8},{28,12},{1,17},{... | collective-permute-start | bytes 1572872 | tf_op jit(solution)/shard_map/ppermute | solution.py:612
  313.3 47.9 %collective-permute-start.9 = (bf16[256,1024]{1,0:T(8,128)(2,1)}, bf16[256,1024]{1,0:T(8,128)(2,1)}, u32[]{:S(2)}, u32[]{:S(2)}) collective-permute-start(bf16[256,1024]{1,0:T(8,128)(2,1)} %get-tuple-element.178), channel_id=1, source_target_pairs={{0,24},{4,28},{8,0},{12,4},{16,8},{20,12},{24,16},{28,20},{1,25},{... | collective-permute-start | bytes 1572872 | tf_op jit(solution)/shard_map/ppermute | solution.py:612
  333.5 46.0 %collective-permute-start.11 = (bf16[256,1024]{1,0:T(8,128)(2,1)}, bf16[256,1024]{1,0:T(8,128)(2,1)S(1)}, u32[]{:S(2)}, u32[]{:S(2)}) collective-permute-start(bf16[256,1024]{1,0:T(8,128)(2,1)} %collective-permute-done.7.refs_2_), channel_id=1, source_target_pairs={{0,4},{4,0},{8,12},{12,8},{16,20},{20,16},{24,28},{28,24},{1,5},{5... | collective-permute-start | bytes 1572872 | tf_op jit(solution)/shard_map/ppermute | solution.py:612
  334.0 32.3 %slice-start = ((s8[8388608]{0:T(1024)(128)(4,1)}), s8[4194304]{0:T(1024)(128)(4,1)S(1)}, s32[]{:S(2)}) async-start(s8[8388608]{0:T(1024)(128)(4,1)} %bitcast.400), calls=%async_computation | async-start | bytes 8388608
  349.4 30.1 %collective-permute-start.12 = (bf16[256,1024]{1,0:T(8,128)(2,1)}, bf16[256,1024]{1,0:T(8,128)(2,1)S(1)}, u32[]{:S(2)}, u32[]{:S(2)}) collective-permute-start(bf16[256,1024]{1,0:T(8,128)(2,1)} %collective-permute-done.8.refs_4_), channel_id=1, source_target_pairs={{0,4},{4,0},{8,12},{12,8},{16,20},{20,16},{24,28},{28,24},{1,5},{5... | collective-permute-start | bytes 1572872 | tf_op jit(solution)/shard_map/ppermute | solution.py:612
  361.2 18.3 %collective-permute-start.13 = (bf16[256,1024]{1,0:T(8,128)(2,1)}, bf16[256,1024]{1,0:T(8,128)(2,1)}, u32[]{:S(2)}, u32[]{:S(2)}) collective-permute-start(bf16[256,1024]{1,0:T(8,128)(2,1)} %collective-permute-done.9.refs_6_), channel_id=1, source_target_pairs={{0,4},{4,0},{8,12},{12,8},{16,20},{20,16},{24,28},{28,24},{1,5},{5... | collective-permute-start | bytes 1572872 | tf_op jit(solution)/shard_map/ppermute | solution.py:612
  378.7 86.1 %collective-permute-start.14 = (bf16[4,352,1024]{2,1,0:T(8,128)(2,1)}, bf16[4,352,1024]{2,1,0:T(8,128)(2,1)}, u32[]{:S(2)}, u32[]{:S(2)}) collective-permute-start(bf16[4,352,1024]{2,1,0:T(8,128)(2,1)} %pad_maximum_fusion.1), channel_id=1, source_target_pairs={{0,4},{4,0},{8,12},{12,8},{16,20},{20,16},{24,28},{28,24},{1,5},{5... | collective-permute-start | bytes 8650760 | tf_op jit(solution)/shard_map/ppermute | solution.py:612
  434.9 147.2 %collective-permute-start.16 = (bf16[4,256,1024]{2,1,0:T(8,128)(2,1)}, bf16[4,256,1024]{2,1,0:T(8,128)(2,1)}, u32[]{:S(2)}, u32[]{:S(2)}) collective-permute-start(bf16[4,256,1024]{2,1,0:T(8,128)(2,1)} %get-tuple-element.266), channel_id=1, source_target_pairs={{0,4},{4,0},{8,12},{12,8},{16,20},{20,16},{24,28},{28,24},{1,5},{5... | collective-permute-start | bytes 6291464 | tf_op jit(solution)/shard_map/ppermute | solution.py:612
  436.4 145.7 %collective-permute-start.15 = (bf16[4,256,1024]{2,1,0:T(8,128)(2,1)}, bf16[4,256,1024]{2,1,0:T(8,128)(2,1)}, u32[]{:S(2)}, u32[]{:S(2)}) collective-permute-start(bf16[4,256,1024]{2,1,0:T(8,128)(2,1)} %get-tuple-element.268), channel_id=1, source_target_pairs={{0,4},{4,0},{8,12},{12,8},{16,20},{20,16},{24,28},{28,24},{1,5},{5... | collective-permute-start | bytes 6291464 | tf_op jit(solution)/shard_map/ppermute | solution.py:612
  469.9 112.2 %collective-permute-start.19 = (bf16[352,1024]{1,0:T(8,128)(2,1)}, bf16[352,1024]{1,0:T(8,128)(2,1)S(1)}, u32[]{:S(2)}, u32[]{:S(2)}) collective-permute-start(bf16[352,1024]{1,0:T(8,128)(2,1)} %get-tuple-element.272), channel_id=1, source_target_pairs={{0,24},{4,28},{8,0},{12,4},{16,8},{20,12},{24,16},{28,20},{1,25},{... | collective-permute-start | bytes 2162696 | tf_op jit(solution)/shard_map/ppermute | solution.py:612
  481.9 100.2 %collective-permute-start.18 = (bf16[352,1024]{1,0:T(8,128)(2,1)}, bf16[352,1024]{1,0:T(8,128)(2,1)S(1)}, u32[]{:S(2)}, u32[]{:S(2)}) collective-permute-start(bf16[352,1024]{1,0:T(8,128)(2,1)} %get-tuple-element.273), channel_id=1, source_target_pairs={{0,16},{4,20},{8,24},{12,28},{16,0},{20,4},{24,8},{28,12},{1,17},{... | collective-permute-start | bytes 2162696 | tf_op jit(solution)/shard_map/ppermute | solution.py:612
  484.7 97.4 %collective-permute-start.17 = (bf16[352,1024]{1,0:T(8,128)(2,1)}, bf16[352,1024]{1,0:T(8,128)(2,1)}, u32[]{:S(2)}, u32[]{:S(2)}) collective-permute-start(bf16[352,1024]{1,0:T(8,128)(2,1)} %get-tuple-element.274), channel_id=1, source_target_pairs={{0,8},{4,12},{8,16},{12,20},{16,24},{20,28},{24,0},{28,4},{1,9},{5... | collective-permute-start | bytes 2162696 | tf_op jit(solution)/shard_map/ppermute | solution.py:612
  496.2 86.8 %copy-start.5 = (bf16[4,256,1024]{2,1,0:T(8,128)(2,1)S(1)}, bf16[4,256,1024]{2,1,0:T(8,128)(2,1)}, u32[]{:S(2)}) copy-start(bf16[4,256,1024]{2,1,0:T(8,128)(2,1)} %get-tuple-element.205) | copy-start | bytes 6291460
  589.2 31.9 %collective-permute-start.20 = (bf16[256,1024]{1,0:T(8,128)(2,1)}, bf16[256,1024]{1,0:T(8,128)(2,1)S(1)}, u32[]{:S(2)}, u32[]{:S(2)}) collective-permute-start(bf16[256,1024]{1,0:T(8,128)(2,1)} %get-tuple-element.283), channel_id=1, source_target_pairs={{0,8},{4,12},{8,16},{12,20},{16,24},{20,28},{24,0},{28,4},{1,9},{5... | collective-permute-start | bytes 1572872 | tf_op jit(solution)/shard_map/ppermute | solution.py:612
  597.1 25.9 %copy-start.34 = (bf16[2,8,8,256]{3,2,0,1:T(8,128)(2,1)S(1)}, bf16[2,8,8,256]{3,2,0,1:T(8,128)(2,1)}, u32[]{:S(2)}) copy-start(bf16[2,8,8,256]{3,2,0,1:T(8,128)(2,1)} %copy-done.33) | copy-start | bytes 196612
  597.1 24.1 %collective-permute-start.21 = (bf16[256,1024]{1,0:T(8,128)(2,1)}, bf16[256,1024]{1,0:T(8,128)(2,1)}, u32[]{:S(2)}, u32[]{:S(2)}) collective-permute-start(bf16[256,1024]{1,0:T(8,128)(2,1)} %get-tuple-element.279), channel_id=1, source_target_pairs={{0,8},{4,12},{8,16},{12,20},{16,24},{20,28},{24,0},{28,4},{1,9},{5... | collective-permute-start | bytes 1572872 | tf_op jit(solution)/shard_map/ppermute | solution.py:612
  633.9 21.5 %collective-permute-start.22 = (bf16[256,1024]{1,0:T(8,128)(2,1)}, bf16[256,1024]{1,0:T(8,128)(2,1)S(1)}, u32[]{:S(2)}, u32[]{:S(2)}) collective-permute-start(bf16[256,1024]{1,0:T(8,128)(2,1)} %get-tuple-element.213), channel_id=1, source_target_pairs={{0,24},{4,28},{8,0},{12,4},{16,8},{20,12},{24,16},{28,20},{1,25},{... | collective-permute-start | bytes 1572872 | tf_op jit(solution)/shard_map/ppermute | solution.py:612
  637.0 23.8 %collective-permute-start.23 = (bf16[256,1024]{1,0:T(8,128)(2,1)}, bf16[256,1024]{1,0:T(8,128)(2,1)}, u32[]{:S(2)}, u32[]{:S(2)}) collective-permute-start(bf16[256,1024]{1,0:T(8,128)(2,1)} %get-tuple-element.214), channel_id=1, source_target_pairs={{0,24},{4,28},{8,0},{12,4},{16,8},{20,12},{24,16},{28,20},{1,25},{... | collective-permute-start | bytes 1572872 | tf_op jit(solution)/shard_map/ppermute | solution.py:612
  661.8 38.4 %collective-permute-start.24 = (bf16[256,1024]{1,0:T(8,128)(2,1)}, bf16[256,1024]{1,0:T(8,128)(2,1)}, u32[]{:S(2)}, u32[]{:S(2)}) collective-permute-start(bf16[256,1024]{1,0:T(8,128)(2,1)} %get-tuple-element.220), channel_id=1, source_target_pairs={{0,16},{4,20},{8,24},{12,28},{16,0},{20,4},{24,8},{28,12},{1,17},{... | collective-permute-start | bytes 1572872 | tf_op jit(solution)/shard_map/ppermute | solution.py:612
  663.0 47.4 %collective-permute-start.25 = (bf16[256,1024]{1,0:T(8,128)(2,1)}, bf16[256,1024]{1,0:T(8,128)(2,1)}, u32[]{:S(2)}, u32[]{:S(2)}) collective-permute-start(bf16[256,1024]{1,0:T(8,128)(2,1)} %get-tuple-element.221), channel_id=1, source_target_pairs={{0,16},{4,20},{8,24},{12,28},{16,0},{20,4},{24,8},{28,12},{1,17},{... | collective-permute-start | bytes 1572872 | tf_op jit(solution)/shard_map/ppermute | solution.py:612
  (79 other events, 539.5 us)

commit v4 on v3

--- a/solution.py
+++ b/solution.py
@@ -945,6 +945,10 @@
         dealt.update(zip(keys, blocks))
         return arrays
 
+    def echoed(arrays, group, step):
+        arrays, mirrored[group, step] = lax.optimization_barrier((arrays, mirrored[group, step]))
+        return arrays
+
     soon = [0] if packed else [0, 2]
 
     lead_float = prefix_tokens.astype(jnp.float32)
@@ -1172,14 +1176,14 @@
         ((inside_low, gate_low, expand_low), sources)
     )
     returns[-2:] = list(zip(sources, others))
-    lead_back = low(against(gate_low, lead_gate) + against(expand_low, lead_expand))
-    (inside_low, lead_back), returns[:-2] = lax.optimization_barrier(
-        ((inside_low, lead_back), returns[:-2])
-    )
+    gate_back = against(gate_low, lead_gate)
+    (expand_low, gate_back), returns[:-2] = lax.optimization_barrier(
+        ((expand_low, gate_back), returns[:-2])
+    )
+    lead_back = low(gate_back + against(expand_low, lead_expand))
     blocks_back = [pass_on(returns[:1])]
     if not packed:
         blocks_back.append(pass_on(returns[1:2]))
-    lead_out = low(against(inside_low, lead_down))
 
     def token_blocks(rows):
         return rows.reshape(depth, breadth, 2, -1, rows.shape[1])
@@ -1271,7 +1275,8 @@
     (pair_grad,) = cam_collect(
         "pair_grads", [jnp.swapaxes(pair_parts, 0, 1).reshape(breadth, 2, -1, pair)]
     )
-    pair_grad = back_tied(pair_grad, 1)
+    pair_grad, inside_low = back_tied((pair_grad, inside_low), 1)
+    lead_out = low(against(inside_low, lead_down))
     low_grad = jnp.concatenate([query_low, low(pair_grad)], 1)
     lead_part, tail_part = low_grad[:lead_total], low_grad[lead_total:]
     lead_back, tail_back = cam_collect(

time: 873 us -> 861 us (0.986)
  waiting for transfers between devices: 44.9 us -> 32 us
  other arithmetic: 40.5 us -> 50.1 us
    ppermute x26, waiting for transfers between devices: 44.9 us -> 32 us  [permute(): return lax.ppermute(array, 'rows', pairs)]
    convert_element_type x13 -> x14, other arithmetic: 21.8 us -> 31.4 us  [low(): return values.astype(jnp.bfloat16)]
  transfers between devices with their start and end apart: 26 -> 26, of which waited for: 5 -> 4; matrix products, arithmetic and copies ran while one was open for 21% -> 22% of each run, Pallas kernels for 32% -> 32%
where the time goes in v4:
time: 861 us; the launch traced here: 857 us
  Pallas kernels  533 us (62%)
  matrix products  165 us (19%)
  other arithmetic  50.1 us (6%)
  starting transfers between devices  43.1 us (5%)
  waiting for transfers between devices  32 us (4%)
  local copies, waits for them, and re-layouts  30.6 us (4%)
    pallas_call x9, Pallas kernels, exchange(): pl.pallas_call(kernel, name=label, out_shape=[shape for shape, _ in outpu...  508 us
    dot_general x10, matrix products, multiply(): return jnp.dot(operand, matrix, preferred_element_type=jnp.float32)  57.5 us
    dot_general x10, matrix products, against(): lax.dot_general(operand, matrix, (((1,), (1,)), ((), ())), preferred_elem...  52.6 us
    dot_general x10, matrix products, outer_sum(): lax.dot_general(operand, matrix, (((0,), (0,)), ((), ())), preferred_elem...  48.4 us
    ppermute x26, starting transfers between devices, permute(): return lax.ppermute(array, 'rows', pairs)  43.1 us
    ppermute x26, waiting for transfers between devices, permute(): return lax.ppermute(array, 'rows', pairs)  32 us
    convert_element_type x14, other arithmetic, low(): return values.astype(jnp.bfloat16)  31.4 us
  transfers between devices with their start and end apart: 26, of which 4 were waited for; matrix products, arithmetic and copies ran while one was open for 22% of the time, Pallas kernels for 32%

profile of v4, /device:TPU:0, one launch (start us, length us, event | category | flops | bytes accessed | tf_op | source)
XLA Modules:
  0.0 856.9 jit_solution(12938951318245229565)
XLA Ops:
  13.4 122.9 %first.1 = (bf16[2,2,128,2048]{3,2,1,0:T(8,128)(2,1)}, bf16[2,2,16,1024]{3,2,1,0:T(8,128)(2,1)}, bf16[4,2,4,64,640]{4,3,2,1,0:T(8,128)(2,1)}, bf16[4,2,4,32,640]...) custom-call(bf16[128,2048]{1,0:T(8,128)(2,1)} %fusion.46.refs_0_, ...), custom_call_target="tpu_custom_call" | custom-call | bytes 3000000 | tf_op jit(solution)/shard_map/first/pallas_call | solution.py:586
  142.7 4.2 convolution_convert_fusion.13
  147.6 13.0 %pairs.1 = bf16[2,2,576,128]{3,2,1,0:T(8,128)(2,1)} custom-call(bf16[576,128]{1,0:T(8,128)(2,1)} %pad_maximum_fusion.9.refs_0_), custom_call_target="tpu_custom_call" | custom-call | bytes 3000000 | tf_op jit(solution)/shard_map/pairs/pallas_call | solution.py:586
  169.7 4.4 convolution_convert_fusion.9
  174.1 22.4 %mixing.1 = (f32[128,2048]{1,0:T(8,128)}, f32[16,1024]{1,0:T(8,128)}) custom-call(bf16[2,2,128,2048]{3,2,1,0:T(8,128)(2,1)} %bitcast.353, bf16[2,2,16,1024]{3,2,1,0:T(8,128)(2,1)} %bitcast.382), custom_call_target="tpu_custom_call" | custom-call | bytes 3000000 | tf_op jit(solution)/shard_map/mixing/pallas_call | solution.py:586
  201.9 19.5 %collective-permute-done.1.refs_4_ = bf16[608,1024]{1,0:T(8,128)(2,1)} collective-permute-done((bf16[608,1024]{1,0:T(8,128)(2,1)}, bf16[608,1024]{1,0:T(8,128)(2,1)}, u32[]{:S(2)}, u32[]{:S(2)}) %collective-permute-start.1) | collective-permute-done | bytes 1245216 | tf_op jit(solution)/shard_map/ppermute | solution.py:612
  225.5 85.2 %gather.1 = (bf16[4,2,2,128,2048]{4,3,2,1,0:T(8,128)(2,1)}, bf16[4,2,2,16,1024]{4,3,2,1,0:T(8,128)(2,1)}) custom-call(bf16[128,2048]{1,0:T(8,128)(2,1)} %multiply_convert_fusion.refs_0_, bf16[16,1024]{1,0:T(8,128)(2,1)} %multiply_convert_fusion.2.refs_1_), custom_call_target="tpu_custom_call" | custom-call | bytes 3000000 | tf_op jit(solution)/shard_map/gather/pallas_call | solution.py:586
  315.6 9.7 %upper.1 = (bf16[4,2,256,1024]{3,2,1,0:T(8,128)(2,1)}, bf16[4,2,256,1024]{3,2,1,0:T(8,128)(2,1)}, bf16[4,2,128,256]{3,2,1,0:T(8,128)(2,1)}, bf16[4,2,128,256]{3,2,1,0:T(8,128)(2,1)}, bf16[4,2,128,256]{3,2,1,0:T(8,128)(2,1)}) custom-call(bf16[608,1024]{1,0:T(8,128)(2,1)} %get-tuple-element.163.refs_0_, bf16[608,1024]{1,0:T(8,128)(2,1)} %collective-permute-done.3.refs_1_, ...), custom_call_target="tpu_custom_call" | custom-call | bytes 19922944 | tf_op jit(solution)/shard_map/upper/pallas_call | solution.py:640
  334.0 11.1 %convolution_convert_fusion.3 = bf16[2048,1024]{1,0:T(8,128)(2,1)S(1)} fusion(bf16[2048,2048]{1,0:T(8,128)(2,1)S(1)} %bitcast.406, bf16[2048,1024]{1,0:T(8,128)(2,1)} %bitcast.409), kind=kOutput, calls=%fused_computation.37 | convolution fusion | flops 8592031744 | bytes 16777216 | tf_op jit(solution)/shard_map/dot_general | solution.py:714
  345.1 4.2 collective-permute-done.8.refs_4_
  349.9 11.4 %convolution_convert_fusion.2 = bf16[2048,1024]{1,0:T(8,128)(2,1)S(1)} fusion(bf16[2048,2048]{1,0:T(8,128)(2,1)} %bitcast.403, bf16[2048,1024]{1,0:T(8,128)(2,1)S(1)} %bitcast.408), kind=kOutput, calls=%fused_computation.36 | convolution fusion | flops 8592031744 | bytes 16777216 | tf_op jit(solution)/shard_map/dot_general | solution.py:714
  366.7 9.8 %convolution_convert_fusion.6 = bf16[2048,1024]{1,0:T(8,128)(2,1)S(1)} fusion(bf16[2048,2048]{1,0:T(8,128)(2,1)S(1)} %bitcast.402, bf16[2048,1024]{1,0:T(8,128)(2,1)S(1)} %fusion.2), kind=kOutput, calls=%fused_computation.40 | convolution fusion | flops 8592031744 | bytes 16777216 | tf_op jit(solution)/shard_map/dot_general | solution.py:724
  380.8 5.6 lower.1
  386.4 19.2 %fusion.19 = (bf16[2048,1024]{1,0:T(8,128)(2,1)S(1)}, bf16[2048,1024]{1,0:T(8,128)(2,1)S(1)}) fusion(bf16[2048,1024]{1,0:T(8,128)(2,1)} %copy-done.10, bf16[2048,1024]{1,0:T(8,128)(2,1)} %copy-done.11, bf16[2048,2048]{1,0:T(8,128)(2,1)} %bitcast.399, bf16[2048,1024]{1,0:T(8,128)(2,1)} %bitcast.340), kind=kOutput, calls=%fused_computation.29 | convolution fusion | flops 8644460544 | bytes 29360128 | tf_op jit(solution)/shard_map/dot_general | solution.py:714
  405.7 14.4 %convolution_convert_fusion.4 = bf16[2048,1024]{1,0:T(8,128)(2,1)S(1)} fusion(bf16[2048,2048]{1,0:T(8,128)(2,1)} %bitcast.404, bf16[2048,1024]{1,0:T(8,128)(2,1)S(1)} %get-tuple-element.194), kind=kOutput, calls=%fused_computation.38 | convolution fusion | flops 8592031744 | bytes 16777216 | tf_op jit(solution)/shard_map/dot_general | solution.py:724
  420.1 11.5 %convolution_convert_fusion.5 = bf16[2048,1024]{1,0:T(8,128)(2,1)S(1)} fusion(bf16[2048,2048]{1,0:T(8,128)(2,1)} %bitcast.405, bf16[2048,1024]{1,0:T(8,128)(2,1)S(1)} %get-tuple-element.188), kind=kOutput, calls=%fused_computation.39 | convolution fusion | flops 8592031744 | bytes 16777216 | tf_op jit(solution)/shard_map/dot_general | solution.py:724
  438.6 10.7 %fusion.115 = f32[2048,2048]{1,0:T(8,128)S(1)} fusion(bf16[2048,1024]{1,0:T(8,128)(2,1)} %copy-done.81, bf16[2048,1024]{1,0:T(8,128)(2,1)S(1)} %bitcast.410), kind=kOutput, calls=%fused_computation.255 | convolution fusion | flops 8589934592 | bytes 25165824 | tf_op jit(solution)/shard_map/dot_general | solution.py:718
  454.3 12.0 %collective-permute-start.19 = (bf16[352,1024]{1,0:T(8,128)(2,1)}, bf16[352,1024]{1,0:T(8,128)(2,1)S(1)}, u32[]{:S(2)}, u32[]{:S(2)}) collective-permute-start(bf16[352,1024]{1,0:T(8,128)(2,1)} %get-tuple-element.274), channel_id=1, source_target_pairs={{0,24},{4,28},{8,0},{12,4},{16,8},{20,12},{24,16},{28,20},{1,25},{... | collective-permute-start | bytes 2162696 | tf_op jit(solution)/shard_map/ppermute | solution.py:612
  469.5 15.4 %fusion.116 = f32[2048,2048]{1,0:T(8,128)} fusion(bf16[2048,1024]{1,0:T(8,128)(2,1)} %copy-done.80, bf16[2048,1024]{1,0:T(8,128)(2,1)} %bitcast.407), kind=kOutput, calls=%fused_computation.256 | convolution fusion | flops 8589934592 | bytes 25165824 | tf_op jit(solution)/shard_map/dot_general | solution.py:718
  484.8 9.7 %add_convert_fusion = bf16[2048,2048]{1,0:T(8,128)(2,1)} fusion(f32[2048,2048]{1,0:T(8,128)S(1)} %fusion.115, f32[2048,2048]{1,0:T(8,128)} %fusion.116), kind=kLoop, calls=%fused_computation.7 | loop fusion | flops 8388608 | bytes 41943040 | tf_op jit(solution)/shard_map/convert_element_type | solution.py:750
  494.5 77.5 %collect.1 = (f32[128,2048]{1,0:T(8,128)}, f32[16,1024]{1,0:T(8,128)}) custom-call(bf16[4,2,2,128,2048]{4,3,2,1,0:T(8,128)(2,1)} %bitcast.324, bf16[4,2,2,16,1024]{4,3,2,1,0:T(8,128)(2,1)} %bitcast.350), custom_call_target="tpu_custom_call" | custom-call | bytes 3000000 | tf_op jit(solution)/shard_map/collect/pallas_call | solution.py:586
  585.3 21.9 %sent.1 = (bf16[2,2,128,2048]{3,2,1,0:T(8,128)(2,1)}, bf16[2,2,16,1024]{3,2,1,0:T(8,128)(2,1)}) custom-call(bf16[128,2048]{1,0:T(8,128)(2,1)} %fusion.101.refs_0_, bf16[16,1024]{1,0:T(8,128)(2,1)} %fusion.98.refs_1_), custom_call_target="tpu_custom_call" | custom-call | bytes 3000000 | tf_op jit(solution)/shard_map/sent/pallas_call | solution.py:586
  611.5 3.6 fusion.117
  620.1 3.7 collective-permute-start.22
  630.1 13.3 %pair_grads.1 = f32[576,128]{1,0:T(8,128)} custom-call(bf16[2,2,576,128]{3,2,1,0:T(8,128)(2,1)} %bitcast.347), custom_call_target="tpu_custom_call" | custom-call | bytes 3000000 | tf_op jit(solution)/shard_map/pair_grads/pallas_call | solution.py:586
  643.5 3.6 collective-permute-done.23.refs_11_
  651.2 14.1 %convolution_convert_fusion = bf16[2048,2048]{1,0:T(8,128)(2,1)} fusion(bf16[2048,1024]{1,0:T(8,128)(2,1)} %copy-done.9, bf16[2048,1024]{1,0:T(8,128)(2,1)} %bitcast.341), kind=kOutput, calls=%fused_computation.31 | convolution fusion | flops 8594128896 | bytes 16777216 | tf_op jit(solution)/shard_map/dot_general | solution.py:718
  669.6 22.4 %backs.1 = (f32[128,2048]{1,0:T(8,128)}, f32[16,1024]{1,0:T(8,128)}) custom-call(bf16[2,2,128,2048]{3,2,1,0:T(8,128)(2,1)} %bitcast.352, bf16[2,2,16,1024]{3,2,1,0:T(8,128)(2,1)} %bitcast.381), custom_call_target="tpu_custom_call" | custom-call | bytes 3000000 | tf_op jit(solution)/shard_map/backs/pallas_call | solution.py:586
  692.1 4.6 collective-permute-done.25.refs_10_
  696.8 5.1 convolution_convert_fusion.7
  706.0 128.9 %fold.1 = (bf16[4,64,640]{2,1,0:T(8,128)(2,1)}, bf16[4,32,640]{2,1,0:T(8,128)(2,1)}, bf16[4,64,512]{2,1,0:T(8,128)(2,1)}, bf16[4,32,512]{2,1,0:T(8,128)(2,1)}, f...) custom-call(bf16[4,2,4,64,640]{4,3,2,1,0:T(8,128)(2,1)} %bitcast.346, ...), custom_call_target="tpu_custom_call" | custom-call | bytes 3000000 | tf_op jit(solution)/shard_map/fold/pallas_call | solution.py:586
  845.8 10.5 %returns.1 = (f32[256,4096]{1,0:T(8,128)}, f32[256,4096]{1,0:T(8,128)}, f32[256,4096]{1,0:T(8,128)}, f32[128,1024]{1,0:T(8,128)}, f32[128,1024]{1,0:T(8,128)}, /*index=5*/f32[128,1024]{1,0:T(8,128)}) custom-call(bf16[352,1024]{1,0:T(8,128)(2,1)} %get-tuple-element.238.refs_0_, bf16[352,1024]{1,0:T(8,128)(2,1)} %collective-permute-done.17.refs_1_, ...), custom_call_target="tpu_custom_call" | custom-call | bytes 21233664 | tf_op jit(solution)/shard_map/returns/pallas_call | solution.py:695
  (333 shorter events, 128.6 us)
Async XLA Ops:
  136.4 60.2 %collective-permute-start = (bf16[608,1024]{1,0:T(8,128)(2,1)}, bf16[608,1024]{1,0:T(8,128)(2,1)S(1)}, u32[]{:S(2)}, u32[]{:S(2)}) collective-permute-start(bf16[608,1024]{1,0:T(8,128)(2,1)} %get-tuple-element.146), channel_id=1, source_target_pairs={{0,8},{4,12},{8,16},{12,20},{16,24},{20,28},{24,0},{28,4},{1,9},{5... | collective-permute-start | bytes 3735560 | tf_op jit(solution)/shard_map/ppermute | solution.py:612
  136.4 84.9 %collective-permute-start.1 = (bf16[608,1024]{1,0:T(8,128)(2,1)}, bf16[608,1024]{1,0:T(8,128)(2,1)}, u32[]{:S(2)}, u32[]{:S(2)}) collective-permute-start(bf16[608,1024]{1,0:T(8,128)(2,1)} %get-tuple-element.149), channel_id=1, source_target_pairs={{0,16},{4,20},{8,24},{12,28},{16,0},{20,4},{24,8},{28,12},{1,17},{... | collective-permute-start | bytes 3735560 | tf_op jit(solution)/shard_map/ppermute | solution.py:612
  138.3 83.1 %collective-permute-start.2 = (bf16[608,1024]{1,0:T(8,128)(2,1)}, bf16[608,1024]{1,0:T(8,128)(2,1)}, u32[]{:S(2)}, u32[]{:S(2)}) collective-permute-start(bf16[608,1024]{1,0:T(8,128)(2,1)} %get-tuple-element.152), channel_id=1, source_target_pairs={{0,24},{4,28},{8,0},{12,4},{16,8},{20,12},{24,16},{28,20},{1,25},{... | collective-permute-start | bytes 3735560 | tf_op jit(solution)/shard_map/ppermute | solution.py:612
  140.4 170.3 %collective-permute-start.3 = (bf16[608,1024]{1,0:T(8,128)(2,1)}, bf16[608,1024]{1,0:T(8,128)(2,1)}, u32[]{:S(2)}, u32[]{:S(2)}) collective-permute-start(bf16[608,1024]{1,0:T(8,128)(2,1)} %get-tuple-element.163.refs_0_), channel_id=1, source_target_pairs={{0,4},{4,0},{8,12},{12,8},{16,20},{20,16},{24,28},{28,24},{1,5},{5... | collective-permute-start | bytes 3735560 | tf_op jit(solution)/shard_map/ppermute | solution.py:612
  174.1 26.1 %copy-start.55 = (f32[1024]{0:T(1024)S(1)}, f32[1024]{0:T(1024)}, u32[]{:S(2)}) copy-start(f32[1024]{0:T(1024)} %param.41) | copy-start | bytes 12292
  174.1 26.8 %copy-start.50 = (f32[2048]{0:T(1024)S(1)}, f32[2048]{0:T(1024)}, u32[]{:S(2)}) copy-start(f32[2048]{0:T(1024)} %param.39) | copy-start | bytes 24580
  196.6 119.0 %copy-start.24 = (bf16[608,1024]{1,0:T(8,128)(2,1)}, bf16[608,1024]{1,0:T(8,128)(2,1)S(1)}, u32[]{:S(2)}) copy-start(bf16[608,1024]{1,0:T(8,128)(2,1)S(1)} %collective-permute-done.refs_2_) | copy-start | bytes 3735556
  221.4 89.4 %collective-permute-start.6 = (bf16[608,1024]{1,0:T(8,128)(2,1)}, bf16[608,1024]{1,0:T(8,128)(2,1)S(1)}, u32[]{:S(2)}, u32[]{:S(2)}) collective-permute-start(bf16[608,1024]{1,0:T(8,128)(2,1)} %collective-permute-done.2.refs_6_), channel_id=1, source_target_pairs={{0,4},{4,0},{8,12},{12,8},{16,20},{20,16},{24,28},{28,24},{1,5},{5... | collective-permute-start | bytes 3735560 | tf_op jit(solution)/shard_map/ppermute | solution.py:612
  222.0 91.4 %collective-permute-start.5 = (bf16[608,1024]{1,0:T(8,128)(2,1)}, bf16[608,1024]{1,0:T(8,128)(2,1)}, u32[]{:S(2)}, u32[]{:S(2)}) collective-permute-start(bf16[608,1024]{1,0:T(8,128)(2,1)} %collective-permute-done.1.refs_4_), channel_id=1, source_target_pairs={{0,4},{4,0},{8,12},{12,8},{16,20},{20,16},{24,28},{28,24},{1,5},{5... | collective-permute-start | bytes 3735560 | tf_op jit(solution)/shard_map/ppermute | solution.py:612
  223.5 92.1 %collective-permute-start.4 = (bf16[608,1024]{1,0:T(8,128)(2,1)S(1)}, bf16[608,1024]{1,0:T(8,128)(2,1)}, u32[]{:S(2)}, u32[]{:S(2)}) collective-permute-start(bf16[608,1024]{1,0:T(8,128)(2,1)S(1)} %collective-permute-done.refs_2_), channel_id=1, source_target_pairs={{0,4},{4,0},{8,12},{12,8},{16,20},{20,16},{24,28},{28,24},{1,5},{5... | collective-permute-start | bytes 3735560 | tf_op jit(solution)/shard_map/ppermute | solution.py:612
  224.0 155.9 %collective-permute-start.10 = (bf16[256,1024]{1,0:T(8,128)(2,1)}, bf16[256,1024]{1,0:T(8,128)(2,1)}, u32[]{:S(2)}, u32[]{:S(2)}) collective-permute-start(bf16[256,1024]{1,0:T(8,128)(2,1)} %get-tuple-element.157.refs_0_), channel_id=1, source_target_pairs={{0,4},{4,0},{8,12},{12,8},{16,20},{20,16},{24,28},{28,24},{1,5},{5... | collective-permute-start | bytes 1572872 | tf_op jit(solution)/shard_map/ppermute | solution.py:612
  310.7 22.8 %collective-permute-start.7 = (bf16[256,1024]{1,0:T(8,128)(2,1)}, bf16[256,1024]{1,0:T(8,128)(2,1)}, u32[]{:S(2)}, u32[]{:S(2)}) collective-permute-start(bf16[256,1024]{1,0:T(8,128)(2,1)} %get-tuple-element.172), channel_id=1, source_target_pairs={{0,8},{4,12},{8,16},{12,20},{16,24},{20,28},{24,0},{28,4},{1,9},{5... | collective-permute-start | bytes 1572872 | tf_op jit(solution)/shard_map/ppermute | solution.py:612
  310.8 38.6 %collective-permute-start.8 = (bf16[256,1024]{1,0:T(8,128)(2,1)}, bf16[256,1024]{1,0:T(8,128)(2,1)}, u32[]{:S(2)}, u32[]{:S(2)}) collective-permute-start(bf16[256,1024]{1,0:T(8,128)(2,1)} %get-tuple-element.175), channel_id=1, source_target_pairs={{0,16},{4,20},{8,24},{12,28},{16,0},{20,4},{24,8},{28,12},{1,17},{... | collective-permute-start | bytes 1572872 | tf_op jit(solution)/shard_map/ppermute | solution.py:612
  313.3 48.2 %collective-permute-start.9 = (bf16[256,1024]{1,0:T(8,128)(2,1)}, bf16[256,1024]{1,0:T(8,128)(2,1)}, u32[]{:S(2)}, u32[]{:S(2)}) collective-permute-start(bf16[256,1024]{1,0:T(8,128)(2,1)} %get-tuple-element.179), channel_id=1, source_target_pairs={{0,24},{4,28},{8,0},{12,4},{16,8},{20,12},{24,16},{28,20},{1,25},{... | collective-permute-start | bytes 1572872 | tf_op jit(solution)/shard_map/ppermute | solution.py:612
  333.5 46.4 %collective-permute-start.11 = (bf16[256,1024]{1,0:T(8,128)(2,1)}, bf16[256,1024]{1,0:T(8,128)(2,1)S(1)}, u32[]{:S(2)}, u32[]{:S(2)}) collective-permute-start(bf16[256,1024]{1,0:T(8,128)(2,1)} %collective-permute-done.7.refs_2_), channel_id=1, source_target_pairs={{0,4},{4,0},{8,12},{12,8},{16,20},{20,16},{24,28},{28,24},{1,5},{5... | collective-permute-start | bytes 1572872 | tf_op jit(solution)/shard_map/ppermute | solution.py:612
  334.0 32.6 %slice-start = ((s8[8388608]{0:T(1024)(128)(4,1)}), s8[4194304]{0:T(1024)(128)(4,1)S(1)}, s32[]{:S(2)}) async-start(s8[8388608]{0:T(1024)(128)(4,1)} %bitcast.400), calls=%async_computation | async-start | bytes 8388608
  349.4 30.5 %collective-permute-start.12 = (bf16[256,1024]{1,0:T(8,128)(2,1)}, bf16[256,1024]{1,0:T(8,128)(2,1)S(1)}, u32[]{:S(2)}, u32[]{:S(2)}) collective-permute-start(bf16[256,1024]{1,0:T(8,128)(2,1)} %collective-permute-done.8.refs_4_), channel_id=1, source_target_pairs={{0,4},{4,0},{8,12},{12,8},{16,20},{20,16},{24,28},{28,24},{1,5},{5... | collective-permute-start | bytes 1572872 | tf_op jit(solution)/shard_map/ppermute | solution.py:612
  361.5 18.4 %collective-permute-start.13 = (bf16[256,1024]{1,0:T(8,128)(2,1)}, bf16[256,1024]{1,0:T(8,128)(2,1)}, u32[]{:S(2)}, u32[]{:S(2)}) collective-permute-start(bf16[256,1024]{1,0:T(8,128)(2,1)} %collective-permute-done.9.refs_6_), channel_id=1, source_target_pairs={{0,4},{4,0},{8,12},{12,8},{16,20},{20,16},{24,28},{28,24},{1,5},{5... | collective-permute-start | bytes 1572872 | tf_op jit(solution)/shard_map/ppermute | solution.py:612
  379.1 70.2 %collective-permute-start.14 = (bf16[4,352,1024]{2,1,0:T(8,128)(2,1)}, bf16[4,352,1024]{2,1,0:T(8,128)(2,1)}, u32[]{:S(2)}, u32[]{:S(2)}) collective-permute-start(bf16[4,352,1024]{2,1,0:T(8,128)(2,1)} %pad_maximum_fusion.1), channel_id=1, source_target_pairs={{0,4},{4,0},{8,12},{12,8},{16,20},{20,16},{24,28},{28,24},{1,5},{5... | collective-permute-start | bytes 8650760 | tf_op jit(solution)/shard_map/ppermute | solution.py:612
  436.6 135.4 %collective-permute-start.16 = (bf16[4,256,1024]{2,1,0:T(8,128)(2,1)}, bf16[4,256,1024]{2,1,0:T(8,128)(2,1)}, u32[]{:S(2)}, u32[]{:S(2)}) collective-permute-start(bf16[4,256,1024]{2,1,0:T(8,128)(2,1)} %get-tuple-element.268), channel_id=1, source_target_pairs={{0,4},{4,0},{8,12},{12,8},{16,20},{20,16},{24,28},{28,24},{1,5},{5... | collective-permute-start | bytes 6291464 | tf_op jit(solution)/shard_map/ppermute | solution.py:612
  438.1 133.9 %collective-permute-start.15 = (bf16[4,256,1024]{2,1,0:T(8,128)(2,1)}, bf16[4,256,1024]{2,1,0:T(8,128)(2,1)}, u32[]{:S(2)}, u32[]{:S(2)}) collective-permute-start(bf16[4,256,1024]{2,1,0:T(8,128)(2,1)} %get-tuple-element.270), channel_id=1, source_target_pairs={{0,4},{4,0},{8,12},{12,8},{16,20},{20,16},{24,28},{28,24},{1,5},{5... | collective-permute-start | bytes 6291464 | tf_op jit(solution)/shard_map/ppermute | solution.py:612
  454.3 117.8 %collective-permute-start.19 = (bf16[352,1024]{1,0:T(8,128)(2,1)}, bf16[352,1024]{1,0:T(8,128)(2,1)S(1)}, u32[]{:S(2)}, u32[]{:S(2)}) collective-permute-start(bf16[352,1024]{1,0:T(8,128)(2,1)} %get-tuple-element.274), channel_id=1, source_target_pairs={{0,24},{4,28},{8,0},{12,4},{16,8},{20,12},{24,16},{28,20},{1,25},{... | collective-permute-start | bytes 2162696 | tf_op jit(solution)/shard_map/ppermute | solution.py:612
  466.3 105.8 %collective-permute-start.18 = (bf16[352,1024]{1,0:T(8,128)(2,1)}, bf16[352,1024]{1,0:T(8,128)(2,1)S(1)}, u32[]{:S(2)}, u32[]{:S(2)}) collective-permute-start(bf16[352,1024]{1,0:T(8,128)(2,1)} %get-tuple-element.275), channel_id=1, source_target_pairs={{0,16},{4,20},{8,24},{12,28},{16,0},{20,4},{24,8},{28,12},{1,17},{... | collective-permute-start | bytes 2162696 | tf_op jit(solution)/shard_map/ppermute | solution.py:612
  469.1 103.0 %collective-permute-start.17 = (bf16[352,1024]{1,0:T(8,128)(2,1)}, bf16[352,1024]{1,0:T(8,128)(2,1)}, u32[]{:S(2)}, u32[]{:S(2)}) collective-permute-start(bf16[352,1024]{1,0:T(8,128)(2,1)} %get-tuple-element.276), channel_id=1, source_target_pairs={{0,8},{4,12},{8,16},{12,20},{16,24},{20,28},{24,0},{28,4},{1,9},{5... | collective-permute-start | bytes 2162696 | tf_op jit(solution)/shard_map/ppermute | solution.py:612
  494.5 78.4 %copy-start.5 = (bf16[4,256,1024]{2,1,0:T(8,128)(2,1)S(1)}, bf16[4,256,1024]{2,1,0:T(8,128)(2,1)}, u32[]{:S(2)}) copy-start(bf16[4,256,1024]{2,1,0:T(8,128)(2,1)} %get-tuple-element.206) | copy-start | bytes 6291460
  579.2 28.1 %collective-permute-start.20 = (bf16[256,1024]{1,0:T(8,128)(2,1)}, bf16[256,1024]{1,0:T(8,128)(2,1)S(1)}, u32[]{:S(2)}, u32[]{:S(2)}) collective-permute-start(bf16[256,1024]{1,0:T(8,128)(2,1)} %get-tuple-element.285), channel_id=1, source_target_pairs={{0,8},{4,12},{8,16},{12,20},{16,24},{20,28},{24,0},{28,4},{1,9},{5... | collective-permute-start | bytes 1572872 | tf_op jit(solution)/shard_map/ppermute | solution.py:612
  583.8 25.3 %copy-start.33 = (bf16[2,8,8,256]{3,2,0,1:T(8,128)(2,1)S(1)}, bf16[2,8,8,256]{3,2,0,1:T(8,128)(2,1)}, u32[]{:S(2)}) copy-start(bf16[2,8,8,256]{3,2,0,1:T(8,128)(2,1)} %copy-done.32) | copy-start | bytes 196612
  583.8 23.5 %collective-permute-start.21 = (bf16[256,1024]{1,0:T(8,128)(2,1)}, bf16[256,1024]{1,0:T(8,128)(2,1)}, u32[]{:S(2)}, u32[]{:S(2)}) collective-permute-start(bf16[256,1024]{1,0:T(8,128)(2,1)} %get-tuple-element.281), channel_id=1, source_target_pairs={{0,8},{4,12},{8,16},{12,20},{16,24},{20,28},{24,0},{28,4},{1,9},{5... | collective-permute-start | bytes 1572872 | tf_op jit(solution)/shard_map/ppermute | solution.py:612
  620.1 23.4 %collective-permute-start.22 = (bf16[256,1024]{1,0:T(8,128)(2,1)}, bf16[256,1024]{1,0:T(8,128)(2,1)S(1)}, u32[]{:S(2)}, u32[]{:S(2)}) collective-permute-start(bf16[256,1024]{1,0:T(8,128)(2,1)} %get-tuple-element.215), channel_id=1, source_target_pairs={{0,24},{4,28},{8,0},{12,4},{16,8},{20,12},{24,16},{28,20},{1,25},{... | collective-permute-start | bytes 1572872 | tf_op jit(solution)/shard_map/ppermute | solution.py:612
  623.7 23.3 %collective-permute-start.23 = (bf16[256,1024]{1,0:T(8,128)(2,1)}, bf16[256,1024]{1,0:T(8,128)(2,1)}, u32[]{:S(2)}, u32[]{:S(2)}) collective-permute-start(bf16[256,1024]{1,0:T(8,128)(2,1)} %get-tuple-element.216), channel_id=1, source_target_pairs={{0,24},{4,28},{8,0},{12,4},{16,8},{20,12},{24,16},{28,20},{1,25},{... | collective-permute-start | bytes 1572872 | tf_op jit(solution)/shard_map/ppermute | solution.py:612
  648.0 44.1 %collective-permute-start.24 = (bf16[256,1024]{1,0:T(8,128)(2,1)}, bf16[256,1024]{1,0:T(8,128)(2,1)}, u32[]{:S(2)}, u32[]{:S(2)}) collective-permute-start(bf16[256,1024]{1,0:T(8,128)(2,1)} %get-tuple-element.222), channel_id=1, source_target_pairs={{0,16},{4,20},{8,24},{12,28},{16,0},{20,4},{24,8},{28,12},{1,17},{... | collective-permute-start | bytes 1572872 | tf_op jit(solution)/shard_map/ppermute | solution.py:612
  651.1 45.6 %collective-permute-start.25 = (bf16[256,1024]{1,0:T(8,128)(2,1)}, bf16[256,1024]{1,0:T(8,128)(2,1)}, u32[]{:S(2)}, u32[]{:S(2)}) collective-permute-start(bf16[256,1024]{1,0:T(8,128)(2,1)} %get-tuple-element.223), channel_id=1, source_target_pairs={{0,16},{4,20},{8,24},{12,28},{16,0},{20,4},{24,8},{28,12},{1,17},{... | collective-permute-start | bytes 1572872 | tf_op jit(solution)/shard_map/ppermute | solution.py:612
  (78 other events, 525.6 us)

commit v5 on v4

--- a/solution.py
+++ b/solution.py
@@ -670,7 +670,7 @@
                 loads[block].wait()
                 waited.add(block)
             kind = shares.index((outs[out].shape[-2], share))
-            turn = turns.get(kind, 0) % 2
+            turn = turns.get(kind, 0) % 4
             turns[kind] = turns.get(kind, 0) + 1
             if (kind, turn) in previous:
                 previous[kind, turn].wait()
@@ -685,7 +685,7 @@
                 target = targets[out].at[z]
             else:
                 target = targets[out].at[:, pl.ds(pl.multiple_of(z * share, share), share)]
-            copy = pltpu.make_async_copy(buffer, target, stored.at[2 * kind + turn])
+            copy = pltpu.make_async_copy(buffer, target, stored.at[4 * kind + turn])
             copy.start()
             previous[kind, turn] = copy
         for copy in previous.values():
@@ -699,8 +699,8 @@
         in_specs=[pl.BlockSpec(memory_space=pl.ANY)] * len(blocks),
         out_specs=[pl.BlockSpec(memory_space=pl.ANY)] * len(outs),
         scratch_shapes=[pltpu.VMEM(block.shape, block.dtype) for block in blocks]
-        + [pltpu.VMEM((2,) + share, jnp.float32) for share in shares]
-        + [pltpu.SemaphoreType.DMA((len(blocks),)), pltpu.SemaphoreType.DMA((2 * len(shares),))],
+        + [pltpu.VMEM((4,) + share, jnp.float32) for share in shares]
+        + [pltpu.SemaphoreType.DMA((len(blocks),)), pltpu.SemaphoreType.DMA((4 * len(shares),))],
         cost_estimate=pl.CostEstimate(flops=0, bytes_accessed=6 * size, transcendentals=0),
         compiler_params=pltpu.CompilerParams(vmem_limit_bytes=60 << 20),
     )(*blocks)

time: 861 us -> 858 us (level)
  no operation moved by 1% of the time
where the time goes in v5:
time: 858 us; the launch traced here: 853 us
  Pallas kernels  530 us (62%)
  matrix products  165 us (19%)
  other arithmetic  50.1 us (6%)
  starting transfers between devices  43.1 us (5%)
  waiting for transfers between devices  32 us (4%)
  local copies, waits for them, and re-layouts  30.6 us (4%)
    pallas_call x9, Pallas kernels, exchange(): pl.pallas_call(kernel, name=label, out_shape=[shape for shape, _ in outpu...  508 us
    dot_general x10, matrix products, multiply(): return jnp.dot(operand, matrix, preferred_element_type=jnp.float32)  57.5 us
    dot_general x10, matrix products, against(): lax.dot_general(operand, matrix, (((1,), (1,)), ((), ())), preferred_elem...  52.6 us
    dot_general x10, matrix products, outer_sum(): lax.dot_general(operand, matrix, (((0,), (0,)), ((), ())), preferred_elem...  48.4 us
    ppermute x26, starting transfers between devices, permute(): return lax.ppermute(array, 'rows', pairs)  43.1 us
    ppermute x26, waiting for transfers between devices, permute(): return lax.ppermute(array, 'rows', pairs)  32 us
    convert_element_type x14, other arithmetic, low(): return values.astype(jnp.bfloat16)  31.4 us
  transfers between devices with their start and end apart: 26, of which 4 were waited for; matrix products, arithmetic and copies ran while one was open for 22% of the time, Pallas kernels for 32%

profile of v5, /device:TPU:0, one launch (start us, length us, event | category | flops | bytes accessed | tf_op | source)
XLA Modules:
  0.0 853.3 jit_solution(18350410581293303666)
XLA Ops:
  13.4 122.9 %first.1 = (bf16[2,2,128,2048]{3,2,1,0:T(8,128)(2,1)}, bf16[2,2,16,1024]{3,2,1,0:T(8,128)(2,1)}, bf16[4,2,4,64,640]{4,3,2,1,0:T(8,128)(2,1)}, bf16[4,2,4,32,640]...) custom-call(bf16[128,2048]{1,0:T(8,128)(2,1)} %fusion.46.refs_0_, ...), custom_call_target="tpu_custom_call" | custom-call | bytes 3000000 | tf_op jit(solution)/shard_map/first/pallas_call | solution.py:586
  142.7 4.2 convolution_convert_fusion.13
  147.6 13.0 %pairs.1 = bf16[2,2,576,128]{3,2,1,0:T(8,128)(2,1)} custom-call(bf16[576,128]{1,0:T(8,128)(2,1)} %pad_maximum_fusion.9.refs_0_), custom_call_target="tpu_custom_call" | custom-call | bytes 3000000 | tf_op jit(solution)/shard_map/pairs/pallas_call | solution.py:586
  169.7 4.4 convolution_convert_fusion.9
  174.1 22.4 %mixing.1 = (f32[128,2048]{1,0:T(8,128)}, f32[16,1024]{1,0:T(8,128)}) custom-call(bf16[2,2,128,2048]{3,2,1,0:T(8,128)(2,1)} %bitcast.353, bf16[2,2,16,1024]{3,2,1,0:T(8,128)(2,1)} %bitcast.382), custom_call_target="tpu_custom_call" | custom-call | bytes 3000000 | tf_op jit(solution)/shard_map/mixing/pallas_call | solution.py:586
  201.9 19.5 %collective-permute-done.1.refs_4_ = bf16[608,1024]{1,0:T(8,128)(2,1)} collective-permute-done((bf16[608,1024]{1,0:T(8,128)(2,1)}, bf16[608,1024]{1,0:T(8,128)(2,1)}, u32[]{:S(2)}, u32[]{:S(2)}) %collective-permute-start.1) | collective-permute-done | bytes 1245216 | tf_op jit(solution)/shard_map/ppermute | solution.py:612
  225.5 85.2 %gather.1 = (bf16[4,2,2,128,2048]{4,3,2,1,0:T(8,128)(2,1)}, bf16[4,2,2,16,1024]{4,3,2,1,0:T(8,128)(2,1)}) custom-call(bf16[128,2048]{1,0:T(8,128)(2,1)} %multiply_convert_fusion.refs_0_, bf16[16,1024]{1,0:T(8,128)(2,1)} %multiply_convert_fusion.2.refs_1_), custom_call_target="tpu_custom_call" | custom-call | bytes 3000000 | tf_op jit(solution)/shard_map/gather/pallas_call | solution.py:586
  315.6 9.7 %upper.1 = (bf16[4,2,256,1024]{3,2,1,0:T(8,128)(2,1)}, bf16[4,2,256,1024]{3,2,1,0:T(8,128)(2,1)}, bf16[4,2,128,256]{3,2,1,0:T(8,128)(2,1)}, bf16[4,2,128,256]{3,2,1,0:T(8,128)(2,1)}, bf16[4,2,128,256]{3,2,1,0:T(8,128)(2,1)}) custom-call(bf16[608,1024]{1,0:T(8,128)(2,1)} %get-tuple-element.163.refs_0_, bf16[608,1024]{1,0:T(8,128)(2,1)} %collective-permute-done.3.refs_1_, ...), custom_call_target="tpu_custom_call" | custom-call | bytes 19922944 | tf_op jit(solution)/shard_map/upper/pallas_call | solution.py:640
  334.0 11.1 %convolution_convert_fusion.3 = bf16[2048,1024]{1,0:T(8,128)(2,1)S(1)} fusion(bf16[2048,2048]{1,0:T(8,128)(2,1)S(1)} %bitcast.406, bf16[2048,1024]{1,0:T(8,128)(2,1)} %bitcast.409), kind=kOutput, calls=%fused_computation.37 | convolution fusion | flops 8592031744 | bytes 16777216 | tf_op jit(solution)/shard_map/dot_general | solution.py:714
  345.1 4.2 collective-permute-done.8.refs_4_
  349.9 11.4 %convolution_convert_fusion.2 = bf16[2048,1024]{1,0:T(8,128)(2,1)S(1)} fusion(bf16[2048,2048]{1,0:T(8,128)(2,1)} %bitcast.403, bf16[2048,1024]{1,0:T(8,128)(2,1)S(1)} %bitcast.408), kind=kOutput, calls=%fused_computation.36 | convolution fusion | flops 8592031744 | bytes 16777216 | tf_op jit(solution)/shard_map/dot_general | solution.py:714
  366.7 9.8 %convolution_convert_fusion.6 = bf16[2048,1024]{1,0:T(8,128)(2,1)S(1)} fusion(bf16[2048,2048]{1,0:T(8,128)(2,1)S(1)} %bitcast.402, bf16[2048,1024]{1,0:T(8,128)(2,1)S(1)} %fusion.2), kind=kOutput, calls=%fused_computation.40 | convolution fusion | flops 8592031744 | bytes 16777216 | tf_op jit(solution)/shard_map/dot_general | solution.py:724
  380.8 5.6 lower.1
  386.4 19.2 %fusion.19 = (bf16[2048,1024]{1,0:T(8,128)(2,1)S(1)}, bf16[2048,1024]{1,0:T(8,128)(2,1)S(1)}) fusion(bf16[2048,1024]{1,0:T(8,128)(2,1)} %copy-done.10, bf16[2048,1024]{1,0:T(8,128)(2,1)} %copy-done.11, bf16[2048,2048]{1,0:T(8,128)(2,1)} %bitcast.399, bf16[2048,1024]{1,0:T(8,128)(2,1)} %bitcast.340), kind=kOutput, calls=%fused_computation.29 | convolution fusion | flops 8644460544 | bytes 29360128 | tf_op jit(solution)/shard_map/dot_general | solution.py:714
  405.7 14.4 %convolution_convert_fusion.4 = bf16[2048,1024]{1,0:T(8,128)(2,1)S(1)} fusion(bf16[2048,2048]{1,0:T(8,128)(2,1)} %bitcast.404, bf16[2048,1024]{1,0:T(8,128)(2,1)S(1)} %get-tuple-element.194), kind=kOutput, calls=%fused_computation.38 | convolution fusion | flops 8592031744 | bytes 16777216 | tf_op jit(solution)/shard_map/dot_general | solution.py:724
  420.1 11.5 %convolution_convert_fusion.5 = bf16[2048,1024]{1,0:T(8,128)(2,1)S(1)} fusion(bf16[2048,2048]{1,0:T(8,128)(2,1)} %bitcast.405, bf16[2048,1024]{1,0:T(8,128)(2,1)S(1)} %get-tuple-element.188), kind=kOutput, calls=%fused_computation.39 | convolution fusion | flops 8592031744 | bytes 16777216 | tf_op jit(solution)/shard_map/dot_general | solution.py:724
  438.6 10.7 %fusion.115 = f32[2048,2048]{1,0:T(8,128)S(1)} fusion(bf16[2048,1024]{1,0:T(8,128)(2,1)} %copy-done.81, bf16[2048,1024]{1,0:T(8,128)(2,1)S(1)} %bitcast.410), kind=kOutput, calls=%fused_computation.255 | convolution fusion | flops 8589934592 | bytes 25165824 | tf_op jit(solution)/shard_map/dot_general | solution.py:718
  454.3 12.0 %collective-permute-start.19 = (bf16[352,1024]{1,0:T(8,128)(2,1)}, bf16[352,1024]{1,0:T(8,128)(2,1)S(1)}, u32[]{:S(2)}, u32[]{:S(2)}) collective-permute-start(bf16[352,1024]{1,0:T(8,128)(2,1)} %get-tuple-element.274), channel_id=1, source_target_pairs={{0,24},{4,28},{8,0},{12,4},{16,8},{20,12},{24,16},{28,20},{1,25},{... | collective-permute-start | bytes 2162696 | tf_op jit(solution)/shard_map/ppermute | solution.py:612
  469.5 15.4 %fusion.116 = f32[2048,2048]{1,0:T(8,128)} fusion(bf16[2048,1024]{1,0:T(8,128)(2,1)} %copy-done.80, bf16[2048,1024]{1,0:T(8,128)(2,1)} %bitcast.407), kind=kOutput, calls=%fused_computation.256 | convolution fusion | flops 8589934592 | bytes 25165824 | tf_op jit(solution)/shard_map/dot_general | solution.py:718
  484.8 9.7 %add_convert_fusion = bf16[2048,2048]{1,0:T(8,128)(2,1)} fusion(f32[2048,2048]{1,0:T(8,128)S(1)} %fusion.115, f32[2048,2048]{1,0:T(8,128)} %fusion.116), kind=kLoop, calls=%fused_computation.7 | loop fusion | flops 8388608 | bytes 41943040 | tf_op jit(solution)/shard_map/convert_element_type | solution.py:750
  494.5 77.5 %collect.1 = (f32[128,2048]{1,0:T(8,128)}, f32[16,1024]{1,0:T(8,128)}) custom-call(bf16[4,2,2,128,2048]{4,3,2,1,0:T(8,128)(2,1)} %bitcast.324, bf16[4,2,2,16,1024]{4,3,2,1,0:T(8,128)(2,1)} %bitcast.350), custom_call_target="tpu_custom_call" | custom-call | bytes 3000000 | tf_op jit(solution)/shard_map/collect/pallas_call | solution.py:586
  585.3 21.9 %sent.1 = (bf16[2,2,128,2048]{3,2,1,0:T(8,128)(2,1)}, bf16[2,2,16,1024]{3,2,1,0:T(8,128)(2,1)}) custom-call(bf16[128,2048]{1,0:T(8,128)(2,1)} %fusion.101.refs_0_, bf16[16,1024]{1,0:T(8,128)(2,1)} %fusion.98.refs_1_), custom_call_target="tpu_custom_call" | custom-call | bytes 3000000 | tf_op jit(solution)/shard_map/sent/pallas_call | solution.py:586
  611.5 3.6 fusion.117
  620.1 3.7 collective-permute-start.22
  630.1 13.3 %pair_grads.1 = f32[576,128]{1,0:T(8,128)} custom-call(bf16[2,2,576,128]{3,2,1,0:T(8,128)(2,1)} %bitcast.347), custom_call_target="tpu_custom_call" | custom-call | bytes 3000000 | tf_op jit(solution)/shard_map/pair_grads/pallas_call | solution.py:586
  643.5 3.6 collective-permute-done.23.refs_11_
  651.2 14.1 %convolution_convert_fusion = bf16[2048,2048]{1,0:T(8,128)(2,1)} fusion(bf16[2048,1024]{1,0:T(8,128)(2,1)} %copy-done.9, bf16[2048,1024]{1,0:T(8,128)(2,1)} %bitcast.341), kind=kOutput, calls=%fused_computation.31 | convolution fusion | flops 8594128896 | bytes 16777216 | tf_op jit(solution)/shard_map/dot_general | solution.py:718
  669.6 22.4 %backs.1 = (f32[128,2048]{1,0:T(8,128)}, f32[16,1024]{1,0:T(8,128)}) custom-call(bf16[2,2,128,2048]{3,2,1,0:T(8,128)(2,1)} %bitcast.352, bf16[2,2,16,1024]{3,2,1,0:T(8,128)(2,1)} %bitcast.381), custom_call_target="tpu_custom_call" | custom-call | bytes 3000000 | tf_op jit(solution)/shard_map/backs/pallas_call | solution.py:586
  692.1 4.6 collective-permute-done.25.refs_10_
  696.8 5.1 convolution_convert_fusion.7
  706.0 128.9 %fold.1 = (bf16[4,64,640]{2,1,0:T(8,128)(2,1)}, bf16[4,32,640]{2,1,0:T(8,128)(2,1)}, bf16[4,64,512]{2,1,0:T(8,128)(2,1)}, bf16[4,32,512]{2,1,0:T(8,128)(2,1)}, f...) custom-call(bf16[4,2,4,64,640]{4,3,2,1,0:T(8,128)(2,1)} %bitcast.346, ...), custom_call_target="tpu_custom_call" | custom-call | bytes 3000000 | tf_op jit(solution)/shard_map/fold/pallas_call | solution.py:586
  845.8 7.0 returns.1
  (333 shorter events, 128.6 us)
Async XLA Ops:
  136.4 60.2 %collective-permute-start = (bf16[608,1024]{1,0:T(8,128)(2,1)}, bf16[608,1024]{1,0:T(8,128)(2,1)S(1)}, u32[]{:S(2)}, u32[]{:S(2)}) collective-permute-start(bf16[608,1024]{1,0:T(8,128)(2,1)} %get-tuple-element.146), channel_id=1, source_target_pairs={{0,8},{4,12},{8,16},{12,20},{16,24},{20,28},{24,0},{28,4},{1,9},{5... | collective-permute-start | bytes 3735560 | tf_op jit(solution)/shard_map/ppermute | solution.py:612
  136.4 84.9 %collective-permute-start.1 = (bf16[608,1024]{1,0:T(8,128)(2,1)}, bf16[608,1024]{1,0:T(8,128)(2,1)}, u32[]{:S(2)}, u32[]{:S(2)}) collective-permute-start(bf16[608,1024]{1,0:T(8,128)(2,1)} %get-tuple-element.149), channel_id=1, source_target_pairs={{0,16},{4,20},{8,24},{12,28},{16,0},{20,4},{24,8},{28,12},{1,17},{... | collective-permute-start | bytes 3735560 | tf_op jit(solution)/shard_map/ppermute | solution.py:612
  138.3 83.1 %collective-permute-start.2 = (bf16[608,1024]{1,0:T(8,128)(2,1)}, bf16[608,1024]{1,0:T(8,128)(2,1)}, u32[]{:S(2)}, u32[]{:S(2)}) collective-permute-start(bf16[608,1024]{1,0:T(8,128)(2,1)} %get-tuple-element.152), channel_id=1, source_target_pairs={{0,24},{4,28},{8,0},{12,4},{16,8},{20,12},{24,16},{28,20},{1,25},{... | collective-permute-start | bytes 3735560 | tf_op jit(solution)/shard_map/ppermute | solution.py:612
  140.4 170.3 %collective-permute-start.3 = (bf16[608,1024]{1,0:T(8,128)(2,1)}, bf16[608,1024]{1,0:T(8,128)(2,1)}, u32[]{:S(2)}, u32[]{:S(2)}) collective-permute-start(bf16[608,1024]{1,0:T(8,128)(2,1)} %get-tuple-element.163.refs_0_), channel_id=1, source_target_pairs={{0,4},{4,0},{8,12},{12,8},{16,20},{20,16},{24,28},{28,24},{1,5},{5... | collective-permute-start | bytes 3735560 | tf_op jit(solution)/shard_map/ppermute | solution.py:612
  174.1 26.1 %copy-start.55 = (f32[1024]{0:T(1024)S(1)}, f32[1024]{0:T(1024)}, u32[]{:S(2)}) copy-start(f32[1024]{0:T(1024)} %param.41) | copy-start | bytes 12292
  174.1 26.8 %copy-start.50 = (f32[2048]{0:T(1024)S(1)}, f32[2048]{0:T(1024)}, u32[]{:S(2)}) copy-start(f32[2048]{0:T(1024)} %param.39) | copy-start | bytes 24580
  196.6 119.0 %copy-start.24 = (bf16[608,1024]{1,0:T(8,128)(2,1)}, bf16[608,1024]{1,0:T(8,128)(2,1)S(1)}, u32[]{:S(2)}) copy-start(bf16[608,1024]{1,0:T(8,128)(2,1)S(1)} %collective-permute-done.refs_2_) | copy-start | bytes 3735556
  221.4 89.4 %collective-permute-start.6 = (bf16[608,1024]{1,0:T(8,128)(2,1)}, bf16[608,1024]{1,0:T(8,128)(2,1)S(1)}, u32[]{:S(2)}, u32[]{:S(2)}) collective-permute-start(bf16[608,1024]{1,0:T(8,128)(2,1)} %collective-permute-done.2.refs_6_), channel_id=1, source_target_pairs={{0,4},{4,0},{8,12},{12,8},{16,20},{20,16},{24,28},{28,24},{1,5},{5... | collective-permute-start | bytes 3735560 | tf_op jit(solution)/shard_map/ppermute | solution.py:612
  222.0 91.4 %collective-permute-start.5 = (bf16[608,1024]{1,0:T(8,128)(2,1)}, bf16[608,1024]{1,0:T(8,128)(2,1)}, u32[]{:S(2)}, u32[]{:S(2)}) collective-permute-start(bf16[608,1024]{1,0:T(8,128)(2,1)} %collective-permute-done.1.refs_4_), channel_id=1, source_target_pairs={{0,4},{4,0},{8,12},{12,8},{16,20},{20,16},{24,28},{28,24},{1,5},{5... | collective-permute-start | bytes 3735560 | tf_op jit(solution)/shard_map/ppermute | solution.py:612
  223.5 92.1 %collective-permute-start.4 = (bf16[608,1024]{1,0:T(8,128)(2,1)S(1)}, bf16[608,1024]{1,0:T(8,128)(2,1)}, u32[]{:S(2)}, u32[]{:S(2)}) collective-permute-start(bf16[608,1024]{1,0:T(8,128)(2,1)S(1)} %collective-permute-done.refs_2_), channel_id=1, source_target_pairs={{0,4},{4,0},{8,12},{12,8},{16,20},{20,16},{24,28},{28,24},{1,5},{5... | collective-permute-start | bytes 3735560 | tf_op jit(solution)/shard_map/ppermute | solution.py:612
  224.0 155.9 %collective-permute-start.10 = (bf16[256,1024]{1,0:T(8,128)(2,1)}, bf16[256,1024]{1,0:T(8,128)(2,1)}, u32[]{:S(2)}, u32[]{:S(2)}) collective-permute-start(bf16[256,1024]{1,0:T(8,128)(2,1)} %get-tuple-element.157.refs_0_), channel_id=1, source_target_pairs={{0,4},{4,0},{8,12},{12,8},{16,20},{20,16},{24,28},{28,24},{1,5},{5... | collective-permute-start | bytes 1572872 | tf_op jit(solution)/shard_map/ppermute | solution.py:612
  310.7 22.8 %collective-permute-start.7 = (bf16[256,1024]{1,0:T(8,128)(2,1)}, bf16[256,1024]{1,0:T(8,128)(2,1)}, u32[]{:S(2)}, u32[]{:S(2)}) collective-permute-start(bf16[256,1024]{1,0:T(8,128)(2,1)} %get-tuple-element.172), channel_id=1, source_target_pairs={{0,8},{4,12},{8,16},{12,20},{16,24},{20,28},{24,0},{28,4},{1,9},{5... | collective-permute-start | bytes 1572872 | tf_op jit(solution)/shard_map/ppermute | solution.py:612
  310.8 38.6 %collective-permute-start.8 = (bf16[256,1024]{1,0:T(8,128)(2,1)}, bf16[256,1024]{1,0:T(8,128)(2,1)}, u32[]{:S(2)}, u32[]{:S(2)}) collective-permute-start(bf16[256,1024]{1,0:T(8,128)(2,1)} %get-tuple-element.175), channel_id=1, source_target_pairs={{0,16},{4,20},{8,24},{12,28},{16,0},{20,4},{24,8},{28,12},{1,17},{... | collective-permute-start | bytes 1572872 | tf_op jit(solution)/shard_map/ppermute | solution.py:612
  313.3 48.2 %collective-permute-start.9 = (bf16[256,1024]{1,0:T(8,128)(2,1)}, bf16[256,1024]{1,0:T(8,128)(2,1)}, u32[]{:S(2)}, u32[]{:S(2)}) collective-permute-start(bf16[256,1024]{1,0:T(8,128)(2,1)} %get-tuple-element.179), channel_id=1, source_target_pairs={{0,24},{4,28},{8,0},{12,4},{16,8},{20,12},{24,16},{28,20},{1,25},{... | collective-permute-start | bytes 1572872 | tf_op jit(solution)/shard_map/ppermute | solution.py:612
  333.5 46.4 %collective-permute-start.11 = (bf16[256,1024]{1,0:T(8,128)(2,1)}, bf16[256,1024]{1,0:T(8,128)(2,1)S(1)}, u32[]{:S(2)}, u32[]{:S(2)}) collective-permute-start(bf16[256,1024]{1,0:T(8,128)(2,1)} %collective-permute-done.7.refs_2_), channel_id=1, source_target_pairs={{0,4},{4,0},{8,12},{12,8},{16,20},{20,16},{24,28},{28,24},{1,5},{5... | collective-permute-start | bytes 1572872 | tf_op jit(solution)/shard_map/ppermute | solution.py:612
  334.0 32.6 %slice-start = ((s8[8388608]{0:T(1024)(128)(4,1)}), s8[4194304]{0:T(1024)(128)(4,1)S(1)}, s32[]{:S(2)}) async-start(s8[8388608]{0:T(1024)(128)(4,1)} %bitcast.400), calls=%async_computation | async-start | bytes 8388608
  349.4 30.5 %collective-permute-start.12 = (bf16[256,1024]{1,0:T(8,128)(2,1)}, bf16[256,1024]{1,0:T(8,128)(2,1)S(1)}, u32[]{:S(2)}, u32[]{:S(2)}) collective-permute-start(bf16[256,1024]{1,0:T(8,128)(2,1)} %collective-permute-done.8.refs_4_), channel_id=1, source_target_pairs={{0,4},{4,0},{8,12},{12,8},{16,20},{20,16},{24,28},{28,24},{1,5},{5... | collective-permute-start | bytes 1572872 | tf_op jit(solution)/shard_map/ppermute | solution.py:612
  361.5 18.4 %collective-permute-start.13 = (bf16[256,1024]{1,0:T(8,128)(2,1)}, bf16[256,1024]{1,0:T(8,128)(2,1)}, u32[]{:S(2)}, u32[]{:S(2)}) collective-permute-start(bf16[256,1024]{1,0:T(8,128)(2,1)} %collective-permute-done.9.refs_6_), channel_id=1, source_target_pairs={{0,4},{4,0},{8,12},{12,8},{16,20},{20,16},{24,28},{28,24},{1,5},{5... | collective-permute-start | bytes 1572872 | tf_op jit(solution)/shard_map/ppermute | solution.py:612
  379.1 70.2 %collective-permute-start.14 = (bf16[4,352,1024]{2,1,0:T(8,128)(2,1)}, bf16[4,352,1024]{2,1,0:T(8,128)(2,1)}, u32[]{:S(2)}, u32[]{:S(2)}) collective-permute-start(bf16[4,352,1024]{2,1,0:T(8,128)(2,1)} %pad_maximum_fusion.1), channel_id=1, source_target_pairs={{0,4},{4,0},{8,12},{12,8},{16,20},{20,16},{24,28},{28,24},{1,5},{5... | collective-permute-start | bytes 8650760 | tf_op jit(solution)/shard_map/ppermute | solution.py:612
  436.6 135.4 %collective-permute-start.16 = (bf16[4,256,1024]{2,1,0:T(8,128)(2,1)}, bf16[4,256,1024]{2,1,0:T(8,128)(2,1)}, u32[]{:S(2)}, u32[]{:S(2)}) collective-permute-start(bf16[4,256,1024]{2,1,0:T(8,128)(2,1)} %get-tuple-element.268), channel_id=1, source_target_pairs={{0,4},{4,0},{8,12},{12,8},{16,20},{20,16},{24,28},{28,24},{1,5},{5... | collective-permute-start | bytes 6291464 | tf_op jit(solution)/shard_map/ppermute | solution.py:612
  438.1 133.9 %collective-permute-start.15 = (bf16[4,256,1024]{2,1,0:T(8,128)(2,1)}, bf16[4,256,1024]{2,1,0:T(8,128)(2,1)}, u32[]{:S(2)}, u32[]{:S(2)}) collective-permute-start(bf16[4,256,1024]{2,1,0:T(8,128)(2,1)} %get-tuple-element.270), channel_id=1, source_target_pairs={{0,4},{4,0},{8,12},{12,8},{16,20},{20,16},{24,28},{28,24},{1,5},{5... | collective-permute-start | bytes 6291464 | tf_op jit(solution)/shard_map/ppermute | solution.py:612
  454.3 117.8 %collective-permute-start.19 = (bf16[352,1024]{1,0:T(8,128)(2,1)}, bf16[352,1024]{1,0:T(8,128)(2,1)S(1)}, u32[]{:S(2)}, u32[]{:S(2)}) collective-permute-start(bf16[352,1024]{1,0:T(8,128)(2,1)} %get-tuple-element.274), channel_id=1, source_target_pairs={{0,24},{4,28},{8,0},{12,4},{16,8},{20,12},{24,16},{28,20},{1,25},{... | collective-permute-start | bytes 2162696 | tf_op jit(solution)/shard_map/ppermute | solution.py:612
  466.3 105.8 %collective-permute-start.18 = (bf16[352,1024]{1,0:T(8,128)(2,1)}, bf16[352,1024]{1,0:T(8,128)(2,1)S(1)}, u32[]{:S(2)}, u32[]{:S(2)}) collective-permute-start(bf16[352,1024]{1,0:T(8,128)(2,1)} %get-tuple-element.275), channel_id=1, source_target_pairs={{0,16},{4,20},{8,24},{12,28},{16,0},{20,4},{24,8},{28,12},{1,17},{... | collective-permute-start | bytes 2162696 | tf_op jit(solution)/shard_map/ppermute | solution.py:612
  469.1 103.0 %collective-permute-start.17 = (bf16[352,1024]{1,0:T(8,128)(2,1)}, bf16[352,1024]{1,0:T(8,128)(2,1)}, u32[]{:S(2)}, u32[]{:S(2)}) collective-permute-start(bf16[352,1024]{1,0:T(8,128)(2,1)} %get-tuple-element.276), channel_id=1, source_target_pairs={{0,8},{4,12},{8,16},{12,20},{16,24},{20,28},{24,0},{28,4},{1,9},{5... | collective-permute-start | bytes 2162696 | tf_op jit(solution)/shard_map/ppermute | solution.py:612
  494.5 78.4 %copy-start.5 = (bf16[4,256,1024]{2,1,0:T(8,128)(2,1)S(1)}, bf16[4,256,1024]{2,1,0:T(8,128)(2,1)}, u32[]{:S(2)}) copy-start(bf16[4,256,1024]{2,1,0:T(8,128)(2,1)} %get-tuple-element.206) | copy-start | bytes 6291460
  579.2 28.1 %collective-permute-start.20 = (bf16[256,1024]{1,0:T(8,128)(2,1)}, bf16[256,1024]{1,0:T(8,128)(2,1)S(1)}, u32[]{:S(2)}, u32[]{:S(2)}) collective-permute-start(bf16[256,1024]{1,0:T(8,128)(2,1)} %get-tuple-element.285), channel_id=1, source_target_pairs={{0,8},{4,12},{8,16},{12,20},{16,24},{20,28},{24,0},{28,4},{1,9},{5... | collective-permute-start | bytes 1572872 | tf_op jit(solution)/shard_map/ppermute | solution.py:612
  583.8 25.3 %copy-start.33 = (bf16[2,8,8,256]{3,2,0,1:T(8,128)(2,1)S(1)}, bf16[2,8,8,256]{3,2,0,1:T(8,128)(2,1)}, u32[]{:S(2)}) copy-start(bf16[2,8,8,256]{3,2,0,1:T(8,128)(2,1)} %copy-done.32) | copy-start | bytes 196612
  583.8 23.5 %collective-permute-start.21 = (bf16[256,1024]{1,0:T(8,128)(2,1)}, bf16[256,1024]{1,0:T(8,128)(2,1)}, u32[]{:S(2)}, u32[]{:S(2)}) collective-permute-start(bf16[256,1024]{1,0:T(8,128)(2,1)} %get-tuple-element.281), channel_id=1, source_target_pairs={{0,8},{4,12},{8,16},{12,20},{16,24},{20,28},{24,0},{28,4},{1,9},{5... | collective-permute-start | bytes 1572872 | tf_op jit(solution)/shard_map/ppermute | solution.py:612
  620.1 23.4 %collective-permute-start.22 = (bf16[256,1024]{1,0:T(8,128)(2,1)}, bf16[256,1024]{1,0:T(8,128)(2,1)S(1)}, u32[]{:S(2)}, u32[]{:S(2)}) collective-permute-start(bf16[256,1024]{1,0:T(8,128)(2,1)} %get-tuple-element.215), channel_id=1, source_target_pairs={{0,24},{4,28},{8,0},{12,4},{16,8},{20,12},{24,16},{28,20},{1,25},{... | collective-permute-start | bytes 1572872 | tf_op jit(solution)/shard_map/ppermute | solution.py:612
  623.7 23.3 %collective-permute-start.23 = (bf16[256,1024]{1,0:T(8,128)(2,1)}, bf16[256,1024]{1,0:T(8,128)(2,1)}, u32[]{:S(2)}, u32[]{:S(2)}) collective-permute-start(bf16[256,1024]{1,0:T(8,128)(2,1)} %get-tuple-element.216), channel_id=1, source_target_pairs={{0,24},{4,28},{8,0},{12,4},{16,8},{20,12},{24,16},{28,20},{1,25},{... | collective-permute-start | bytes 1572872 | tf_op jit(solution)/shard_map/ppermute | solution.py:612
  648.0 44.1 %collective-permute-start.24 = (bf16[256,1024]{1,0:T(8,128)(2,1)}, bf16[256,1024]{1,0:T(8,128)(2,1)}, u32[]{:S(2)}, u32[]{:S(2)}) collective-permute-start(bf16[256,1024]{1,0:T(8,128)(2,1)} %get-tuple-element.222), channel_id=1, source_target_pairs={{0,16},{4,20},{8,24},{12,28},{16,0},{20,4},{24,8},{28,12},{1,17},{... | collective-permute-start | bytes 1572872 | tf_op jit(solution)/shard_map/ppermute | solution.py:612
  651.1 45.6 %collective-permute-start.25 = (bf16[256,1024]{1,0:T(8,128)(2,1)}, bf16[256,1024]{1,0:T(8,128)(2,1)}, u32[]{:S(2)}, u32[]{:S(2)}) collective-permute-start(bf16[256,1024]{1,0:T(8,128)(2,1)} %get-tuple-element.223), channel_id=1, source_target_pairs={{0,16},{4,20},{8,24},{12,28},{16,0},{20,4},{24,8},{28,12},{1,17},{... | collective-permute-start | bytes 1572872 | tf_op jit(solution)/shard_map/ppermute | solution.py:612
  (78 other events, 525.6 us)
